TPU v7x, 256 devices: a whole 4x4x8 slice. The times are simulated.
256 devices in a mesh: wide: 32 (over y, z), narrow: 8 (over x, core).
Axes of the slice: x: 4, y: 4, z: 8, core: 2. Of those that a mesh axis runs over, the one named last changes fastest.
Arguments:
- displacement: float32 [32, 8, 2048, 128], P('wide', 'narrow'), may hold values from -6 to 6
- applied_loads: float32 [32, 8, 2048, 128], P('wide', 'narrow'), may hold values from -6 to 6
- stiff_blocks: bfloat16 [32, 8, 16, 7, 128, 128], P('wide', 'narrow'), may hold values from -0.1875 to 0.1875
- stiff_columns: int32 [32, 8, 16, 7], P('wide', 'narrow'), may hold values from 0 to 15, all different within a row
- face_rows: int32 [32, 8, 2, 256], P('wide', 'narrow'), may hold values from 0 to 2047, as said below
- coupling: bfloat16 [32, 8, 2, 256, 256], P('wide', 'narrow'), may hold values from -0.375 to 0.375
- inverse_blocks: bfloat16 [32, 8, 16, 8, 128, 128], P('wide', 'narrow'), may hold values from -0.09375 to 0.09375
- inverse_columns: int32 [32, 8, 16, 8], P('wide', 'narrow'), may hold values from 0 to 15, all different within a row
Outputs:
- solution: float32 [32, 8, 2048, 128], P('wide', 'narrow')
- last_residual: float32 [32, 8, 2048, 128], P('wide', 'narrow')
Inputs may be any that keep to these rules, and one draw needn't show every extreme that they name: `stiff_columns`: within each block row the 7 column blocks are distinct. `inverse_columns`: within each block row the 8 coefficient blocks are distinct. `face_rows`: on each subdomain the 512 listed rows are distinct; entry 0 lists the rows of the lower face, entry 1 those of the upper face.
All inputs are finite; a program needn't handle non-finite values.
Results may differ from a plain program's by a relative error of at most 0.003.
Values may be sent and summed in bfloat16 or wider, within the bound.
No kernel may reach another device: no remote copies, remote signals or barrier semaphores. Data moves between devices by JAX's collectives and lax.ppermute only.
A program may use at most 128 MiB of HBM per device.

v0:
```python
import functools

import jax
import jax.numpy as jnp
from jax import lax
from jax.experimental import pallas as pl
from jax.experimental.pallas import tpu as pltpu
from jax.sharding import PartitionSpec as P

ITERS = 2
BLK = 128
NB = 16
KNZ = 7
XNZ = 8
FACE = 256
LEVELS = 8
GROUP = 4
SLICES = 8
PIECE = 2 * (BLK // SLICES)

bf16 = jnp.bfloat16
f32 = jnp.float32
VMEM = pltpu.VMEM
SMEM = pltpu.SMEM


def gather_rows(cur_ref, face_ref, rows_ref, low_ref, high_ref):
    def body(t, _):
        base = t * 16
        for k in range(16):
            rows_ref[pl.ds(base + k, 1), :] = cur_ref[pl.ds(face_ref[base + k], 1), :]
        return 0

    lax.fori_loop(0, 2 * FACE // 16, body, 0)
    low_ref[...] = rows_ref[0:FACE, :].astype(bf16)
    high_ref[...] = rows_ref[FACE : 2 * FACE, :].astype(bf16)


def faces_kernel(face_ref, cur_ref, low_ref, high_ref, rows_ref):
    gather_rows(cur_ref, face_ref, rows_ref, low_ref, high_ref)


def product_kernel(cols_ref, stiff_ref, cur_ref, applied_ref, out_ref, curb_ref):
    g = pl.program_id(0)

    @pl.when(g == 0)
    def _():
        curb_ref[...] = cur_ref[...].astype(bf16).reshape(NB, BLK, BLK)

    for ii in range(GROUP):
        row = (g * GROUP + ii) * KNZ
        mats = jnp.concatenate([stiff_ref[ii, j] for j in range(KNZ)], axis=1)
        picked = jnp.concatenate([curb_ref[cols_ref[row + j]] for j in range(KNZ)], axis=0)
        prod = jnp.dot(mats, picked, preferred_element_type=f32)
        out_ref[ii * BLK : (ii + 1) * BLK, :] = applied_ref[ii * BLK : (ii + 1) * BLK, :] - prod


def partial_kernel(
    cols_ref, face_ref, me_ref, inv_ref, base_ref, below_ref, above_ref, couple_ref,
    res_ref, keep_ref, send_ref, side_ref, acc_ref,
):
    g = pl.program_id(0)

    @pl.when(g == 0)
    def _():
        res_ref[...] = base_ref[...]
        side_ref[0:FACE, :] = jnp.dot(couple_ref[0], below_ref[...], preferred_element_type=f32)
        side_ref[FACE : 2 * FACE, :] = jnp.dot(
            couple_ref[1], above_ref[...], preferred_element_type=f32
        )

        def body(t, _):
            first = t * 16
            rows = [face_ref[first + k] for k in range(16)]
            olds = [res_ref[pl.ds(rows[k], 1), :] for k in range(16)]
            for k in range(16):
                res_ref[pl.ds(rows[k], 1), :] = olds[k] - side_ref[pl.ds(first + k, 1), :]
            return 0

        lax.fori_loop(0, 2 * FACE // 16, body, 0)
        acc_ref[...] = jnp.zeros_like(acc_ref)

    for ii in range(GROUP):
        i = g * GROUP + ii
        block = res_ref[pl.ds(pl.multiple_of(i * BLK, BLK), BLK), :].astype(bf16)
        mats = jnp.concatenate([inv_ref[ii, j] for j in range(XNZ)], axis=1)
        terms = jnp.dot(block.T, mats, preferred_element_type=f32)
        for j in range(XNZ):
            acc_ref[cols_ref[i * XNZ + j]] += terms[:, j * BLK : (j + 1) * BLK]

    @pl.when(g == NB // GROUP - 1)
    def _():
        me = me_ref[0]
        half = PIECE // 2
        for rel in range(SLICES):
            start = pl.multiple_of((me ^ rel) * half, half)
            for c in range(NB):
                level, h = divmod(c, 2)
                value = acc_ref[c, pl.ds(start, half), :]
                if rel < SLICES // 2:
                    keep_ref[rel, level, h * half : (h + 1) * half, :] = value
                else:
                    send_ref[rel - SLICES // 2, level, h * half : (h + 1) * half, :] = value.astype(
                        bf16
                    )


def update_kernel(gather, cols_ref, face_ref, me_ref, inv_ref, own_ref, got_ref, cur_ref, *rest):
    if gather:
        new_ref, low_ref, high_ref, coeff_ref, rows_ref = rest
    else:
        new_ref, coeff_ref = rest
    g = pl.program_id(0)

    @pl.when(g == 0)
    def _():
        me = me_ref[0]
        half = PIECE // 2
        for rel in range(SLICES):
            start = pl.multiple_of((me ^ rel) * half, half)
            src = own_ref if rel < SLICES // 2 else got_ref
            for c in range(NB):
                level, h = divmod(c, 2)
                coeff_ref[c, pl.ds(start, half), :] = src[
                    rel % (SLICES // 2), level, h * half : (h + 1) * half, :
                ]

    for ii in range(GROUP):
        i = g * GROUP + ii
        mats = jnp.concatenate([inv_ref[ii, j] for j in range(XNZ)], axis=1)
        picked = jnp.concatenate([coeff_ref[cols_ref[i * XNZ + j]] for j in range(XNZ)], axis=1)
        upd = lax.dot_general(mats, picked, (((1,), (1,)), ((), ())), preferred_element_type=f32)
        rows = pl.ds(pl.multiple_of(i * BLK, BLK), BLK)
        new_ref[rows, :] = cur_ref[rows, :] + upd

    if gather:

        @pl.when(g == NB // GROUP - 1)
        def _():
            gather_rows(new_ref, face_ref, rows_ref, low_ref, high_ref)


def sds(shape, dtype):
    return jax.ShapeDtypeStruct(shape, dtype)


def whole(shape):
    return pl.BlockSpec(shape, lambda g, *_: (0,) * len(shape))


ROWS = NB * BLK
STEPS = NB // GROUP
KEEP = (SLICES // 2, LEVELS, PIECE, BLK)


def faces_of(cur, faces):
    return pl.pallas_call(
        faces_kernel,
        grid_spec=pltpu.PrefetchScalarGridSpec(
            num_scalar_prefetch=1,
            grid=(1,),
            in_specs=[whole((ROWS, BLK))],
            out_specs=[whole((FACE, BLK))] * 2,
            scratch_shapes=[VMEM((2 * FACE, BLK), f32)],
        ),
        out_shape=[sds((FACE, BLK), bf16)] * 2,
        name="faces",
    )(faces, cur)


def base_of(cur, applied, stiff, cols):
    return pl.pallas_call(
        product_kernel,
        grid_spec=pltpu.PrefetchScalarGridSpec(
            num_scalar_prefetch=1,
            grid=(STEPS,),
            in_specs=[
                pl.BlockSpec((GROUP, KNZ, BLK, BLK), lambda g, *_: (g, 0, 0, 0)),
                whole((ROWS, BLK)),
                pl.BlockSpec((GROUP * BLK, BLK), lambda g, *_: (g, 0)),
            ],
            out_specs=pl.BlockSpec((GROUP * BLK, BLK), lambda g, *_: (g, 0)),
            scratch_shapes=[VMEM((NB, BLK, BLK), bf16)],
        ),
        out_shape=sds((ROWS, BLK), f32),
        cost_estimate=pl.CostEstimate(
            flops=2 * NB * KNZ * BLK**3, bytes_accessed=8_000_000, transcendentals=0
        ),
        name="product",
    )(cols, stiff, cur, applied)


def partial_of(base, below, above, couple, inverse, cols, faces, me):
    return pl.pallas_call(
        partial_kernel,
        grid_spec=pltpu.PrefetchScalarGridSpec(
            num_scalar_prefetch=3,
            grid=(STEPS,),
            in_specs=[
                pl.BlockSpec((GROUP, XNZ, BLK, BLK), lambda g, *_: (g, 0, 0, 0)),
                whole((ROWS, BLK)),
                whole((FACE, BLK)),
                whole((FACE, BLK)),
                whole((2, FACE, FACE)),
            ],
            out_specs=[whole((ROWS, BLK)), whole(KEEP), whole(KEEP)],
            scratch_shapes=[VMEM((2 * FACE, BLK), f32), VMEM((NB, BLK, BLK), f32)],
        ),
        out_shape=[sds((ROWS, BLK), f32), sds(KEEP, f32), sds(KEEP, bf16)],
        cost_estimate=pl.CostEstimate(
            flops=2 * NB * XNZ * BLK**3, bytes_accessed=8_000_000, transcendentals=0
        ),
        name="partial",
    )(cols, faces, me, inverse, base, below, above, couple)


def update_of(own, got, cur, inverse, cols, faces, me, gather):
    scratch = [VMEM((NB, BLK, BLK), bf16)]
    outs, specs = [sds((ROWS, BLK), f32)], [whole((ROWS, BLK))]
    if gather:
        scratch.append(VMEM((2 * FACE, BLK), f32))
        outs += [sds((FACE, BLK), bf16)] * 2
        specs += [whole((FACE, BLK))] * 2
    return pl.pallas_call(
        functools.partial(update_kernel, gather),
        grid_spec=pltpu.PrefetchScalarGridSpec(
            num_scalar_prefetch=3,
            grid=(STEPS,),
            in_specs=[
                pl.BlockSpec((GROUP, XNZ, BLK, BLK), lambda g, *_: (g, 0, 0, 0)),
                whole(KEEP),
                whole(KEEP),
                whole((ROWS, BLK)),
            ],
            out_specs=specs,
            scratch_shapes=scratch,
        ),
        out_shape=outs,
        cost_estimate=pl.CostEstimate(
            flops=2 * NB * XNZ * BLK**3, bytes_accessed=8_000_000, transcendentals=0
        ),
        name="update",
    )(cols, faces, me, inverse, own, got, cur)


def swapped(value, axis, mask):
    return lax.ppermute(value, axis, [(i, i ^ mask) for i in range(lax.axis_size(axis))])


def shifted(value, steps):
    count = lax.axis_size("narrow")
    pairs = [(i, i + steps) for i in range(count) if 0 <= i + steps < count]
    return lax.ppermute(value, "narrow", pairs)


def rounded(total, level):
    return (total * f32(2.0 ** (-level / 2))).astype(bf16)


def summed(keep, send):
    done = {}
    total = keep + swapped(send, "narrow", 1).astype(f32)
    done[1] = rounded(total[:, :1], 1)
    for level, mask in ((2, 2), (3, 6)):
        size = total.shape[0] // 2
        got = swapped(total[size:, 1:].astype(bf16), "narrow", mask)
        total = total[:size, 1:] + got.astype(f32)
        done[level] = rounded(total[:, :1], level)
    for level, mask in ((4, 1), (5, 2), (6, 6), (7, 8), (8, 24)):
        total = total[:, 1:]
        total = total + swapped(total.astype(bf16), "wide", mask).astype(f32)
        done[level] = rounded(total[:, :1], level)
    mine = jnp.concatenate([done[level] for level in range(3, LEVELS + 1)], axis=1)
    for level, mask in ((2, 6), (1, 2)):
        mine = jnp.concatenate([mine, swapped(mine, "narrow", mask)], axis=0)
        mine = jnp.concatenate([done[level], mine], axis=1)
    return mine, swapped(mine, "narrow", 1)


def per_device(
    displacement, applied_loads, stiff_blocks, stiff_columns,
    face_rows, coupling, inverse_blocks, inverse_columns,
):
    current = displacement[0, 0]
    applied = applied_loads[0, 0]
    stiff = stiff_blocks[0, 0]
    stiff_cols = stiff_columns[0, 0].reshape(-1)
    faces = face_rows[0, 0].reshape(-1)
    couple = coupling[0, 0]
    inverse = inverse_blocks[0, 0]
    inverse_cols = inverse_columns[0, 0].reshape(-1)
    place = lax.axis_index("narrow").astype(jnp.int32)
    core, bit0, bit1 = place & 1, (place >> 1) & 1, (place >> 2) & 1
    me = (core * 4 + (bit0 ^ bit1) * 2 + bit1).reshape(1)
    low, high = faces_of(current, faces)
    for sweep in range(ITERS):
        below = shifted(high, 1)
        above = shifted(low, -1)
        base = base_of(current, applied, stiff, stiff_cols)
        residual, keep, send = partial_of(
            base, below, above, couple, inverse, inverse_cols, faces, me
        )
        own, got = summed(keep, send)
        last = sweep == ITERS - 1
        outs = update_of(own, got, current, inverse, inverse_cols, faces, me, not last)
        current = outs[0]
        if not last:
            low, high = outs[1:]
    return (current[None, None], residual[None, None])


def solution(mesh):
    placed = (
        P("wide", "narrow", None, None),
        P("wide", "narrow", None, None),
        P("wide", "narrow", None, None, None, None),
        P("wide", "narrow", None, None),
        P("wide", "narrow", None, None),
        P("wide", "narrow", None, None, None),
        P("wide", "narrow", None, None, None, None),
        P("wide", "narrow", None, None),
    )
    return jax.shard_map(
        per_device,
        mesh=mesh,
        in_specs=placed,
        out_specs=(P("wide", "narrow", None, None), P("wide", "narrow", None, None)),
        check_vma=False,
    )
```

profile of v0, /device:TPU:1, one launch (start us, length us, event | category | flops | bytes accessed | tf_op | source)
XLA Modules:
  0.0 164.0 jit_solution(16924129040021744232)
XLA Ops:
  1.9 3.1 %faces.1 = (bf16[256,128]{1,0:T(8,128)(2,1)}, bf16[256,128]{1,0:T(8,128)(2,1)}) custom-call(s32[512]{0:T(512)} %bitcast.28, f32[2048,128]{1,0:T(8,128)} %bitcast.20), custom_call_target="tpu_custom_call" | custom-call | tf_op jit(solution)/shard_map/faces/pallas_call | solution.py:157
  5.0 4.5 %collective-permute-start = (bf16[256,128]{1,0:T(8,128)(2,1)}, bf16[256,128]{1,0:T(8,128)(2,1)S(1)}, u32[]{:S(2)}, u32[]{:S(2)}) collective-permute-start(bf16[256,128]{1,0:T(8,128)(2,1)} %get-tuple-element.12), channel_id=1, source_target_pairs={{0,1},{1,2},{2,3},{3,4},{4,5},{5,6},{6,7},{8,9},{9,10},{10,11},{11... | collective-permute-start | bytes 196616 | tf_op jit(solution)/shard_map/ppermute | solution.py:253
  9.5 1.9 %collective-permute-start.1 = (bf16[256,128]{1,0:T(8,128)(2,1)}, bf16[256,128]{1,0:T(8,128)(2,1)S(1)}, u32[]{:S(2)}, u32[]{:S(2)}) collective-permute-start(bf16[256,128]{1,0:T(8,128)(2,1)} %get-tuple-element.13), channel_id=1, source_target_pairs={{1,0},{2,1},{3,2},{4,3},{5,4},{6,5},{7,6},{9,8},{10,9},{11,10},{12... | collective-permute-start | bytes 196616 | tf_op jit(solution)/shard_map/ppermute | solution.py:253
  14.2 5.8 %product.2.base_ref = f32[2048,128]{1,0:T(8,128)} custom-call(s32[112]{0:T(128)} %reshape_squeeze.11.cols_ref, bf16[16,7,128,128]{3,2,1,0:T(8,128)(2,1)} %bitcast.18, f32[2048,128]{1,0:T(8,128)} %bitcast.21, f32[2048,128]{1,0:T(8,128)} %bitcast.23), custom_call_target="tpu_custom_call" | custom-call | flops 469762048 | bytes 8000000 | tf_op jit(solution)/shard_map/product/pallas_call | solution.py:172
  20.6 7.7 %partial.2 = (f32[2048,128]{1,0:T(8,128)}, f32[4,8,32,128]{3,2,1,0:T(8,128)}, bf16[4,8,32,128]{3,2,1,0:T(8,128)(2,1)}) custom-call(s32[128]{0:T(128)} %reshape_squeeze.9.cols_ref, s32[512]{0:T(512)} %bitcast.29, s32[1]{0:T(128)} %bitcast.me_ref, bf16[16,8,128,128]{3,2,1,0:T(8,128)(2,1)} %bitcast.14, f32[2048,128]{1,0:T(8,128)} %product.2.base_ref, ...), custom_call_target="tpu_custom_call" | custom-call | flops 536870912 | bytes 8000000 | tf_op jit(solution)/shard_map/partial/pallas_call | solution.py:194
  28.3 1.7 %collective-permute-done.2 = bf16[4,8,32,128]{3,2,1,0:T(8,128)(2,1)S(1)} collective-permute-done((bf16[4,8,32,128]{3,2,1,0:T(8,128)(2,1)}, bf16[4,8,32,128]{3,2,1,0:T(8,128)(2,1)S(1)}, u32[]{:S(2)}, u32[]{:S(2)}) %collective-permute-start.2) | collective-permute-done | bytes 262176 | tf_op jit(solution)/shard_map/ppermute | solution.py:247
  32.8 3.1 %collective-permute-done.3 = bf16[2,7,32,128]{3,2,1,0:T(8,128)(2,1)S(1)} collective-permute-done((bf16[2,7,32,128]{3,2,1,0:T(8,128)(2,1)S(1)}, bf16[2,7,32,128]{3,2,1,0:T(8,128)(2,1)S(1)}, u32[]{:S(2)}, u32[]{:S(2)}) %collective-permute-start.3) | collective-permute-done | bytes 114720 | tf_op jit(solution)/shard_map/ppermute | solution.py:247
  36.0 2.6 %collective-permute-start.4 = (bf16[1,6,32,128]{3,2,1,0:T(8,128)(2,1)S(1)}, bf16[1,6,32,128]{3,2,1,0:T(8,128)(2,1)S(1)}, u32[]{:S(2)}, u32[]{:S(2)}) collective-permute-start(bf16[1,6,32,128]{3,2,1,0:T(8,128)(2,1)S(1)} %slice.261), channel_id=1, source_target_pairs={{0,6},{1,7},{2,4},{3,5},{4,2},{5,3},{6,0},{7,1},{8,14},{9,15},{10,... | collective-permute-start | bytes 147464 | tf_op jit(solution)/shard_map/ppermute | solution.py:247
  40.2 1.7 %collective-permute-start.5 = (bf16[1,5,32,128]{3,2,1,0:T(8,128)(2,1)S(1)}, bf16[1,5,32,128]{3,2,1,0:T(8,128)(2,1)S(1)}, u32[]{:S(2)}, u32[]{:S(2)}) collective-permute-start(bf16[1,5,32,128]{3,2,1,0:T(8,128)(2,1)S(1)} %slice.263), channel_id=1, source_target_pairs={{0,8},{8,0},{16,24},{24,16},{32,40},{40,32},{48,56},{56,48},{64,72... | collective-permute-start | bytes 122888 | tf_op jit(solution)/shard_map/ppermute | solution.py:247
  43.4 3.1 %collective-permute-start.6 = (bf16[1,4,32,128]{3,2,1,0:T(8,128)(2,1)S(1)}, bf16[1,4,32,128]{3,2,1,0:T(8,128)(2,1)S(1)}, u32[]{:S(2)}, u32[]{:S(2)}) collective-permute-start(bf16[1,4,32,128]{3,2,1,0:T(8,128)(2,1)S(1)} %slice.265), channel_id=1, source_target_pairs={{0,16},{8,24},{16,0},{24,8},{32,48},{40,56},{48,32},{56,40},{64,80... | collective-permute-start | bytes 98312 | tf_op jit(solution)/shard_map/ppermute | solution.py:247
  47.8 5.3 %collective-permute-start.7 = (bf16[1,3,32,128]{3,2,1,0:T(8,128)(2,1)S(1)}, bf16[1,3,32,128]{3,2,1,0:T(8,128)(2,1)S(1)}, u32[]{:S(2)}, u32[]{:S(2)}) collective-permute-start(bf16[1,3,32,128]{3,2,1,0:T(8,128)(2,1)S(1)} %slice.267), channel_id=1, source_target_pairs={{0,48},{8,56},{16,32},{24,40},{32,16},{40,24},{48,0},{56,8},{64,11... | collective-permute-start | bytes 73736 | tf_op jit(solution)/shard_map/ppermute | solution.py:247
  57.0 2.8 %collective-permute-start.9 = (bf16[1,1,32,128]{3,2,1,0:T(8,128)(2,1)S(1)}, bf16[1,1,32,128]{3,2,1,0:T(8,128)(2,1)S(1)}, u32[]{:S(2)}, u32[]{:S(2)}) collective-permute-start(bf16[1,1,32,128]{3,2,1,0:T(8,128)(2,1)S(1)} %get-tuple-element.24), channel_id=1, source_target_pairs={{0,192},{8,200},{16,208},{24,216},{32,224},{40,232},{48,240},{56,2... | collective-permute-start | bytes 24584 | tf_op jit(solution)/shard_map/ppermute | solution.py:247
  60.9 2.5 %collective-permute-start.10 = (bf16[1,6,32,128]{3,2,1,0:T(8,128)(2,1)S(1)}, bf16[1,6,32,128]{3,2,1,0:T(8,128)(2,1)S(1)}, u32[]{:S(2)}, u32[]{:S(2)}) collective-permute-start(bf16[1,6,32,128]{3,2,1,0:T(8,128)(2,1)S(1)} %constant_dynamic-update-slice_fusion), channel_id=1, source_target_pairs={{0,6},{1,7},{2,4},{3,5},{4,2},{5,3},{6,0},{7,1},{8,14},{9,15},{10,... | collective-permute-start | bytes 147464 | tf_op jit(solution)/shard_map/ppermute | solution.py:247
  65.2 3.6 %collective-permute-done.11 = bf16[2,7,32,128]{3,2,1,0:T(8,128)(2,1)S(1)} collective-permute-done((bf16[2,7,32,128]{3,2,1,0:T(8,128)(2,1)S(1)}, bf16[2,7,32,128]{3,2,1,0:T(8,128)(2,1)S(1)}, u32[]{:S(2)}, u32[]{:S(2)}) %collective-permute-start.11) | collective-permute-done | bytes 114720 | tf_op jit(solution)/shard_map/ppermute | solution.py:247
  68.9 9.9 %collective-permute-start.12 = (bf16[4,8,32,128]{3,2,1,0:T(8,128)(2,1)S(1)}, bf16[4,8,32,128]{3,2,1,0:T(8,128)(2,1)S(1)}, u32[]{:S(2)}, u32[]{:S(2)}) collective-permute-start(bf16[4,8,32,128]{3,2,1,0:T(8,128)(2,1)S(1)} %maximum_maximum_fusion.own_ref), channel_id=1, source_target_pairs={{0,1},{1,0},{2,3},{3,2},{4,5},{5,4},{6,7},{7,6},{8,9},{9,8},{10,11... | collective-permute-start | bytes 786440 | tf_op jit(solution)/shard_map/ppermute | solution.py:247
  80.7 6.7 %update.2 = (f32[2048,128]{1,0:T(8,128)}, bf16[256,128]{1,0:T(8,128)(2,1)}, bf16[256,128]{1,0:T(8,128)(2,1)}) custom-call(s32[128]{0:T(128)} %reshape_squeeze.9.cols_ref, s32[512]{0:T(512)} %bitcast.30, s32[1]{0:T(128)} %bitcast.me_ref, bf16[16,8,128,128]{3,2,1,0:T(8,128)(2,1)} %bitcast.15, bf16[4,8,32,128]{3,2,1,0:T(8,128)(2,1)} %copy-done, ...), custom_call_target="tpu_custom_call" | custom-call | flops 536870912 | bytes 8000000 | tf_op jit(solution)/shard_map/update/pallas_call | solution.py:224
  87.4 1.9 %collective-permute-start.13 = (bf16[256,128]{1,0:T(8,128)(2,1)}, bf16[256,128]{1,0:T(8,128)(2,1)S(1)}, u32[]{:S(2)}, u32[]{:S(2)}) collective-permute-start(bf16[256,128]{1,0:T(8,128)(2,1)} %get-tuple-element.17), channel_id=1, source_target_pairs={{0,1},{1,2},{2,3},{3,4},{4,5},{5,6},{6,7},{8,9},{9,10},{10,11},{11... | collective-permute-start | bytes 196616 | tf_op jit(solution)/shard_map/ppermute | solution.py:253
  89.4 2.4 %collective-permute-start.14 = (bf16[256,128]{1,0:T(8,128)(2,1)}, bf16[256,128]{1,0:T(8,128)(2,1)S(1)}, u32[]{:S(2)}, u32[]{:S(2)}) collective-permute-start(bf16[256,128]{1,0:T(8,128)(2,1)} %get-tuple-element.18), channel_id=1, source_target_pairs={{1,0},{2,1},{3,2},{4,3},{5,4},{6,5},{7,6},{9,8},{10,9},{11,10},{12... | collective-permute-start | bytes 196616 | tf_op jit(solution)/shard_map/ppermute | solution.py:253
  91.8 5.8 %product.3.base_ref = f32[2048,128]{1,0:T(8,128)} custom-call(s32[112]{0:T(128)} %reshape_squeeze.11.cols_ref, bf16[16,7,128,128]{3,2,1,0:T(8,128)(2,1)} %bitcast.19, f32[2048,128]{1,0:T(8,128)} %get-tuple-element.16.cur_ref, f32[2048,128]{1,0:T(8,128)} %bitcast.24), custom_call_target="tpu_custom_call" | custom-call | flops 469762048 | bytes 8000000 | tf_op jit(solution)/shard_map/product/pallas_call | solution.py:172
  98.8 7.7 %partial.3 = (f32[2048,128]{1,0:T(8,128)}, f32[4,8,32,128]{3,2,1,0:T(8,128)}, bf16[4,8,32,128]{3,2,1,0:T(8,128)(2,1)}) custom-call(s32[128]{0:T(128)} %reshape_squeeze.9.cols_ref, s32[512]{0:T(512)} %bitcast.31, s32[1]{0:T(128)} %bitcast.me_ref, bf16[16,8,128,128]{3,2,1,0:T(8,128)(2,1)} %bitcast.16, f32[2048,128]{1,0:T(8,128)} %product.3.base_ref, ...), custom_call_target="tpu_custom_call" | custom-call | flops 536870912 | bytes 8000000 | tf_op jit(solution)/shard_map/partial/pallas_call | solution.py:194
  106.5 1.7 %collective-permute-done.15 = bf16[4,8,32,128]{3,2,1,0:T(8,128)(2,1)S(1)} collective-permute-done((bf16[4,8,32,128]{3,2,1,0:T(8,128)(2,1)}, bf16[4,8,32,128]{3,2,1,0:T(8,128)(2,1)S(1)}, u32[]{:S(2)}, u32[]{:S(2)}) %collective-permute-start.15) | collective-permute-done | bytes 262176 | tf_op jit(solution)/shard_map/ppermute | solution.py:247
  111.1 3.3 %collective-permute-done.16 = bf16[2,7,32,128]{3,2,1,0:T(8,128)(2,1)S(1)} collective-permute-done((bf16[2,7,32,128]{3,2,1,0:T(8,128)(2,1)S(1)}, bf16[2,7,32,128]{3,2,1,0:T(8,128)(2,1)S(1)}, u32[]{:S(2)}, u32[]{:S(2)}) %collective-permute-start.16) | collective-permute-done | bytes 114720 | tf_op jit(solution)/shard_map/ppermute | solution.py:247
  114.4 3.5 %collective-permute-start.17 = (bf16[1,6,32,128]{3,2,1,0:T(8,128)(2,1)S(1)}, bf16[1,6,32,128]{3,2,1,0:T(8,128)(2,1)S(1)}, u32[]{:S(2)}, u32[]{:S(2)}) collective-permute-start(bf16[1,6,32,128]{3,2,1,0:T(8,128)(2,1)S(1)} %slice.260), channel_id=1, source_target_pairs={{0,6},{1,7},{2,4},{3,5},{4,2},{5,3},{6,0},{7,1},{8,14},{9,15},{10,... | collective-permute-start | bytes 147464 | tf_op jit(solution)/shard_map/ppermute | solution.py:247
  120.4 2.1 %collective-permute-done.18 = bf16[1,5,32,128]{3,2,1,0:T(8,128)(2,1)S(1)} collective-permute-done((bf16[1,5,32,128]{3,2,1,0:T(8,128)(2,1)S(1)}, bf16[1,5,32,128]{3,2,1,0:T(8,128)(2,1)S(1)}, u32[]{:S(2)}, u32[]{:S(2)}) %collective-permute-start.18) | collective-permute-done | bytes 40992 | tf_op jit(solution)/shard_map/ppermute | solution.py:247
  123.9 2.5 %collective-permute-done.19 = bf16[1,4,32,128]{3,2,1,0:T(8,128)(2,1)S(1)} collective-permute-done((bf16[1,4,32,128]{3,2,1,0:T(8,128)(2,1)S(1)}, bf16[1,4,32,128]{3,2,1,0:T(8,128)(2,1)S(1)}, u32[]{:S(2)}, u32[]{:S(2)}) %collective-permute-start.19) | collective-permute-done | bytes 32800 | tf_op jit(solution)/shard_map/ppermute | solution.py:247
  126.4 3.9 %collective-permute-start.20 = (bf16[1,3,32,128]{3,2,1,0:T(8,128)(2,1)S(1)}, bf16[1,3,32,128]{3,2,1,0:T(8,128)(2,1)S(1)}, u32[]{:S(2)}, u32[]{:S(2)}) collective-permute-start(bf16[1,3,32,128]{3,2,1,0:T(8,128)(2,1)S(1)} %slice.266), channel_id=1, source_target_pairs={{0,48},{8,56},{16,32},{24,40},{32,16},{40,24},{48,0},{56,8},{64,11... | collective-permute-start | bytes 73736 | tf_op jit(solution)/shard_map/ppermute | solution.py:247
  131.7 2.5 %collective-permute-done.21 = bf16[1,2,32,128]{3,2,1,0:T(8,128)(2,1)S(1)} collective-permute-done((bf16[1,2,32,128]{3,2,1,0:T(8,128)(2,1)S(1)}, bf16[1,2,32,128]{3,2,1,0:T(8,128)(2,1)S(1)}, u32[]{:S(2)}, u32[]{:S(2)}) %collective-permute-start.21) | collective-permute-done | bytes 16416 | tf_op jit(solution)/shard_map/ppermute | solution.py:247
  134.2 2.8 %collective-permute-start.22 = (bf16[1,1,32,128]{3,2,1,0:T(8,128)(2,1)S(1)}, bf16[1,1,32,128]{3,2,1,0:T(8,128)(2,1)S(1)}, u32[]{:S(2)}, u32[]{:S(2)}) collective-permute-start(bf16[1,1,32,128]{3,2,1,0:T(8,128)(2,1)S(1)} %get-tuple-element.22), channel_id=1, source_target_pairs={{0,192},{8,200},{16,208},{24,216},{32,224},{40,232},{48,240},{56,2... | collective-permute-start | bytes 24584 | tf_op jit(solution)/shard_map/ppermute | solution.py:247
  138.1 2.7 %collective-permute-start.23 = (bf16[1,6,32,128]{3,2,1,0:T(8,128)(2,1)S(1)}, bf16[1,6,32,128]{3,2,1,0:T(8,128)(2,1)S(1)}, u32[]{:S(2)}, u32[]{:S(2)}) collective-permute-start(bf16[1,6,32,128]{3,2,1,0:T(8,128)(2,1)S(1)} %constant_dynamic-update-slice_fusion.6), channel_id=1, source_target_pairs={{0,6},{1,7},{2,4},{3,5},{4,2},{5,3},{6,0},{7,1},{8,14},{9,15},{10,... | collective-permute-start | bytes 147464 | tf_op jit(solution)/shard_map/ppermute | solution.py:247
  142.5 3.6 %collective-permute-done.24 = bf16[2,7,32,128]{3,2,1,0:T(8,128)(2,1)S(1)} collective-permute-done((bf16[2,7,32,128]{3,2,1,0:T(8,128)(2,1)S(1)}, bf16[2,7,32,128]{3,2,1,0:T(8,128)(2,1)S(1)}, u32[]{:S(2)}, u32[]{:S(2)}) %collective-permute-start.24) | collective-permute-done | bytes 114720 | tf_op jit(solution)/shard_map/ppermute | solution.py:247
  146.1 9.9 %collective-permute-start.25 = (bf16[4,8,32,128]{3,2,1,0:T(8,128)(2,1)S(1)}, bf16[4,8,32,128]{3,2,1,0:T(8,128)(2,1)S(1)}, u32[]{:S(2)}, u32[]{:S(2)}) collective-permute-start(bf16[4,8,32,128]{3,2,1,0:T(8,128)(2,1)S(1)} %maximum_maximum_fusion.1.own_ref), channel_id=1, source_target_pairs={{0,1},{1,0},{2,3},{3,2},{4,5},{5,4},{6,7},{7,6},{8,9},{9,8},{10,11... | collective-permute-start | bytes 786440 | tf_op jit(solution)/shard_map/ppermute | solution.py:247
  157.9 6.1 %update.3 = f32[2048,128]{1,0:T(8,128)} custom-call(s32[128]{0:T(128)} %reshape_squeeze.9.cols_ref, s32[512]{0:T(512)} %bitcast.32, s32[1]{0:T(128)} %bitcast.me_ref, bf16[16,8,128,128]{3,2,1,0:T(8,128)(2,1)} %bitcast.17, bf16[4,8,32,128]{3,2,1,0:T(8,128)(2,1)} %copy-done.1, bf16[4,8,32,128]{3,2,1,0:T(8,128)(2,1)} %copy-done.3, ...), custom_call_target="tpu_custom_call" | custom-call | flops 536870912 | bytes 8000000 | tf_op jit(solution)/shard_map/update/pallas_call | solution.py:224
  (94 shorter events, 34.4 us)
Async XLA Ops:
  5.0 15.0 %collective-permute-start = (bf16[256,128]{1,0:T(8,128)(2,1)}, bf16[256,128]{1,0:T(8,128)(2,1)S(1)}, u32[]{:S(2)}, u32[]{:S(2)}) collective-permute-start(bf16[256,128]{1,0:T(8,128)(2,1)} %get-tuple-element.12), channel_id=1, source_target_pairs={{0,1},{1,2},{2,3},{3,4},{4,5},{5,6},{6,7},{8,9},{9,10},{10,11},{11... | collective-permute-start | bytes 196616 | tf_op jit(solution)/shard_map/ppermute | solution.py:253
  9.5 10.5 %collective-permute-start.1 = (bf16[256,128]{1,0:T(8,128)(2,1)}, bf16[256,128]{1,0:T(8,128)(2,1)S(1)}, u32[]{:S(2)}, u32[]{:S(2)}) collective-permute-start(bf16[256,128]{1,0:T(8,128)(2,1)} %get-tuple-element.13), channel_id=1, source_target_pairs={{1,0},{2,1},{3,2},{4,3},{5,4},{6,5},{7,6},{9,8},{10,9},{11,10},{12... | collective-permute-start | bytes 196616 | tf_op jit(solution)/shard_map/ppermute | solution.py:253
  20.0 0.6 copy-start.4
  20.0 0.6 copy-start.5
  28.3 1.7 %collective-permute-start.2 = (bf16[4,8,32,128]{3,2,1,0:T(8,128)(2,1)}, bf16[4,8,32,128]{3,2,1,0:T(8,128)(2,1)S(1)}, u32[]{:S(2)}, u32[]{:S(2)}) collective-permute-start(bf16[4,8,32,128]{3,2,1,0:T(8,128)(2,1)} %get-tuple-element.15), channel_id=1, source_target_pairs={{0,1},{1,0},{2,3},{3,2},{4,5},{5,4},{6,7},{7,6},{8,9},{9,8},{10,11... | collective-permute-start | bytes 786440 | tf_op jit(solution)/shard_map/ppermute | solution.py:247
  31.2 4.7 %collective-permute-start.3 = (bf16[2,7,32,128]{3,2,1,0:T(8,128)(2,1)S(1)}, bf16[2,7,32,128]{3,2,1,0:T(8,128)(2,1)S(1)}, u32[]{:S(2)}, u32[]{:S(2)}) collective-permute-start(bf16[2,7,32,128]{3,2,1,0:T(8,128)(2,1)S(1)} %slice.259), channel_id=1, source_target_pairs={{0,2},{1,3},{2,0},{3,1},{4,6},{5,7},{6,4},{7,5},{8,10},{9,11},{10,... | collective-permute-start | bytes 344072 | tf_op jit(solution)/shard_map/ppermute | solution.py:247
  36.0 4.2 %collective-permute-start.4 = (bf16[1,6,32,128]{3,2,1,0:T(8,128)(2,1)S(1)}, bf16[1,6,32,128]{3,2,1,0:T(8,128)(2,1)S(1)}, u32[]{:S(2)}, u32[]{:S(2)}) collective-permute-start(bf16[1,6,32,128]{3,2,1,0:T(8,128)(2,1)S(1)} %slice.261), channel_id=1, source_target_pairs={{0,6},{1,7},{2,4},{3,5},{4,2},{5,3},{6,0},{7,1},{8,14},{9,15},{10,... | collective-permute-start | bytes 147464 | tf_op jit(solution)/shard_map/ppermute | solution.py:247
  40.2 3.1 %collective-permute-start.5 = (bf16[1,5,32,128]{3,2,1,0:T(8,128)(2,1)S(1)}, bf16[1,5,32,128]{3,2,1,0:T(8,128)(2,1)S(1)}, u32[]{:S(2)}, u32[]{:S(2)}) collective-permute-start(bf16[1,5,32,128]{3,2,1,0:T(8,128)(2,1)S(1)} %slice.263), channel_id=1, source_target_pairs={{0,8},{8,0},{16,24},{24,16},{32,40},{40,32},{48,56},{56,48},{64,72... | collective-permute-start | bytes 122888 | tf_op jit(solution)/shard_map/ppermute | solution.py:247
  43.4 4.4 %collective-permute-start.6 = (bf16[1,4,32,128]{3,2,1,0:T(8,128)(2,1)S(1)}, bf16[1,4,32,128]{3,2,1,0:T(8,128)(2,1)S(1)}, u32[]{:S(2)}, u32[]{:S(2)}) collective-permute-start(bf16[1,4,32,128]{3,2,1,0:T(8,128)(2,1)S(1)} %slice.265), channel_id=1, source_target_pairs={{0,16},{8,24},{16,0},{24,8},{32,48},{40,56},{48,32},{56,40},{64,80... | collective-permute-start | bytes 98312 | tf_op jit(solution)/shard_map/ppermute | solution.py:247
  47.8 6.5 %collective-permute-start.7 = (bf16[1,3,32,128]{3,2,1,0:T(8,128)(2,1)S(1)}, bf16[1,3,32,128]{3,2,1,0:T(8,128)(2,1)S(1)}, u32[]{:S(2)}, u32[]{:S(2)}) collective-permute-start(bf16[1,3,32,128]{3,2,1,0:T(8,128)(2,1)S(1)} %slice.267), channel_id=1, source_target_pairs={{0,48},{8,56},{16,32},{24,40},{32,16},{40,24},{48,0},{56,8},{64,11... | collective-permute-start | bytes 73736 | tf_op jit(solution)/shard_map/ppermute | solution.py:247
  54.3 2.7 %collective-permute-start.8 = (bf16[1,2,32,128]{3,2,1,0:T(8,128)(2,1)S(1)}, bf16[1,2,32,128]{3,2,1,0:T(8,128)(2,1)S(1)}, u32[]{:S(2)}, u32[]{:S(2)}) collective-permute-start(bf16[1,2,32,128]{3,2,1,0:T(8,128)(2,1)S(1)} %slice.269), channel_id=1, source_target_pairs={{0,64},{8,72},{16,80},{24,88},{32,96},{40,104},{48,112},{56,120},{... | collective-permute-start | bytes 49160 | tf_op jit(solution)/shard_map/ppermute | solution.py:247
  57.0 3.9 %collective-permute-start.9 = (bf16[1,1,32,128]{3,2,1,0:T(8,128)(2,1)S(1)}, bf16[1,1,32,128]{3,2,1,0:T(8,128)(2,1)S(1)}, u32[]{:S(2)}, u32[]{:S(2)}) collective-permute-start(bf16[1,1,32,128]{3,2,1,0:T(8,128)(2,1)S(1)} %get-tuple-element.24), channel_id=1, source_target_pairs={{0,192},{8,200},{16,208},{24,216},{32,224},{40,232},{48,240},{56,2... | collective-permute-start | bytes 24584 | tf_op jit(solution)/shard_map/ppermute | solution.py:247
  60.9 4.2 %collective-permute-start.10 = (bf16[1,6,32,128]{3,2,1,0:T(8,128)(2,1)S(1)}, bf16[1,6,32,128]{3,2,1,0:T(8,128)(2,1)S(1)}, u32[]{:S(2)}, u32[]{:S(2)}) collective-permute-start(bf16[1,6,32,128]{3,2,1,0:T(8,128)(2,1)S(1)} %constant_dynamic-update-slice_fusion), channel_id=1, source_target_pairs={{0,6},{1,7},{2,4},{3,5},{4,2},{5,3},{6,0},{7,1},{8,14},{9,15},{10,... | collective-permute-start | bytes 147464 | tf_op jit(solution)/shard_map/ppermute | solution.py:247
  65.1 3.7 %collective-permute-start.11 = (bf16[2,7,32,128]{3,2,1,0:T(8,128)(2,1)S(1)}, bf16[2,7,32,128]{3,2,1,0:T(8,128)(2,1)S(1)}, u32[]{:S(2)}, u32[]{:S(2)}) collective-permute-start(bf16[2,7,32,128]{3,2,1,0:T(8,128)(2,1)S(1)} %maximum_maximum_fusion.2), channel_id=1, source_target_pairs={{0,2},{1,3},{2,0},{3,1},{4,6},{5,7},{6,4},{7,5},{8,10},{9,11},{10,... | collective-permute-start | bytes 344072 | tf_op jit(solution)/shard_map/ppermute | solution.py:247
  68.9 11.1 %copy-start = (bf16[4,8,32,128]{3,2,1,0:T(8,128)(2,1)}, bf16[4,8,32,128]{3,2,1,0:T(8,128)(2,1)S(1)}, u32[]{:S(2)}) copy-start(bf16[4,8,32,128]{3,2,1,0:T(8,128)(2,1)S(1)} %maximum_maximum_fusion.own_ref) | copy-start | bytes 786436
  68.9 11.1 %collective-permute-start.12 = (bf16[4,8,32,128]{3,2,1,0:T(8,128)(2,1)S(1)}, bf16[4,8,32,128]{3,2,1,0:T(8,128)(2,1)S(1)}, u32[]{:S(2)}, u32[]{:S(2)}) collective-permute-start(bf16[4,8,32,128]{3,2,1,0:T(8,128)(2,1)S(1)} %maximum_maximum_fusion.own_ref), channel_id=1, source_target_pairs={{0,1},{1,0},{2,3},{3,2},{4,5},{5,4},{6,7},{7,6},{8,9},{9,8},{10,11... | collective-permute-start | bytes 786440 | tf_op jit(solution)/shard_map/ppermute | solution.py:247
  80.0 0.7 copy-start.2
  87.4 10.2 %collective-permute-start.13 = (bf16[256,128]{1,0:T(8,128)(2,1)}, bf16[256,128]{1,0:T(8,128)(2,1)S(1)}, u32[]{:S(2)}, u32[]{:S(2)}) collective-permute-start(bf16[256,128]{1,0:T(8,128)(2,1)} %get-tuple-element.17), channel_id=1, source_target_pairs={{0,1},{1,2},{2,3},{3,4},{4,5},{5,6},{6,7},{8,9},{9,10},{10,11},{11... | collective-permute-start | bytes 196616 | tf_op jit(solution)/shard_map/ppermute | solution.py:253
  89.4 8.3 %collective-permute-start.14 = (bf16[256,128]{1,0:T(8,128)(2,1)}, bf16[256,128]{1,0:T(8,128)(2,1)S(1)}, u32[]{:S(2)}, u32[]{:S(2)}) collective-permute-start(bf16[256,128]{1,0:T(8,128)(2,1)} %get-tuple-element.18), channel_id=1, source_target_pairs={{1,0},{2,1},{3,2},{4,3},{5,4},{6,5},{7,6},{9,8},{10,9},{11,10},{12... | collective-permute-start | bytes 196616 | tf_op jit(solution)/shard_map/ppermute | solution.py:253
  106.5 1.7 %collective-permute-start.15 = (bf16[4,8,32,128]{3,2,1,0:T(8,128)(2,1)}, bf16[4,8,32,128]{3,2,1,0:T(8,128)(2,1)S(1)}, u32[]{:S(2)}, u32[]{:S(2)}) collective-permute-start(bf16[4,8,32,128]{3,2,1,0:T(8,128)(2,1)} %get-tuple-element.20), channel_id=1, source_target_pairs={{0,1},{1,0},{2,3},{3,2},{4,5},{5,4},{6,7},{7,6},{8,9},{9,8},{10,11... | collective-permute-start | bytes 786440 | tf_op jit(solution)/shard_map/ppermute | solution.py:247
  109.4 5.0 %collective-permute-start.16 = (bf16[2,7,32,128]{3,2,1,0:T(8,128)(2,1)S(1)}, bf16[2,7,32,128]{3,2,1,0:T(8,128)(2,1)S(1)}, u32[]{:S(2)}, u32[]{:S(2)}) collective-permute-start(bf16[2,7,32,128]{3,2,1,0:T(8,128)(2,1)S(1)} %slice.258), channel_id=1, source_target_pairs={{0,2},{1,3},{2,0},{3,1},{4,6},{5,7},{6,4},{7,5},{8,10},{9,11},{10,... | collective-permute-start | bytes 344072 | tf_op jit(solution)/shard_map/ppermute | solution.py:247
  114.4 5.0 %collective-permute-start.17 = (bf16[1,6,32,128]{3,2,1,0:T(8,128)(2,1)S(1)}, bf16[1,6,32,128]{3,2,1,0:T(8,128)(2,1)S(1)}, u32[]{:S(2)}, u32[]{:S(2)}) collective-permute-start(bf16[1,6,32,128]{3,2,1,0:T(8,128)(2,1)S(1)} %slice.260), channel_id=1, source_target_pairs={{0,6},{1,7},{2,4},{3,5},{4,2},{5,3},{6,0},{7,1},{8,14},{9,15},{10,... | collective-permute-start | bytes 147464 | tf_op jit(solution)/shard_map/ppermute | solution.py:247
  119.4 3.1 %collective-permute-start.18 = (bf16[1,5,32,128]{3,2,1,0:T(8,128)(2,1)S(1)}, bf16[1,5,32,128]{3,2,1,0:T(8,128)(2,1)S(1)}, u32[]{:S(2)}, u32[]{:S(2)}) collective-permute-start(bf16[1,5,32,128]{3,2,1,0:T(8,128)(2,1)S(1)} %slice.262), channel_id=1, source_target_pairs={{0,8},{8,0},{16,24},{24,16},{32,40},{40,32},{48,56},{56,48},{64,72... | collective-permute-start | bytes 122888 | tf_op jit(solution)/shard_map/ppermute | solution.py:247
  122.6 3.8 %collective-permute-start.19 = (bf16[1,4,32,128]{3,2,1,0:T(8,128)(2,1)S(1)}, bf16[1,4,32,128]{3,2,1,0:T(8,128)(2,1)S(1)}, u32[]{:S(2)}, u32[]{:S(2)}) collective-permute-start(bf16[1,4,32,128]{3,2,1,0:T(8,128)(2,1)S(1)} %slice.264), channel_id=1, source_target_pairs={{0,16},{8,24},{16,0},{24,8},{32,48},{40,56},{48,32},{56,40},{64,80... | collective-permute-start | bytes 98312 | tf_op jit(solution)/shard_map/ppermute | solution.py:247
  126.4 5.2 %collective-permute-start.20 = (bf16[1,3,32,128]{3,2,1,0:T(8,128)(2,1)S(1)}, bf16[1,3,32,128]{3,2,1,0:T(8,128)(2,1)S(1)}, u32[]{:S(2)}, u32[]{:S(2)}) collective-permute-start(bf16[1,3,32,128]{3,2,1,0:T(8,128)(2,1)S(1)} %slice.266), channel_id=1, source_target_pairs={{0,48},{8,56},{16,32},{24,40},{32,16},{40,24},{48,0},{56,8},{64,11... | collective-permute-start | bytes 73736 | tf_op jit(solution)/shard_map/ppermute | solution.py:247
  131.5 2.7 %collective-permute-start.21 = (bf16[1,2,32,128]{3,2,1,0:T(8,128)(2,1)S(1)}, bf16[1,2,32,128]{3,2,1,0:T(8,128)(2,1)S(1)}, u32[]{:S(2)}, u32[]{:S(2)}) collective-permute-start(bf16[1,2,32,128]{3,2,1,0:T(8,128)(2,1)S(1)} %slice.268), channel_id=1, source_target_pairs={{0,64},{8,72},{16,80},{24,88},{32,96},{40,104},{48,112},{56,120},{... | collective-permute-start | bytes 49160 | tf_op jit(solution)/shard_map/ppermute | solution.py:247
  134.2 3.9 %collective-permute-start.22 = (bf16[1,1,32,128]{3,2,1,0:T(8,128)(2,1)S(1)}, bf16[1,1,32,128]{3,2,1,0:T(8,128)(2,1)S(1)}, u32[]{:S(2)}, u32[]{:S(2)}) collective-permute-start(bf16[1,1,32,128]{3,2,1,0:T(8,128)(2,1)S(1)} %get-tuple-element.22), channel_id=1, source_target_pairs={{0,192},{8,200},{16,208},{24,216},{32,224},{40,232},{48,240},{56,2... | collective-permute-start | bytes 24584 | tf_op jit(solution)/shard_map/ppermute | solution.py:247
  138.1 4.2 %collective-permute-start.23 = (bf16[1,6,32,128]{3,2,1,0:T(8,128)(2,1)S(1)}, bf16[1,6,32,128]{3,2,1,0:T(8,128)(2,1)S(1)}, u32[]{:S(2)}, u32[]{:S(2)}) collective-permute-start(bf16[1,6,32,128]{3,2,1,0:T(8,128)(2,1)S(1)} %constant_dynamic-update-slice_fusion.6), channel_id=1, source_target_pairs={{0,6},{1,7},{2,4},{3,5},{4,2},{5,3},{6,0},{7,1},{8,14},{9,15},{10,... | collective-permute-start | bytes 147464 | tf_op jit(solution)/shard_map/ppermute | solution.py:247
  142.4 3.7 %collective-permute-start.24 = (bf16[2,7,32,128]{3,2,1,0:T(8,128)(2,1)S(1)}, bf16[2,7,32,128]{3,2,1,0:T(8,128)(2,1)S(1)}, u32[]{:S(2)}, u32[]{:S(2)}) collective-permute-start(bf16[2,7,32,128]{3,2,1,0:T(8,128)(2,1)S(1)} %maximum_maximum_fusion.3), channel_id=1, source_target_pairs={{0,2},{1,3},{2,0},{3,1},{4,6},{5,7},{6,4},{7,5},{8,10},{9,11},{10,... | collective-permute-start | bytes 344072 | tf_op jit(solution)/shard_map/ppermute | solution.py:247
  146.1 11.1 %copy-start.1 = (bf16[4,8,32,128]{3,2,1,0:T(8,128)(2,1)}, bf16[4,8,32,128]{3,2,1,0:T(8,128)(2,1)S(1)}, u32[]{:S(2)}) copy-start(bf16[4,8,32,128]{3,2,1,0:T(8,128)(2,1)S(1)} %maximum_maximum_fusion.1.own_ref) | copy-start | bytes 786436
  146.1 11.0 %collective-permute-start.25 = (bf16[4,8,32,128]{3,2,1,0:T(8,128)(2,1)S(1)}, bf16[4,8,32,128]{3,2,1,0:T(8,128)(2,1)S(1)}, u32[]{:S(2)}, u32[]{:S(2)}) collective-permute-start(bf16[4,8,32,128]{3,2,1,0:T(8,128)(2,1)S(1)} %maximum_maximum_fusion.1.own_ref), channel_id=1, source_target_pairs={{0,1},{1,0},{2,3},{3,2},{4,5},{5,4},{6,7},{7,6},{8,9},{9,8},{10,11... | collective-permute-start | bytes 786440 | tf_op jit(solution)/shard_map/ppermute | solution.py:247
  157.2 0.7 copy-start.3
  (2 other events, 1.2 us)
where the time goes:
time: 165 us; the launch traced here: 164 us
  starting transfers between devices  68.8 us (42%)
  Pallas kernels  43 us (26%)
  waiting for transfers between devices  41.3 us (25%)
  local copies, waits for them, and re-layouts  7.37 us (4%)
  other arithmetic  2.63 us (2%)
    ppermute x22, starting transfers between devices, swapped(): lax.ppermute(value, axis, [(i, i ^ mask) for i in range(lax.axis_size(axi...  58.1 us
    ppermute x22, waiting for transfers between devices, swapped(): lax.ppermute(value, axis, [(i, i ^ mask) for i in range(lax.axis_size(axi...  41.3 us
    pallas_call x2, Pallas kernels, partial_of(): pl.pallas_call(partial_kernel, grid_spec=pltpu.PrefetchScalarGridSpec(num...  15.3 us
    pallas_call x2, Pallas kernels, update_of(): pl.pallas_call(functools.partial(update_kernel, gather), grid_spec=pltpu....  12.8 us
    pallas_call x2, Pallas kernels, base_of(): pl.pallas_call(product_kernel, grid_spec=pltpu.PrefetchScalarGridSpec(num...  11.7 us
    ppermute x4, starting transfers between devices, shifted(): return lax.ppermute(value, 'narrow', pairs)  10.7 us
    unnamed x19, local copies, waits for them, and re-layouts  6.04 us
  transfers between devices with their start and end apart: 26, of which 22 were waited for; matrix products, arithmetic and copies ran while one was open for 2% of the time, Pallas kernels for 7%

commit v1 on v0

--- a/solution.py
+++ b/solution.py
@@ -15,8 +15,11 @@
 FACE = 256
 LEVELS = 8
 GROUP = 4
-SLICES = 8
-PIECE = 2 * (BLK // SLICES)
+SLICES = 4
+HALF = BLK // SLICES
+PIECE = 2 * HALF
+
+LIMIT = 20 * 2**20
 
 bf16 = jnp.bfloat16
 f32 = jnp.float32
@@ -24,20 +27,23 @@
 SMEM = pltpu.SMEM
 
 
-def gather_rows(cur_ref, face_ref, rows_ref, low_ref, high_ref):
+def gather_rows(cur_ref, face_ref, place_ref, rows_ref, inner_ref, outer_ref):
+    core = place_ref[0]
+
     def body(t, _):
         base = t * 16
+        source = jnp.where(t < FACE // 16, base + (1 - core) * FACE, base - FACE + core * FACE)
         for k in range(16):
-            rows_ref[pl.ds(base + k, 1), :] = cur_ref[pl.ds(face_ref[base + k], 1), :]
+            rows_ref[pl.ds(base + k, 1), :] = cur_ref[pl.ds(face_ref[source + k], 1), :]
         return 0
 
     lax.fori_loop(0, 2 * FACE // 16, body, 0)
-    low_ref[...] = rows_ref[0:FACE, :].astype(bf16)
-    high_ref[...] = rows_ref[FACE : 2 * FACE, :].astype(bf16)
-
-
-def faces_kernel(face_ref, cur_ref, low_ref, high_ref, rows_ref):
-    gather_rows(cur_ref, face_ref, rows_ref, low_ref, high_ref)
+    inner_ref[...] = rows_ref[0:FACE, :].astype(bf16)
+    outer_ref[...] = rows_ref[FACE : 2 * FACE, :].astype(bf16)
+
+
+def faces_kernel(face_ref, place_ref, cur_ref, inner_ref, outer_ref, rows_ref):
+    gather_rows(cur_ref, face_ref, place_ref, rows_ref, inner_ref, outer_ref)
 
 
 def product_kernel(cols_ref, stiff_ref, cur_ref, applied_ref, out_ref, curb_ref):
@@ -56,7 +62,7 @@
 
 
 def partial_kernel(
-    cols_ref, face_ref, me_ref, inv_ref, base_ref, below_ref, above_ref, couple_ref,
+    cols_ref, face_ref, place_ref, inv_ref, base_ref, inner_ref, outer_ref, couple_ref,
     res_ref, keep_ref, send_ref, side_ref, acc_ref,
 ):
     g = pl.program_id(0)
@@ -64,10 +70,13 @@
     @pl.when(g == 0)
     def _():
         res_ref[...] = base_ref[...]
-        side_ref[0:FACE, :] = jnp.dot(couple_ref[0], below_ref[...], preferred_element_type=f32)
-        side_ref[FACE : 2 * FACE, :] = jnp.dot(
-            couple_ref[1], above_ref[...], preferred_element_type=f32
-        )
+        core = place_ref[0]
+        inner = inner_ref[...]
+        outer = jnp.where(place_ref[2] != 0, outer_ref[...], jnp.zeros_like(inner))
+        for face, got in ((1 - core, inner), (core, outer)):
+            side_ref[pl.ds(pl.multiple_of(face * FACE, FACE), FACE), :] = jnp.dot(
+                couple_ref[face], got, preferred_element_type=f32
+            )
 
         def body(t, _):
             first = t * 16
@@ -90,22 +99,16 @@
 
     @pl.when(g == NB // GROUP - 1)
     def _():
-        me = me_ref[0]
-        half = PIECE // 2
         for rel in range(SLICES):
-            start = pl.multiple_of((me ^ rel) * half, half)
+            start = pl.multiple_of((place_ref[1] ^ rel) * HALF, HALF)
             for c in range(NB):
                 level, h = divmod(c, 2)
-                value = acc_ref[c, pl.ds(start, half), :]
-                if rel < SLICES // 2:
-                    keep_ref[rel, level, h * half : (h + 1) * half, :] = value
-                else:
-                    send_ref[rel - SLICES // 2, level, h * half : (h + 1) * half, :] = value.astype(
-                        bf16
-                    )
-
-
-def update_kernel(gather, cols_ref, face_ref, me_ref, inv_ref, own_ref, got_ref, cur_ref, *rest):
+                value = acc_ref[c, pl.ds(start, HALF), :]
+                keep_ref[rel, level, h * HALF : (h + 1) * HALF, :] = value
+                send_ref[rel, level, h * HALF : (h + 1) * HALF, :] = value.astype(bf16)
+
+
+def update_kernel(gather, cols_ref, face_ref, place_ref, inv_ref, own_ref, got_ref, cur_ref, *rest):
     if gather:
         new_ref, low_ref, high_ref, coeff_ref, rows_ref = rest
     else:
@@ -114,16 +117,22 @@
 
     @pl.when(g == 0)
     def _():
-        me = me_ref[0]
-        half = PIECE // 2
-        for rel in range(SLICES):
-            start = pl.multiple_of((me ^ rel) * half, half)
-            src = own_ref if rel < SLICES // 2 else got_ref
-            for c in range(NB):
-                level, h = divmod(c, 2)
-                coeff_ref[c, pl.ds(start, half), :] = src[
-                    rel % (SLICES // 2), level, h * half : (h + 1) * half, :
-                ]
+        def spread(src):
+            for rel in range(SLICES):
+                start = pl.multiple_of((place_ref[1] ^ rel) * HALF, HALF)
+                for c in range(NB):
+                    level, h = divmod(c, 2)
+                    coeff_ref[c, pl.ds(start, HALF), :] = src[
+                        rel, level, h * HALF : (h + 1) * HALF, :
+                    ]
+
+        @pl.when(place_ref[0] == 0)
+        def _():
+            spread(got_ref)
+
+        @pl.when(place_ref[0] != 0)
+        def _():
+            spread(own_ref)
 
     for ii in range(GROUP):
         i = g * GROUP + ii
@@ -137,7 +146,7 @@
 
         @pl.when(g == NB // GROUP - 1)
         def _():
-            gather_rows(new_ref, face_ref, rows_ref, low_ref, high_ref)
+            gather_rows(new_ref, face_ref, place_ref, rows_ref, low_ref, high_ref)
 
 
 def sds(shape, dtype):
@@ -150,22 +159,23 @@
 
 ROWS = NB * BLK
 STEPS = NB // GROUP
-KEEP = (SLICES // 2, LEVELS, PIECE, BLK)
-
-
-def faces_of(cur, faces):
+KEEP = (SLICES, LEVELS, PIECE, BLK)
+
+
+def faces_of(cur, faces, place):
     return pl.pallas_call(
         faces_kernel,
         grid_spec=pltpu.PrefetchScalarGridSpec(
-            num_scalar_prefetch=1,
+            num_scalar_prefetch=2,
             grid=(1,),
             in_specs=[whole((ROWS, BLK))],
             out_specs=[whole((FACE, BLK))] * 2,
             scratch_shapes=[VMEM((2 * FACE, BLK), f32)],
         ),
         out_shape=[sds((FACE, BLK), bf16)] * 2,
+        compiler_params=pltpu.CompilerParams(vmem_limit_bytes=LIMIT),
         name="faces",
-    )(faces, cur)
+    )(faces, place, cur)
 
 
 def base_of(cur, applied, stiff, cols):
@@ -186,11 +196,12 @@
         cost_estimate=pl.CostEstimate(
             flops=2 * NB * KNZ * BLK**3, bytes_accessed=8_000_000, transcendentals=0
         ),
+        compiler_params=pltpu.CompilerParams(vmem_limit_bytes=LIMIT),
         name="product",
     )(cols, stiff, cur, applied)
 
 
-def partial_of(base, below, above, couple, inverse, cols, faces, me):
+def partial_of(base, inner, outer, couple, inverse, cols, faces, place):
     return pl.pallas_call(
         partial_kernel,
         grid_spec=pltpu.PrefetchScalarGridSpec(
@@ -210,11 +221,12 @@
         cost_estimate=pl.CostEstimate(
             flops=2 * NB * XNZ * BLK**3, bytes_accessed=8_000_000, transcendentals=0
         ),
+        compiler_params=pltpu.CompilerParams(vmem_limit_bytes=LIMIT),
         name="partial",
-    )(cols, faces, me, inverse, base, below, above, couple)
-
-
-def update_of(own, got, cur, inverse, cols, faces, me, gather):
+    )(cols, faces, place, inverse, base, inner, outer, couple)
+
+
+def update_of(own, got, cur, inverse, cols, faces, place, gather):
     scratch = [VMEM((NB, BLK, BLK), bf16)]
     outs, specs = [sds((ROWS, BLK), f32)], [whole((ROWS, BLK))]
     if gather:
@@ -239,18 +251,37 @@
         cost_estimate=pl.CostEstimate(
             flops=2 * NB * XNZ * BLK**3, bytes_accessed=8_000_000, transcendentals=0
         ),
+        compiler_params=pltpu.CompilerParams(vmem_limit_bytes=LIMIT),
         name="update",
-    )(cols, faces, me, inverse, own, got, cur)
-
-
-def swapped(value, axis, mask):
-    return lax.ppermute(value, axis, [(i, i ^ mask) for i in range(lax.axis_size(axis))])
-
-
-def shifted(value, steps):
+    )(cols, faces, place, inverse, own, got, cur)
+
+
+def moved(value, pairs):
+    return lax.ppermute(value, ("wide", "narrow"), pairs)
+
+
+def swapped(value, wide_mask, narrow_mask):
+    wide, narrow = lax.axis_size("wide"), lax.axis_size("narrow")
+    other = (8, 0) if narrow_mask else (0, 2)
+    pairs = []
+    for w in range(wide):
+        for n in range(narrow):
+            masks = (wide_mask, narrow_mask) if n % 2 else other
+            pairs.append((w * narrow + n, (w ^ masks[0]) * narrow + (n ^ masks[1])))
+    return moved(value, pairs)
+
+
+def handed(value):
+    count = lax.axis_size("wide") * lax.axis_size("narrow")
+    return moved(value, [(i, i ^ 1) for i in range(count)])
+
+
+def faces_swapped(inner, outer):
     count = lax.axis_size("narrow")
-    pairs = [(i, i + steps) for i in range(count) if 0 <= i + steps < count]
-    return lax.ppermute(value, "narrow", pairs)
+    return (
+        lax.ppermute(inner, "narrow", [(i, i ^ 1) for i in range(count)]),
+        lax.ppermute(outer, "narrow", [(i, (i + 1 if i % 2 else i - 1) % count) for i in range(count)]),
+    )
 
 
 def rounded(total, level):
@@ -259,22 +290,29 @@
 
 def summed(keep, send):
     done = {}
-    total = keep + swapped(send, "narrow", 1).astype(f32)
-    done[1] = rounded(total[:, :1], 1)
+    got = handed(send)
+    low, high = ((keep[part], got[part].astype(f32)) for part in (slice(0, 2), slice(2, 4)))
+    sent = (high[0][:, 1:] + high[1][:, 1:]).astype(bf16)
+    total = low[0] + low[1]
+    done[1] = jnp.concatenate(
+        [rounded(total[:, :1], 1), rounded(high[0][:, :1] + high[1][:, :1], 1)], axis=0
+    )
     for level, mask in ((2, 2), (3, 6)):
-        size = total.shape[0] // 2
-        got = swapped(total[size:, 1:].astype(bf16), "narrow", mask)
-        total = total[:size, 1:] + got.astype(f32)
+        got = swapped(sent, 0, mask).astype(f32)
+        total = total[:, 1:] + got
         done[level] = rounded(total[:, :1], level)
+        if level == 2:
+            sent = total[1:, 1:].astype(bf16)
+            total = total[:1]
     for level, mask in ((4, 1), (5, 2), (6, 6), (7, 8), (8, 24)):
         total = total[:, 1:]
-        total = total + swapped(total.astype(bf16), "wide", mask).astype(f32)
+        total = total + swapped(total.astype(bf16), mask, 0).astype(f32)
         done[level] = rounded(total[:, :1], level)
     mine = jnp.concatenate([done[level] for level in range(3, LEVELS + 1)], axis=1)
     for level, mask in ((2, 6), (1, 2)):
-        mine = jnp.concatenate([mine, swapped(mine, "narrow", mask)], axis=0)
+        mine = jnp.concatenate([mine, swapped(mine, 0, mask)], axis=0)
         mine = jnp.concatenate([done[level], mine], axis=1)
-    return mine, swapped(mine, "narrow", 1)
+    return mine, handed(mine)
 
 
 def per_device(
@@ -289,23 +327,23 @@
     couple = coupling[0, 0]
     inverse = inverse_blocks[0, 0]
     inverse_cols = inverse_columns[0, 0].reshape(-1)
-    place = lax.axis_index("narrow").astype(jnp.int32)
-    core, bit0, bit1 = place & 1, (place >> 1) & 1, (place >> 2) & 1
-    me = (core * 4 + (bit0 ^ bit1) * 2 + bit1).reshape(1)
-    low, high = faces_of(current, faces)
+    number = lax.axis_index("narrow").astype(jnp.int32)
+    core, bit0, bit1 = number & 1, (number >> 1) & 1, (number >> 2) & 1
+    inside = ((number > 0) & (number < lax.axis_size("narrow") - 1)).astype(jnp.int32)
+    place = jnp.stack([core, (bit0 ^ bit1) * 2 + bit1, inside])
+    inner, outer = faces_of(current, faces, place)
     for sweep in range(ITERS):
-        below = shifted(high, 1)
-        above = shifted(low, -1)
+        inner, outer = faces_swapped(inner, outer)
         base = base_of(current, applied, stiff, stiff_cols)
         residual, keep, send = partial_of(
-            base, below, above, couple, inverse, inverse_cols, faces, me
+            base, inner, outer, couple, inverse, inverse_cols, faces, place
         )
         own, got = summed(keep, send)
         last = sweep == ITERS - 1
-        outs = update_of(own, got, current, inverse, inverse_cols, faces, me, not last)
+        outs = update_of(own, got, current, inverse, inverse_cols, faces, place, not last)
         current = outs[0]
         if not last:
-            low, high = outs[1:]
+            inner, outer = outs[1:]
     return (current[None, None], residual[None, None])
 
 

time: 165 us -> 133 us (0.81)
  starting transfers between devices: 68.8 us -> 44.3 us
  Pallas kernels: 43 us -> 22.2 us
  waiting for transfers between devices: 41.3 us -> 55.2 us
    ppermute x26, starting transfers between devices: 68.8 us -> 44.3 us  [the longest x22 39.7 us: moved(): return lax.ppermute(value, ('wide', 'narrow'), pairs)]
    ppermute x26, waiting for transfers between devices: 41.3 us -> 55.2 us  [the longest x22 54.7 us: moved(): return lax.ppermute(value, ('wide', 'narrow'), pairs)]
    pallas_call x2, Pallas kernels: 11.7 us -> 4.57 us  [base_of(): pl.pallas_call(product_kernel, grid_spec=pltpu.PrefetchScalarGridSpec(num...]
    pallas_call x2, Pallas kernels: 12.8 us -> 6.55 us  [update_of(): pl.pallas_call(functools.partial(update_kernel, gather), grid_spec=pltpu....]
    pallas_call x2, Pallas kernels: 15.3 us -> 9.86 us  [partial_of(): pl.pallas_call(partial_kernel, grid_spec=pltpu.PrefetchScalarGridSpec(num...]
    unnamed x19, local copies, waits for them, and re-layouts: 6.04 us -> 8.25 us
    add x14, other arithmetic: 2.36 us -> 0.36 us  [the longest x4 0.15 us: summed(): total = total[:, 1:] + got]
    pallas_call x1, Pallas kernels: 3.11 us -> 1.19 us  [faces_of(): pl.pallas_call(faces_kernel, grid_spec=pltpu.PrefetchScalarGridSpec(num_s...]
  transfers between devices with their start and end apart: 26 -> 26, of which waited for: 22 -> 23; matrix products, arithmetic and copies ran while one was open for 2% -> 1% of each run, Pallas kernels for 7% -> 3%
where the time goes in v1:
time: 133 us; the launch traced here: 132 us
  waiting for transfers between devices  55.2 us (42%)
  starting transfers between devices  44.3 us (33%)
  Pallas kernels  22.2 us (17%)
  local copies, waits for them, and re-layouts  8.54 us (6%)
    ppermute x22, waiting for transfers between devices, moved(): return lax.ppermute(value, ('wide', 'narrow'), pairs)  54.7 us
    ppermute x22, starting transfers between devices, moved(): return lax.ppermute(value, ('wide', 'narrow'), pairs)  39.7 us
    pallas_call x2, Pallas kernels, partial_of(): pl.pallas_call(partial_kernel, grid_spec=pltpu.PrefetchScalarGridSpec(num...  9.86 us
    unnamed x19, local copies, waits for them, and re-layouts  8.25 us
    pallas_call x2, Pallas kernels, update_of(): pl.pallas_call(functools.partial(update_kernel, gather), grid_spec=pltpu....  6.55 us
    pallas_call x2, Pallas kernels, base_of(): pl.pallas_call(product_kernel, grid_spec=pltpu.PrefetchScalarGridSpec(num...  4.57 us
    ppermute x2, starting transfers between devices, faces_swapped(): lax.ppermute(inner, 'narrow', [(i, i ^ 1) for i in range(count)])  3.74 us
  transfers between devices with their start and end apart: 26, of which 23 were waited for; matrix products, arithmetic and copies ran while one was open for 1% of the time, Pallas kernels for 3%

profile of v1, /device:TPU:1, one launch (start us, length us, event | category | flops | bytes accessed | tf_op | source)
XLA Modules:
  0.0 132.3 jit_solution(183193901134164874)
XLA Ops:
  3.8 3.3 %collective-permute-start = (bf16[256,128]{1,0:T(8,128)(2,1)S(1)}, bf16[256,128]{1,0:T(8,128)(2,1)S(1)}, u32[]{:S(2)}, u32[]{:S(2)}) collective-permute-start(bf16[256,128]{1,0:T(8,128)(2,1)S(1)} %get-tuple-element.12), channel_id=1, source_target_pairs={{0,1},{1,0},{2,3},{3,2},{4,5},{5,4},{6,7},{7,6},{8,9},{9,8},{10,11... | collective-permute-start | bytes 196616 | tf_op jit(solution)/shard_map/ppermute | solution.py:282
  8.8 2.2 %copy-done.1 = bf16[1,1,16,7,128,128]{5,4,3,2,1,0:T(8,128)(2,1)S(1)} copy-done((bf16[1,1,16,7,128,128]{5,4,3,2,1,0:T(8,128)(2,1)S(1)}, bf16[1,1,16,7,128,128]{5,4,3,2,1,0:T(8,128)(2,1)}, u32[]{:S(2)}) %copy-start.1) | copy-done | bytes 3670040
  13.6 2.3 %product.2.base_ref = f32[2048,128]{1,0:T(8,128)S(1)} custom-call(s32[112]{0:T(128)S(1)} %reshape_squeeze.11.cols_ref, bf16[16,7,128,128]{3,2,1,0:T(8,128)(2,1)S(1)} %bitcast.20, f32[2048,128]{1,0:T(8,128)S(1)} %bitcast.23, f32[2048,128]{1,0:T(8,128)S(1)} %bitcast.25), custom_call_target="tpu_custom_call" | custom-call | flops 469762048 | bytes 8000000 | tf_op jit(solution)/shard_map/product/pallas_call | solution.py:182
  16.0 4.9 %partial.2 = (f32[2048,128]{1,0:T(8,128)}, f32[4,8,64,128]{3,2,1,0:T(8,128)S(1)}, bf16[4,8,64,128]{3,2,1,0:T(8,128)(2,1)S(1)}) custom-call(s32[128]{0:T(128)S(1)} %reshape_squeeze.9.cols_ref, s32[512]{0:T(512)S(1)} %bitcast.30, s32[3]{0:T(128)S(1)} %pad_add_fusion.place_ref, bf16[16,8,128,128]{3,2,1,0:T(8,128)(2,1)S(1)} %bitcast.16, ...), custom_call_target="tpu_custom_call" | custom-call | flops 536870912 | bytes 8000000 | tf_op jit(solution)/shard_map/partial/pallas_call | solution.py:205
  22.1 1.5 %collective-permute-done.2 = bf16[4,8,64,128]{3,2,1,0:T(8,128)(2,1)S(1)} collective-permute-done((bf16[4,8,64,128]{3,2,1,0:T(8,128)(2,1)S(1)}, bf16[4,8,64,128]{3,2,1,0:T(8,128)(2,1)S(1)}, u32[]{:S(2)}, u32[]{:S(2)}) %collective-permute-start.2) | collective-permute-done | bytes 524320 | tf_op jit(solution)/shard_map/ppermute | solution.py:260
  24.6 4.4 %collective-permute-done.3 = bf16[2,7,64,128]{3,2,1,0:T(8,128)(2,1)S(1)} collective-permute-done((bf16[2,7,64,128]{3,2,1,0:T(8,128)(2,1)S(1)}, bf16[2,7,64,128]{3,2,1,0:T(8,128)(2,1)S(1)}, u32[]{:S(2)}, u32[]{:S(2)}) %collective-permute-start.3) | collective-permute-done | bytes 229408 | tf_op jit(solution)/shard_map/ppermute | solution.py:260
  29.1 2.0 %collective-permute-start.4 = (bf16[1,6,64,128]{3,2,1,0:T(8,128)(2,1)S(1)}, bf16[1,6,64,128]{3,2,1,0:T(8,128)(2,1)S(1)}, u32[]{:S(2)}, u32[]{:S(2)}) collective-permute-start(bf16[1,6,64,128]{3,2,1,0:T(8,128)(2,1)S(1)} %slice.345), channel_id=1, source_target_pairs={{0,64},{1,7},{2,66},{3,5},{4,68},{5,3},{6,70},{7,1},{8,72},{9,15},... | collective-permute-start | bytes 294920 | tf_op jit(solution)/shard_map/ppermute | solution.py:260
  31.0 2.8 %collective-permute-done.4 = bf16[1,6,64,128]{3,2,1,0:T(8,128)(2,1)S(1)} collective-permute-done((bf16[1,6,64,128]{3,2,1,0:T(8,128)(2,1)S(1)}, bf16[1,6,64,128]{3,2,1,0:T(8,128)(2,1)S(1)}, u32[]{:S(2)}, u32[]{:S(2)}) %collective-permute-start.4) | collective-permute-done | bytes 98336 | tf_op jit(solution)/shard_map/ppermute | solution.py:260
  33.9 1.7 %collective-permute-start.5 = (bf16[1,5,64,128]{3,2,1,0:T(8,128)(2,1)S(1)}, bf16[1,5,64,128]{3,2,1,0:T(8,128)(2,1)S(1)}, u32[]{:S(2)}, u32[]{:S(2)}) collective-permute-start(bf16[1,5,64,128]{3,2,1,0:T(8,128)(2,1)S(1)} %slice.347), channel_id=1, source_target_pairs={{0,2},{1,9},{2,0},{3,11},{4,6},{5,13},{6,4},{7,15},{8,10},{9,1},{1... | collective-permute-start | bytes 245768 | tf_op jit(solution)/shard_map/ppermute | solution.py:260
  35.6 1.8 %collective-permute-done.5 = bf16[1,5,64,128]{3,2,1,0:T(8,128)(2,1)S(1)} collective-permute-done((bf16[1,5,64,128]{3,2,1,0:T(8,128)(2,1)S(1)}, bf16[1,5,64,128]{3,2,1,0:T(8,128)(2,1)S(1)}, u32[]{:S(2)}, u32[]{:S(2)}) %collective-permute-start.5) | collective-permute-done | bytes 81952 | tf_op jit(solution)/shard_map/ppermute | solution.py:260
  37.5 3.1 %collective-permute-start.6 = (bf16[1,4,64,128]{3,2,1,0:T(8,128)(2,1)S(1)}, bf16[1,4,64,128]{3,2,1,0:T(8,128)(2,1)S(1)}, u32[]{:S(2)}, u32[]{:S(2)}) collective-permute-start(bf16[1,4,64,128]{3,2,1,0:T(8,128)(2,1)S(1)} %slice.349), channel_id=1, source_target_pairs={{0,2},{1,17},{2,0},{3,19},{4,6},{5,21},{6,4},{7,23},{8,10},{9,25},... | collective-permute-start | bytes 196616 | tf_op jit(solution)/shard_map/ppermute | solution.py:260
  40.5 1.6 %collective-permute-done.6 = bf16[1,4,64,128]{3,2,1,0:T(8,128)(2,1)S(1)} collective-permute-done((bf16[1,4,64,128]{3,2,1,0:T(8,128)(2,1)S(1)}, bf16[1,4,64,128]{3,2,1,0:T(8,128)(2,1)S(1)}, u32[]{:S(2)}, u32[]{:S(2)}) %collective-permute-start.6) | collective-permute-done | bytes 65568 | tf_op jit(solution)/shard_map/ppermute | solution.py:260
  42.2 5.4 %collective-permute-start.7 = (bf16[1,3,64,128]{3,2,1,0:T(8,128)(2,1)S(1)}, bf16[1,3,64,128]{3,2,1,0:T(8,128)(2,1)S(1)}, u32[]{:S(2)}, u32[]{:S(2)}) collective-permute-start(bf16[1,3,64,128]{3,2,1,0:T(8,128)(2,1)S(1)} %slice.351), channel_id=1, source_target_pairs={{0,2},{1,49},{2,0},{3,51},{4,6},{5,53},{6,4},{7,55},{8,10},{9,57},... | collective-permute-start | bytes 147464 | tf_op jit(solution)/shard_map/ppermute | solution.py:260
  52.1 2.8 %collective-permute-start.9 = (bf16[1,1,64,128]{3,2,1,0:T(8,128)(2,1)S(1)}, bf16[1,1,64,128]{3,2,1,0:T(8,128)(2,1)S(1)}, u32[]{:S(2)}, u32[]{:S(2)}) collective-permute-start(bf16[1,1,64,128]{3,2,1,0:T(8,128)(2,1)S(1)} %get-tuple-element.24), channel_id=1, source_target_pairs={{0,2},{1,193},{2,0},{3,195},{4,6},{5,197},{6,4},{7,199},{8,10},{9,... | collective-permute-start | bytes 49160 | tf_op jit(solution)/shard_map/ppermute | solution.py:260
  56.7 4.1 %collective-permute-done.10 = bf16[1,6,64,128]{3,2,1,0:T(8,128)(2,1)S(1)} collective-permute-done((bf16[1,6,64,128]{3,2,1,0:T(8,128)(2,1)S(1)}, bf16[1,6,64,128]{3,2,1,0:T(8,128)(2,1)S(1)}, u32[]{:S(2)}, u32[]{:S(2)}) %collective-permute-start.10) | collective-permute-done | bytes 98336 | tf_op jit(solution)/shard_map/ppermute | solution.py:260
  61.0 5.1 %collective-permute-done.11 = bf16[2,7,64,128]{3,2,1,0:T(8,128)(2,1)S(1)} collective-permute-done((bf16[2,7,64,128]{3,2,1,0:T(8,128)(2,1)S(1)}, bf16[2,7,64,128]{3,2,1,0:T(8,128)(2,1)S(1)}, u32[]{:S(2)}, u32[]{:S(2)}) %collective-permute-start.11) | collective-permute-done | bytes 229408 | tf_op jit(solution)/shard_map/ppermute | solution.py:260
  67.1 1.5 %collective-permute-done.12.got_ref = bf16[4,8,64,128]{3,2,1,0:T(8,128)(2,1)S(1)} collective-permute-done((bf16[4,8,64,128]{3,2,1,0:T(8,128)(2,1)S(1)}, bf16[4,8,64,128]{3,2,1,0:T(8,128)(2,1)S(1)}, u32[]{:S(2)}, u32[]{:S(2)}) %collective-permute-start.12) | collective-permute-done | bytes 524320 | tf_op jit(solution)/shard_map/ppermute | solution.py:260
  68.6 3.1 %update.2 = (f32[2048,128]{1,0:T(8,128)S(1)}, bf16[256,128]{1,0:T(8,128)(2,1)S(1)}, bf16[256,128]{1,0:T(8,128)(2,1)S(1)}) custom-call(s32[128]{0:T(128)S(1)} %reshape_squeeze.9.cols_ref, s32[512]{0:T(512)S(1)} %bitcast.31, s32[3]{0:T(128)S(1)} %pad_add_fusion.place_ref, bf16[16,8,128,128]{3,2,1,0:T(8,128)(2,1)S(1)} %bitcast.17, ...), custom_call_target="tpu_custom_call" | custom-call | flops 536870912 | bytes 8000000 | tf_op jit(solution)/shard_map/update/pallas_call | solution.py:236
  73.1 2.3 %product.3.base_ref = f32[2048,128]{1,0:T(8,128)S(1)} custom-call(s32[112]{0:T(128)S(1)} %reshape_squeeze.11.cols_ref, bf16[16,7,128,128]{3,2,1,0:T(8,128)(2,1)S(1)} %bitcast.21, f32[2048,128]{1,0:T(8,128)S(1)} %get-tuple-element.16.cur_ref, f32[2048,128]{1,0:T(8,128)S(1)} %bitcast.26), custom_call_target="tpu_custom_call" | custom-call | flops 469762048 | bytes 8000000 | tf_op jit(solution)/shard_map/product/pallas_call | solution.py:182
  75.9 4.9 %partial.3 = (f32[2048,128]{1,0:T(8,128)}, f32[4,8,64,128]{3,2,1,0:T(8,128)S(1)}, bf16[4,8,64,128]{3,2,1,0:T(8,128)(2,1)S(1)}) custom-call(s32[128]{0:T(128)S(1)} %reshape_squeeze.9.cols_ref, s32[512]{0:T(512)S(1)} %bitcast.32, s32[3]{0:T(128)S(1)} %pad_add_fusion.place_ref, bf16[16,8,128,128]{3,2,1,0:T(8,128)(2,1)S(1)} %bitcast.18, ...), custom_call_target="tpu_custom_call" | custom-call | flops 536870912 | bytes 8000000 | tf_op jit(solution)/shard_map/partial/pallas_call | solution.py:205
  84.1 5.1 %collective-permute-done.16 = bf16[2,7,64,128]{3,2,1,0:T(8,128)(2,1)S(1)} collective-permute-done((bf16[2,7,64,128]{3,2,1,0:T(8,128)(2,1)S(1)}, bf16[2,7,64,128]{3,2,1,0:T(8,128)(2,1)S(1)}, u32[]{:S(2)}, u32[]{:S(2)}) %collective-permute-start.16) | collective-permute-done | bytes 229408 | tf_op jit(solution)/shard_map/ppermute | solution.py:260
  89.3 1.8 %collective-permute-start.17 = (bf16[1,6,64,128]{3,2,1,0:T(8,128)(2,1)S(1)}, bf16[1,6,64,128]{3,2,1,0:T(8,128)(2,1)S(1)}, u32[]{:S(2)}, u32[]{:S(2)}) collective-permute-start(bf16[1,6,64,128]{3,2,1,0:T(8,128)(2,1)S(1)} %slice.344), channel_id=1, source_target_pairs={{0,64},{1,7},{2,66},{3,5},{4,68},{5,3},{6,70},{7,1},{8,72},{9,15},... | collective-permute-start | bytes 294920 | tf_op jit(solution)/shard_map/ppermute | solution.py:260
  91.1 2.9 %collective-permute-done.17 = bf16[1,6,64,128]{3,2,1,0:T(8,128)(2,1)S(1)} collective-permute-done((bf16[1,6,64,128]{3,2,1,0:T(8,128)(2,1)S(1)}, bf16[1,6,64,128]{3,2,1,0:T(8,128)(2,1)S(1)}, u32[]{:S(2)}, u32[]{:S(2)}) %collective-permute-start.17) | collective-permute-done | bytes 98336 | tf_op jit(solution)/shard_map/ppermute | solution.py:260
  94.1 1.7 %collective-permute-start.18 = (bf16[1,5,64,128]{3,2,1,0:T(8,128)(2,1)S(1)}, bf16[1,5,64,128]{3,2,1,0:T(8,128)(2,1)S(1)}, u32[]{:S(2)}, u32[]{:S(2)}) collective-permute-start(bf16[1,5,64,128]{3,2,1,0:T(8,128)(2,1)S(1)} %slice.346), channel_id=1, source_target_pairs={{0,2},{1,9},{2,0},{3,11},{4,6},{5,13},{6,4},{7,15},{8,10},{9,1},{1... | collective-permute-start | bytes 245768 | tf_op jit(solution)/shard_map/ppermute | solution.py:260
  95.8 1.8 %collective-permute-done.18 = bf16[1,5,64,128]{3,2,1,0:T(8,128)(2,1)S(1)} collective-permute-done((bf16[1,5,64,128]{3,2,1,0:T(8,128)(2,1)S(1)}, bf16[1,5,64,128]{3,2,1,0:T(8,128)(2,1)S(1)}, u32[]{:S(2)}, u32[]{:S(2)}) %collective-permute-start.18) | collective-permute-done | bytes 81952 | tf_op jit(solution)/shard_map/ppermute | solution.py:260
  97.7 3.1 %collective-permute-start.19 = (bf16[1,4,64,128]{3,2,1,0:T(8,128)(2,1)S(1)}, bf16[1,4,64,128]{3,2,1,0:T(8,128)(2,1)S(1)}, u32[]{:S(2)}, u32[]{:S(2)}) collective-permute-start(bf16[1,4,64,128]{3,2,1,0:T(8,128)(2,1)S(1)} %slice.348), channel_id=1, source_target_pairs={{0,2},{1,17},{2,0},{3,19},{4,6},{5,21},{6,4},{7,23},{8,10},{9,25},... | collective-permute-start | bytes 196616 | tf_op jit(solution)/shard_map/ppermute | solution.py:260
  100.8 1.6 %collective-permute-done.19 = bf16[1,4,64,128]{3,2,1,0:T(8,128)(2,1)S(1)} collective-permute-done((bf16[1,4,64,128]{3,2,1,0:T(8,128)(2,1)S(1)}, bf16[1,4,64,128]{3,2,1,0:T(8,128)(2,1)S(1)}, u32[]{:S(2)}, u32[]{:S(2)}) %collective-permute-start.19) | collective-permute-done | bytes 65568 | tf_op jit(solution)/shard_map/ppermute | solution.py:260
  102.5 5.4 %collective-permute-start.20 = (bf16[1,3,64,128]{3,2,1,0:T(8,128)(2,1)S(1)}, bf16[1,3,64,128]{3,2,1,0:T(8,128)(2,1)S(1)}, u32[]{:S(2)}, u32[]{:S(2)}) collective-permute-start(bf16[1,3,64,128]{3,2,1,0:T(8,128)(2,1)S(1)} %slice.350), channel_id=1, source_target_pairs={{0,2},{1,49},{2,0},{3,51},{4,6},{5,53},{6,4},{7,55},{8,10},{9,57},... | collective-permute-start | bytes 147464 | tf_op jit(solution)/shard_map/ppermute | solution.py:260
  112.3 2.8 %collective-permute-start.22 = (bf16[1,1,64,128]{3,2,1,0:T(8,128)(2,1)S(1)}, bf16[1,1,64,128]{3,2,1,0:T(8,128)(2,1)S(1)}, u32[]{:S(2)}, u32[]{:S(2)}) collective-permute-start(bf16[1,1,64,128]{3,2,1,0:T(8,128)(2,1)S(1)} %get-tuple-element.22), channel_id=1, source_target_pairs={{0,2},{1,193},{2,0},{3,195},{4,6},{5,197},{6,4},{7,199},{8,10},{9,... | collective-permute-start | bytes 49160 | tf_op jit(solution)/shard_map/ppermute | solution.py:260
  117.2 3.8 %collective-permute-done.23 = bf16[1,6,64,128]{3,2,1,0:T(8,128)(2,1)S(1)} collective-permute-done((bf16[1,6,64,128]{3,2,1,0:T(8,128)(2,1)S(1)}, bf16[1,6,64,128]{3,2,1,0:T(8,128)(2,1)S(1)}, u32[]{:S(2)}, u32[]{:S(2)}) %collective-permute-start.23) | collective-permute-done | bytes 98336 | tf_op jit(solution)/shard_map/ppermute | solution.py:260
  121.2 5.1 %collective-permute-done.24 = bf16[2,7,64,128]{3,2,1,0:T(8,128)(2,1)S(1)} collective-permute-done((bf16[2,7,64,128]{3,2,1,0:T(8,128)(2,1)S(1)}, bf16[2,7,64,128]{3,2,1,0:T(8,128)(2,1)S(1)}, u32[]{:S(2)}, u32[]{:S(2)}) %collective-permute-start.24) | collective-permute-done | bytes 229408 | tf_op jit(solution)/shard_map/ppermute | solution.py:260
  128.8 3.4 %update.3 = f32[2048,128]{1,0:T(8,128)} custom-call(s32[128]{0:T(128)S(1)} %reshape_squeeze.9.cols_ref, s32[512]{0:T(512)S(1)} %bitcast.33, s32[3]{0:T(128)S(1)} %pad_add_fusion.place_ref, bf16[16,8,128,128]{3,2,1,0:T(8,128)(2,1)S(1)} %bitcast.19, bf16[4,8,64,128]{3,2,1,0:T(8,128)(2,1)S(1)} %maximum_maximum_fusion.1.own_ref, ...), custom_call_target="tpu_custom_call" | custom-call | flops 536870912 | bytes 8000000 | tf_op jit(solution)/shard_map/update/pallas_call | solution.py:236
  (98 shorter events, 31.6 us)
Async XLA Ops:
  2.6 13.3 %copy-start.7 = (bf16[1,1,2,256,256]{4,3,2,1,0:T(8,128)(2,1)S(1)}, bf16[1,1,2,256,256]{4,3,2,1,0:T(8,128)(2,1)}, u32[]{:S(2)}) copy-start(bf16[1,1,2,256,256]{4,3,2,1,0:T(8,128)(2,1)} %param.13) | copy-start | bytes 786436
  3.8 12.1 %collective-permute-start = (bf16[256,128]{1,0:T(8,128)(2,1)S(1)}, bf16[256,128]{1,0:T(8,128)(2,1)S(1)}, u32[]{:S(2)}, u32[]{:S(2)}) collective-permute-start(bf16[256,128]{1,0:T(8,128)(2,1)S(1)} %get-tuple-element.12), channel_id=1, source_target_pairs={{0,1},{1,0},{2,3},{3,2},{4,5},{5,4},{6,7},{7,6},{8,9},{9,8},{10,11... | collective-permute-start | bytes 196616 | tf_op jit(solution)/shard_map/ppermute | solution.py:282
  7.1 8.8 %collective-permute-start.1 = (bf16[256,128]{1,0:T(8,128)(2,1)S(1)}, bf16[256,128]{1,0:T(8,128)(2,1)S(1)}, u32[]{:S(2)}, u32[]{:S(2)}) collective-permute-start(bf16[256,128]{1,0:T(8,128)(2,1)S(1)} %get-tuple-element.13), channel_id=1, source_target_pairs={{0,7},{1,2},{2,1},{3,4},{4,3},{5,6},{6,5},{7,0},{8,15},{9,10},{10,... | collective-permute-start | bytes 196616 | tf_op jit(solution)/shard_map/ppermute | solution.py:283
  8.8 7.1 %copy-start = (bf16[1,1,16,8,128,128]{5,4,3,2,1,0:T(8,128)(2,1)S(1)}, bf16[1,1,16,8,128,128]{5,4,3,2,1,0:T(8,128)(2,1)}, u32[]{:S(2)}) copy-start(bf16[1,1,16,8,128,128]{5,4,3,2,1,0:T(8,128)(2,1)} %param.14) | copy-start | bytes 12582916
  8.8 2.2 %copy-start.1 = (bf16[1,1,16,7,128,128]{5,4,3,2,1,0:T(8,128)(2,1)S(1)}, bf16[1,1,16,7,128,128]{5,4,3,2,1,0:T(8,128)(2,1)}, u32[]{:S(2)}) copy-start(bf16[1,1,16,7,128,128]{5,4,3,2,1,0:T(8,128)(2,1)} %param.10) | copy-start | bytes 11010052
  11.0 1.4 %copy-start.4 = (f32[1,1,2048,128]{3,2,1,0:T(8,128)S(1)}, f32[1,1,2048,128]{3,2,1,0:T(8,128)}, u32[]{:S(2)}) copy-start(f32[1,1,2048,128]{3,2,1,0:T(8,128)} %param.8) | copy-start | bytes 3145732
  20.9 2.7 %collective-permute-start.2 = (bf16[4,8,64,128]{3,2,1,0:T(8,128)(2,1)S(1)}, bf16[4,8,64,128]{3,2,1,0:T(8,128)(2,1)S(1)}, u32[]{:S(2)}, u32[]{:S(2)}) collective-permute-start(bf16[4,8,64,128]{3,2,1,0:T(8,128)(2,1)S(1)} %get-tuple-element.15), channel_id=1, source_target_pairs={{0,1},{1,0},{2,3},{3,2},{4,5},{5,4},{6,7},{7,6},{8,9},{9,8},{10,11... | collective-permute-start | bytes 1572872 | tf_op jit(solution)/shard_map/ppermute | solution.py:260
  23.7 5.3 %collective-permute-start.3 = (bf16[2,7,64,128]{3,2,1,0:T(8,128)(2,1)S(1)}, bf16[2,7,64,128]{3,2,1,0:T(8,128)(2,1)S(1)}, u32[]{:S(2)}, u32[]{:S(2)}) collective-permute-start(bf16[2,7,64,128]{3,2,1,0:T(8,128)(2,1)S(1)} %fusion.1), channel_id=1, source_target_pairs={{0,64},{1,3},{2,66},{3,1},{4,68},{5,7},{6,70},{7,5},{8,72},{9,11},... | collective-permute-start | bytes 688136 | tf_op jit(solution)/shard_map/ppermute | solution.py:260
  29.1 4.8 %collective-permute-start.4 = (bf16[1,6,64,128]{3,2,1,0:T(8,128)(2,1)S(1)}, bf16[1,6,64,128]{3,2,1,0:T(8,128)(2,1)S(1)}, u32[]{:S(2)}, u32[]{:S(2)}) collective-permute-start(bf16[1,6,64,128]{3,2,1,0:T(8,128)(2,1)S(1)} %slice.345), channel_id=1, source_target_pairs={{0,64},{1,7},{2,66},{3,5},{4,68},{5,3},{6,70},{7,1},{8,72},{9,15},... | collective-permute-start | bytes 294920 | tf_op jit(solution)/shard_map/ppermute | solution.py:260
  33.9 3.6 %collective-permute-start.5 = (bf16[1,5,64,128]{3,2,1,0:T(8,128)(2,1)S(1)}, bf16[1,5,64,128]{3,2,1,0:T(8,128)(2,1)S(1)}, u32[]{:S(2)}, u32[]{:S(2)}) collective-permute-start(bf16[1,5,64,128]{3,2,1,0:T(8,128)(2,1)S(1)} %slice.347), channel_id=1, source_target_pairs={{0,2},{1,9},{2,0},{3,11},{4,6},{5,13},{6,4},{7,15},{8,10},{9,1},{1... | collective-permute-start | bytes 245768 | tf_op jit(solution)/shard_map/ppermute | solution.py:260
  37.5 4.7 %collective-permute-start.6 = (bf16[1,4,64,128]{3,2,1,0:T(8,128)(2,1)S(1)}, bf16[1,4,64,128]{3,2,1,0:T(8,128)(2,1)S(1)}, u32[]{:S(2)}, u32[]{:S(2)}) collective-permute-start(bf16[1,4,64,128]{3,2,1,0:T(8,128)(2,1)S(1)} %slice.349), channel_id=1, source_target_pairs={{0,2},{1,17},{2,0},{3,19},{4,6},{5,21},{6,4},{7,23},{8,10},{9,25},... | collective-permute-start | bytes 196616 | tf_op jit(solution)/shard_map/ppermute | solution.py:260
  42.2 6.9 %collective-permute-start.7 = (bf16[1,3,64,128]{3,2,1,0:T(8,128)(2,1)S(1)}, bf16[1,3,64,128]{3,2,1,0:T(8,128)(2,1)S(1)}, u32[]{:S(2)}, u32[]{:S(2)}) collective-permute-start(bf16[1,3,64,128]{3,2,1,0:T(8,128)(2,1)S(1)} %slice.351), channel_id=1, source_target_pairs={{0,2},{1,49},{2,0},{3,51},{4,6},{5,53},{6,4},{7,55},{8,10},{9,57},... | collective-permute-start | bytes 147464 | tf_op jit(solution)/shard_map/ppermute | solution.py:260
  49.2 2.9 %collective-permute-start.8 = (bf16[1,2,64,128]{3,2,1,0:T(8,128)(2,1)S(1)}, bf16[1,2,64,128]{3,2,1,0:T(8,128)(2,1)S(1)}, u32[]{:S(2)}, u32[]{:S(2)}) collective-permute-start(bf16[1,2,64,128]{3,2,1,0:T(8,128)(2,1)S(1)} %slice.353), channel_id=1, source_target_pairs={{0,2},{1,65},{2,0},{3,67},{4,6},{5,69},{6,4},{7,71},{8,10},{9,73},... | collective-permute-start | bytes 98312 | tf_op jit(solution)/shard_map/ppermute | solution.py:260
  52.0 21.0 %copy-start.2 = (bf16[1,1,16,7,128,128]{5,4,3,2,1,0:T(8,128)(2,1)S(1)}, bf16[1,1,16,7,128,128]{5,4,3,2,1,0:T(8,128)(2,1)}, u32[]{:S(2)}) copy-start(bf16[1,1,16,7,128,128]{5,4,3,2,1,0:T(8,128)(2,1)} %param.10) | copy-start | bytes 11010052
  52.1 21.0 %copy-start.6 = (f32[1,1,2048,128]{3,2,1,0:T(8,128)S(1)}, f32[1,1,2048,128]{3,2,1,0:T(8,128)}, u32[]{:S(2)}) copy-start(f32[1,1,2048,128]{3,2,1,0:T(8,128)} %param.9) | copy-start | bytes 3145732
  52.1 4.0 %collective-permute-start.9 = (bf16[1,1,64,128]{3,2,1,0:T(8,128)(2,1)S(1)}, bf16[1,1,64,128]{3,2,1,0:T(8,128)(2,1)S(1)}, u32[]{:S(2)}, u32[]{:S(2)}) collective-permute-start(bf16[1,1,64,128]{3,2,1,0:T(8,128)(2,1)S(1)} %get-tuple-element.24), channel_id=1, source_target_pairs={{0,2},{1,193},{2,0},{3,195},{4,6},{5,197},{6,4},{7,199},{8,10},{9,... | collective-permute-start | bytes 49160 | tf_op jit(solution)/shard_map/ppermute | solution.py:260
  56.1 4.8 %collective-permute-start.10 = (bf16[1,6,64,128]{3,2,1,0:T(8,128)(2,1)S(1)}, bf16[1,6,64,128]{3,2,1,0:T(8,128)(2,1)S(1)}, u32[]{:S(2)}, u32[]{:S(2)}) collective-permute-start(bf16[1,6,64,128]{3,2,1,0:T(8,128)(2,1)S(1)} %constant_dynamic-update-slice_fusion), channel_id=1, source_target_pairs={{0,64},{1,7},{2,66},{3,5},{4,68},{5,3},{6,70},{7,1},{8,72},{9,15},... | collective-permute-start | bytes 294920 | tf_op jit(solution)/shard_map/ppermute | solution.py:260
  60.9 5.3 %collective-permute-start.11 = (bf16[2,7,64,128]{3,2,1,0:T(8,128)(2,1)S(1)}, bf16[2,7,64,128]{3,2,1,0:T(8,128)(2,1)S(1)}, u32[]{:S(2)}, u32[]{:S(2)}) collective-permute-start(bf16[2,7,64,128]{3,2,1,0:T(8,128)(2,1)S(1)} %maximum_maximum_fusion.2), channel_id=1, source_target_pairs={{0,64},{1,3},{2,66},{3,1},{4,68},{5,7},{6,70},{7,5},{8,72},{9,11},... | collective-permute-start | bytes 688136 | tf_op jit(solution)/shard_map/ppermute | solution.py:260
  66.2 2.5 %collective-permute-start.12 = (bf16[4,8,64,128]{3,2,1,0:T(8,128)(2,1)S(1)}, bf16[4,8,64,128]{3,2,1,0:T(8,128)(2,1)S(1)}, u32[]{:S(2)}, u32[]{:S(2)}) collective-permute-start(bf16[4,8,64,128]{3,2,1,0:T(8,128)(2,1)S(1)} %maximum_maximum_fusion.own_ref), channel_id=1, source_target_pairs={{0,1},{1,0},{2,3},{3,2},{4,5},{5,4},{6,7},{7,6},{8,9},{9,8},{10,11... | collective-permute-start | bytes 1572872 | tf_op jit(solution)/shard_map/ppermute | solution.py:260
  71.7 3.6 %collective-permute-start.13 = (bf16[256,128]{1,0:T(8,128)(2,1)S(1)}, bf16[256,128]{1,0:T(8,128)(2,1)S(1)}, u32[]{:S(2)}, u32[]{:S(2)}) collective-permute-start(bf16[256,128]{1,0:T(8,128)(2,1)S(1)} %get-tuple-element.17), channel_id=1, source_target_pairs={{0,1},{1,0},{2,3},{3,2},{4,5},{5,4},{6,7},{7,6},{8,9},{9,8},{10,11... | collective-permute-start | bytes 196616 | tf_op jit(solution)/shard_map/ppermute | solution.py:282
  72.2 3.7 %collective-permute-start.14 = (bf16[256,128]{1,0:T(8,128)(2,1)S(1)}, bf16[256,128]{1,0:T(8,128)(2,1)S(1)}, u32[]{:S(2)}, u32[]{:S(2)}) collective-permute-start(bf16[256,128]{1,0:T(8,128)(2,1)S(1)} %get-tuple-element.18), channel_id=1, source_target_pairs={{0,7},{1,2},{2,1},{3,4},{4,3},{5,6},{6,5},{7,0},{8,15},{9,10},{10,... | collective-permute-start | bytes 196616 | tf_op jit(solution)/shard_map/ppermute | solution.py:283
  80.8 3.0 %collective-permute-start.15 = (bf16[4,8,64,128]{3,2,1,0:T(8,128)(2,1)S(1)}, bf16[4,8,64,128]{3,2,1,0:T(8,128)(2,1)S(1)}, u32[]{:S(2)}, u32[]{:S(2)}) collective-permute-start(bf16[4,8,64,128]{3,2,1,0:T(8,128)(2,1)S(1)} %get-tuple-element.20), channel_id=1, source_target_pairs={{0,1},{1,0},{2,3},{3,2},{4,5},{5,4},{6,7},{7,6},{8,9},{9,8},{10,11... | collective-permute-start | bytes 1572872 | tf_op jit(solution)/shard_map/ppermute | solution.py:260
  84.0 5.3 %collective-permute-start.16 = (bf16[2,7,64,128]{3,2,1,0:T(8,128)(2,1)S(1)}, bf16[2,7,64,128]{3,2,1,0:T(8,128)(2,1)S(1)}, u32[]{:S(2)}, u32[]{:S(2)}) collective-permute-start(bf16[2,7,64,128]{3,2,1,0:T(8,128)(2,1)S(1)} %fusion), channel_id=1, source_target_pairs={{0,64},{1,3},{2,66},{3,1},{4,68},{5,7},{6,70},{7,5},{8,72},{9,11},... | collective-permute-start | bytes 688136 | tf_op jit(solution)/shard_map/ppermute | solution.py:260
  89.3 4.8 %collective-permute-start.17 = (bf16[1,6,64,128]{3,2,1,0:T(8,128)(2,1)S(1)}, bf16[1,6,64,128]{3,2,1,0:T(8,128)(2,1)S(1)}, u32[]{:S(2)}, u32[]{:S(2)}) collective-permute-start(bf16[1,6,64,128]{3,2,1,0:T(8,128)(2,1)S(1)} %slice.344), channel_id=1, source_target_pairs={{0,64},{1,7},{2,66},{3,5},{4,68},{5,3},{6,70},{7,1},{8,72},{9,15},... | collective-permute-start | bytes 294920 | tf_op jit(solution)/shard_map/ppermute | solution.py:260
  94.1 3.6 %collective-permute-start.18 = (bf16[1,5,64,128]{3,2,1,0:T(8,128)(2,1)S(1)}, bf16[1,5,64,128]{3,2,1,0:T(8,128)(2,1)S(1)}, u32[]{:S(2)}, u32[]{:S(2)}) collective-permute-start(bf16[1,5,64,128]{3,2,1,0:T(8,128)(2,1)S(1)} %slice.346), channel_id=1, source_target_pairs={{0,2},{1,9},{2,0},{3,11},{4,6},{5,13},{6,4},{7,15},{8,10},{9,1},{1... | collective-permute-start | bytes 245768 | tf_op jit(solution)/shard_map/ppermute | solution.py:260
  97.7 4.7 %collective-permute-start.19 = (bf16[1,4,64,128]{3,2,1,0:T(8,128)(2,1)S(1)}, bf16[1,4,64,128]{3,2,1,0:T(8,128)(2,1)S(1)}, u32[]{:S(2)}, u32[]{:S(2)}) collective-permute-start(bf16[1,4,64,128]{3,2,1,0:T(8,128)(2,1)S(1)} %slice.348), channel_id=1, source_target_pairs={{0,2},{1,17},{2,0},{3,19},{4,6},{5,21},{6,4},{7,23},{8,10},{9,25},... | collective-permute-start | bytes 196616 | tf_op jit(solution)/shard_map/ppermute | solution.py:260
  102.5 6.9 %collective-permute-start.20 = (bf16[1,3,64,128]{3,2,1,0:T(8,128)(2,1)S(1)}, bf16[1,3,64,128]{3,2,1,0:T(8,128)(2,1)S(1)}, u32[]{:S(2)}, u32[]{:S(2)}) collective-permute-start(bf16[1,3,64,128]{3,2,1,0:T(8,128)(2,1)S(1)} %slice.350), channel_id=1, source_target_pairs={{0,2},{1,49},{2,0},{3,51},{4,6},{5,53},{6,4},{7,55},{8,10},{9,57},... | collective-permute-start | bytes 147464 | tf_op jit(solution)/shard_map/ppermute | solution.py:260
  109.4 2.9 %collective-permute-start.21 = (bf16[1,2,64,128]{3,2,1,0:T(8,128)(2,1)S(1)}, bf16[1,2,64,128]{3,2,1,0:T(8,128)(2,1)S(1)}, u32[]{:S(2)}, u32[]{:S(2)}) collective-permute-start(bf16[1,2,64,128]{3,2,1,0:T(8,128)(2,1)S(1)} %slice.352), channel_id=1, source_target_pairs={{0,2},{1,65},{2,0},{3,67},{4,6},{5,69},{6,4},{7,71},{8,10},{9,73},... | collective-permute-start | bytes 98312 | tf_op jit(solution)/shard_map/ppermute | solution.py:260
  112.3 4.0 %collective-permute-start.22 = (bf16[1,1,64,128]{3,2,1,0:T(8,128)(2,1)S(1)}, bf16[1,1,64,128]{3,2,1,0:T(8,128)(2,1)S(1)}, u32[]{:S(2)}, u32[]{:S(2)}) collective-permute-start(bf16[1,1,64,128]{3,2,1,0:T(8,128)(2,1)S(1)} %get-tuple-element.22), channel_id=1, source_target_pairs={{0,2},{1,193},{2,0},{3,195},{4,6},{5,197},{6,4},{7,199},{8,10},{9,... | collective-permute-start | bytes 49160 | tf_op jit(solution)/shard_map/ppermute | solution.py:260
  116.3 4.8 %collective-permute-start.23 = (bf16[1,6,64,128]{3,2,1,0:T(8,128)(2,1)S(1)}, bf16[1,6,64,128]{3,2,1,0:T(8,128)(2,1)S(1)}, u32[]{:S(2)}, u32[]{:S(2)}) collective-permute-start(bf16[1,6,64,128]{3,2,1,0:T(8,128)(2,1)S(1)} %constant_dynamic-update-slice_fusion.6), channel_id=1, source_target_pairs={{0,64},{1,7},{2,66},{3,5},{4,68},{5,3},{6,70},{7,1},{8,72},{9,15},... | collective-permute-start | bytes 294920 | tf_op jit(solution)/shard_map/ppermute | solution.py:260
  121.1 5.3 %collective-permute-start.24 = (bf16[2,7,64,128]{3,2,1,0:T(8,128)(2,1)S(1)}, bf16[2,7,64,128]{3,2,1,0:T(8,128)(2,1)S(1)}, u32[]{:S(2)}, u32[]{:S(2)}) collective-permute-start(bf16[2,7,64,128]{3,2,1,0:T(8,128)(2,1)S(1)} %maximum_maximum_fusion.3), channel_id=1, source_target_pairs={{0,64},{1,3},{2,66},{3,1},{4,68},{5,7},{6,70},{7,5},{8,72},{9,11},... | collective-permute-start | bytes 688136 | tf_op jit(solution)/shard_map/ppermute | solution.py:260
  126.4 2.4 %collective-permute-start.25 = (bf16[4,8,64,128]{3,2,1,0:T(8,128)(2,1)S(1)}, bf16[4,8,64,128]{3,2,1,0:T(8,128)(2,1)S(1)}, u32[]{:S(2)}, u32[]{:S(2)}) collective-permute-start(bf16[4,8,64,128]{3,2,1,0:T(8,128)(2,1)S(1)} %maximum_maximum_fusion.1.own_ref), channel_id=1, source_target_pairs={{0,1},{1,0},{2,3},{3,2},{4,5},{5,4},{6,7},{7,6},{8,9},{9,8},{10,11... | collective-permute-start | bytes 1572872 | tf_op jit(solution)/shard_map/ppermute | solution.py:260
  (2 other events, 2.5 us)

commit v2 on v1

--- a/solution.py
+++ b/solution.py
@@ -18,6 +18,7 @@
 SLICES = 4
 HALF = BLK // SLICES
 PIECE = 2 * HALF
+Z = 8
 
 LIMIT = 20 * 2**20
 
@@ -260,15 +261,26 @@
     return lax.ppermute(value, ("wide", "narrow"), pairs)
 
 
-def swapped(value, wide_mask, narrow_mask):
+def sent(value, real, other):
     wide, narrow = lax.axis_size("wide"), lax.axis_size("narrow")
-    other = (8, 0) if narrow_mask else (0, 2)
     pairs = []
     for w in range(wide):
         for n in range(narrow):
-            masks = (wide_mask, narrow_mask) if n % 2 else other
-            pairs.append((w * narrow + n, (w ^ masks[0]) * narrow + (n ^ masks[1])))
-    return moved(value, pairs)
+            to = real(w, n) if n % 2 else other(w, n)
+            pairs.append((w * narrow + n, to[0] * narrow + to[1]))
+    return moved(value, pairs).astype(f32)
+
+
+def masked(wide_mask, narrow_mask):
+    return lambda w, n: (w ^ wide_mask, n ^ narrow_mask)
+
+
+def along_z(steps):
+    return lambda w, n: (w - w % Z + (w + steps) % Z, n)
+
+
+X1, X2, X3 = masked(0, 2), masked(0, 4), masked(0, 6)
+Z1, Y1, Y2, Y3 = masked(1, 0), masked(8, 0), masked(16, 0), masked(24, 0)
 
 
 def handed(value):
@@ -288,30 +300,57 @@
     return (total * f32(2.0 ** (-level / 2))).astype(bf16)
 
 
-def summed(keep, send):
-    done = {}
+def summed(keep, send, spot):
     got = handed(send)
-    low, high = ((keep[part], got[part].astype(f32)) for part in (slice(0, 2), slice(2, 4)))
-    sent = (high[0][:, 1:] + high[1][:, 1:]).astype(bf16)
-    total = low[0] + low[1]
-    done[1] = jnp.concatenate(
-        [rounded(total[:, :1], 1), rounded(high[0][:, :1] + high[1][:, :1], 1)], axis=0
+
+    def pair(slices, levels):
+        return keep[slices, levels] + got[slices, levels].astype(f32)
+
+    upper = slice(2, LEVELS)
+    near = jnp.concatenate([pair(slice(2, 4), 1), pair(2, upper)], axis=0).astype(bf16)
+    near = sent(near, X1, Z1)
+    across = sent(pair(1, upper).astype(bf16), X3, Y1)
+    far = sent(pair(3, upper).astype(bf16), X2, Y3)
+    done1 = rounded(pair(slice(0, SLICES), slice(0, 1)), 1)
+    done2 = rounded(pair(slice(0, 2), 1) + near[:2], 2)
+    total = pair(0, upper) + near[2:] + across + far
+    done3 = rounded(total[:1], 3)
+
+    own = total[1:]
+    wire = own.astype(bf16)
+    left = sent(wire, along_z(1), X1)
+    right = sent(wire, along_z(-1), X3)
+    done4 = rounded(own[:1] + jnp.where(spot % 2 == 1, left[:1], right[:1]), 4)
+    first, last = spot % 4 == 0, spot % 4 == 3
+    own, left, right = own[1:], left[1:], right[1:]
+    zero = jnp.zeros_like(own[:1])
+    quad = own[:1]
+    window = left[1:] + own[1:] + right[1:]
+    down = jnp.concatenate([left[:1] + jnp.where(last, quad, zero), window], axis=0)
+    up = jnp.concatenate([right[:1] + jnp.where(first, quad, zero), own[1:] + right[1:]], axis=0)
+    above = sent(down.astype(bf16), along_z(-3), X1)
+    below = sent(up.astype(bf16), along_z(3), X3)
+    quad = quad + jnp.where(first, zero, left[:1]) + jnp.where(last, zero, right[:1])
+    done5 = rounded(quad + jnp.where(spot % 4 < 2, above[:1], below[:1]), 5)
+    total = window + above[1:] + below[1:]
+    done6 = rounded(total[:1], 6)
+
+    own = total[1:]
+    wire = own.astype(bf16)
+    near = sent(wire, Y1, X1)
+    across = sent(wire[1:], Y3, X3)
+    far = sent(wire[1:], Y2, Z1)
+    done7 = rounded(own[:1] + near[:1], 7)
+    done8 = rounded(own[1:] + near[1:] + across + far, 8)
+
+    mine = jnp.concatenate([done3, done4, done5, done6, done7, done8], axis=0)
+    near = sent(jnp.concatenate([done2, mine], axis=0), X1, Z1).astype(bf16)
+    across = sent(mine, X3, Y1).astype(bf16)
+    far = sent(mine, X2, Y3).astype(bf16)
+    slices = ((done2[:1], mine), (done2[1:], across), (near[:1], near[2:]), (near[1:2], far))
+    mine = jnp.stack(
+        [jnp.concatenate([done1[r], two, rest], axis=0) for r, (two, rest) in enumerate(slices)]
     )
-    for level, mask in ((2, 2), (3, 6)):
-        got = swapped(sent, 0, mask).astype(f32)
-        total = total[:, 1:] + got
-        done[level] = rounded(total[:, :1], level)
-        if level == 2:
-            sent = total[1:, 1:].astype(bf16)
-            total = total[:1]
-    for level, mask in ((4, 1), (5, 2), (6, 6), (7, 8), (8, 24)):
-        total = total[:, 1:]
-        total = total + swapped(total.astype(bf16), mask, 0).astype(f32)
-        done[level] = rounded(total[:, :1], level)
-    mine = jnp.concatenate([done[level] for level in range(3, LEVELS + 1)], axis=1)
-    for level, mask in ((2, 6), (1, 2)):
-        mine = jnp.concatenate([mine, swapped(mine, 0, mask)], axis=0)
-        mine = jnp.concatenate([done[level], mine], axis=1)
     return mine, handed(mine)
 
 
@@ -327,6 +366,7 @@
     couple = coupling[0, 0]
     inverse = inverse_blocks[0, 0]
     inverse_cols = inverse_columns[0, 0].reshape(-1)
+    spot = lax.axis_index("wide").astype(jnp.int32) % Z
     number = lax.axis_index("narrow").astype(jnp.int32)
     core, bit0, bit1 = number & 1, (number >> 1) & 1, (number >> 2) & 1
     inside = ((number > 0) & (number < lax.axis_size("narrow") - 1)).astype(jnp.int32)
@@ -338,7 +378,7 @@
         residual, keep, send = partial_of(
             base, inner, outer, couple, inverse, inverse_cols, faces, place
         )
-        own, got = summed(keep, send)
+        own, got = summed(keep, send, spot)
         last = sweep == ITERS - 1
         outs = update_of(own, got, current, inverse, inverse_cols, faces, place, not last)
         current = outs[0]

time: 133 us -> 121 us (0.910)
  waiting for transfers between devices: 55.2 us -> 39.6 us
  starting transfers between devices: 44.3 us -> 47.5 us
    ppermute x22 -> x30, waiting for transfers between devices: 54.7 us -> 38.4 us  [moved(): return lax.ppermute(value, ('wide', 'narrow'), pairs)]
    ppermute x22 -> x30, starting transfers between devices: 39.7 us -> 43.7 us  [moved(): return lax.ppermute(value, ('wide', 'narrow'), pairs)]
    unnamed x19 -> x30, local copies, waits for them, and re-layouts: 8.25 us -> 8.32 us
  transfers between devices with their start and end apart: 26 -> 34, of which waited for: 23 -> 21; matrix products, arithmetic and copies ran while one was open for 1% -> 2% of each run, Pallas kernels for 3% -> 4%
where the time goes in v2:
time: 121 us; the launch traced here: 120 us
  starting transfers between devices  47.5 us (39%)
  waiting for transfers between devices  39.6 us (33%)
  Pallas kernels  22.2 us (18%)
  local copies, waits for them, and re-layouts  8.61 us (7%)
  other arithmetic  1.26 us (1%)
  between operations  1.23 us (1%)
    ppermute x30, starting transfers between devices, moved(): return lax.ppermute(value, ('wide', 'narrow'), pairs)  43.7 us
    ppermute x30, waiting for transfers between devices, moved(): return lax.ppermute(value, ('wide', 'narrow'), pairs)  38.4 us
    pallas_call x2, Pallas kernels, partial_of(): pl.pallas_call(partial_kernel, grid_spec=pltpu.PrefetchScalarGridSpec(num...  9.86 us
    unnamed x30, local copies, waits for them, and re-layouts  8.32 us
    pallas_call x2, Pallas kernels, update_of(): pl.pallas_call(functools.partial(update_kernel, gather), grid_spec=pltpu....  6.54 us
    pallas_call x2, Pallas kernels, base_of(): pl.pallas_call(product_kernel, grid_spec=pltpu.PrefetchScalarGridSpec(num...  4.57 us
    ppermute x2, starting transfers between devices, faces_swapped(): lax.ppermute(inner, 'narrow', [(i, i ^ 1) for i in range(count)])  3.51 us
  transfers between devices with their start and end apart: 34, of which 21 were waited for; matrix products, arithmetic and copies ran while one was open for 2% of the time, Pallas kernels for 4%

profile of v2, /device:TPU:1, one launch (start us, length us, event | category | flops | bytes accessed | tf_op | source)
XLA Modules:
  0.0 120.3 jit_solution(10373382956651576033)
XLA Ops:
  3.8 3.3 %collective-permute-start = (bf16[256,128]{1,0:T(8,128)(2,1)S(1)}, bf16[256,128]{1,0:T(8,128)(2,1)S(1)}, u32[]{:S(2)}, u32[]{:S(2)}) collective-permute-start(bf16[256,128]{1,0:T(8,128)(2,1)S(1)} %get-tuple-element.12), channel_id=1, source_target_pairs={{0,1},{1,0},{2,3},{3,2},{4,5},{5,4},{6,7},{7,6},{8,9},{9,8},{10,11... | collective-permute-start | bytes 196616 | tf_op jit(solution)/shard_map/ppermute | solution.py:294
  8.8 2.2 %copy-done.2 = bf16[1,1,16,7,128,128]{5,4,3,2,1,0:T(8,128)(2,1)S(1)} copy-done((bf16[1,1,16,7,128,128]{5,4,3,2,1,0:T(8,128)(2,1)S(1)}, bf16[1,1,16,7,128,128]{5,4,3,2,1,0:T(8,128)(2,1)}, u32[]{:S(2)}) %copy-start.2) | copy-done | bytes 3670040
  13.6 2.3 %product.2.base_ref = f32[2048,128]{1,0:T(8,128)S(1)} custom-call(s32[112]{0:T(128)S(1)} %reshape_squeeze.11.cols_ref, bf16[16,7,128,128]{3,2,1,0:T(8,128)(2,1)S(1)} %bitcast.95, f32[2048,128]{1,0:T(8,128)S(1)} %bitcast.98, f32[2048,128]{1,0:T(8,128)S(1)} %bitcast.100), custom_call_target="tpu_custom_call" | custom-call | flops 469762048 | bytes 8000000 | tf_op jit(solution)/shard_map/product/pallas_call | solution.py:183
  16.0 4.9 %partial.2 = (f32[2048,128]{1,0:T(8,128)}, f32[4,8,64,128]{3,2,1,0:T(8,128)S(1)}, bf16[4,8,64,128]{3,2,1,0:T(8,128)(2,1)S(1)}) custom-call(s32[128]{0:T(128)S(1)} %reshape_squeeze.9.cols_ref, s32[512]{0:T(512)S(1)} %bitcast.105, s32[3]{0:T(128)S(1)} %pad_add_fusion.place_ref, bf16[16,8,128,128]{3,2,1,0:T(8,128)(2,1)S(1)} %bitcast.91, ...), custom_call_target="tpu_custom_call" | custom-call | flops 536870912 | bytes 8000000 | tf_op jit(solution)/shard_map/partial/pallas_call | solution.py:206
  23.7 2.0 %collective-permute-start.4 = (bf16[6,64,128]{2,1,0:T(8,128)(2,1)S(1)}, bf16[6,64,128]{2,1,0:T(8,128)(2,1)S(1)}, u32[]{:S(2)}, u32[]{:S(2)}) collective-permute-start(bf16[6,64,128]{2,1,0:T(8,128)(2,1)S(1)} %get-tuple-element.49), channel_id=1, source_target_pairs={{0,64},{1,7},{2,66},{3,5},{4,68},{5,3},{6,70},{7,1},{8,72},{9,15},... | collective-permute-start | bytes 294920 | tf_op jit(solution)/shard_map/ppermute | solution.py:261
  27.2 3.5 %collective-permute-done.3 = bf16[8,64,128]{2,1,0:T(8,128)(2,1)S(1)} collective-permute-done((bf16[8,64,128]{2,1,0:T(8,128)(2,1)S(1)}, bf16[8,64,128]{2,1,0:T(8,128)(2,1)S(1)}, u32[]{:S(2)}, u32[]{:S(2)}) %collective-permute-start.3) | collective-permute-done | bytes 131104 | tf_op jit(solution)/shard_map/ppermute | solution.py:261
  30.9 1.7 %collective-permute-start.6 = (bf16[5,64,128]{2,1,0:T(8,128)(2,1)S(1)}, bf16[5,64,128]{2,1,0:T(8,128)(2,1)S(1)}, u32[]{:S(2)}, u32[]{:S(2)}) collective-permute-start(bf16[5,64,128]{2,1,0:T(8,128)(2,1)S(1)} %slice.758), channel_id=1, source_target_pairs={{0,2},{1,9},{2,0},{3,11},{4,6},{5,13},{6,4},{7,15},{8,10},{9,17},{... | collective-permute-start | bytes 245768 | tf_op jit(solution)/shard_map/ppermute | solution.py:261
  32.6 4.0 %collective-permute-start.7 = (bf16[5,64,128]{2,1,0:T(8,128)(2,1)S(1)}, bf16[5,64,128]{2,1,0:T(8,128)(2,1)S(1)}, u32[]{:S(2)}, u32[]{:S(2)}) collective-permute-start(bf16[5,64,128]{2,1,0:T(8,128)(2,1)S(1)} %slice.758), channel_id=1, source_target_pairs={{0,6},{1,57},{2,4},{3,59},{4,2},{5,61},{6,0},{7,63},{8,14},{9,1},{... | collective-permute-start | bytes 245768 | tf_op jit(solution)/shard_map/ppermute | solution.py:261
  36.7 1.9 %collective-permute-done.6 = bf16[5,64,128]{2,1,0:T(8,128)(2,1)S(1)} collective-permute-done((bf16[5,64,128]{2,1,0:T(8,128)(2,1)S(1)}, bf16[5,64,128]{2,1,0:T(8,128)(2,1)S(1)}, u32[]{:S(2)}, u32[]{:S(2)}) %collective-permute-start.6) | collective-permute-done | bytes 81952 | tf_op jit(solution)/shard_map/ppermute | solution.py:261
  38.7 4.4 %collective-permute-start.9 = (bf16[4,64,128]{2,1,0:T(8,128)(2,1)S(1)}, bf16[4,64,128]{2,1,0:T(8,128)(2,1)S(1)}, u32[]{:S(2)}, u32[]{:S(2)}) collective-permute-start(bf16[4,64,128]{2,1,0:T(8,128)(2,1)S(1)} %pad_maximum_fusion.5), channel_id=1, source_target_pairs={{0,6},{1,25},{2,4},{3,27},{4,2},{5,29},{6,0},{7,31},{8,14},{9,33},... | collective-permute-start | bytes 196616 | tf_op jit(solution)/shard_map/ppermute | solution.py:261
  43.3 1.6 %collective-permute-done.9 = bf16[4,64,128]{2,1,0:T(8,128)(2,1)S(1)} collective-permute-done((bf16[4,64,128]{2,1,0:T(8,128)(2,1)S(1)}, bf16[4,64,128]{2,1,0:T(8,128)(2,1)S(1)}, u32[]{:S(2)}, u32[]{:S(2)}) %collective-permute-start.9) | collective-permute-done | bytes 65568 | tf_op jit(solution)/shard_map/ppermute | solution.py:261
  45.0 3.1 %collective-permute-done.8 = bf16[4,64,128]{2,1,0:T(8,128)(2,1)S(1)} collective-permute-done((bf16[4,64,128]{2,1,0:T(8,128)(2,1)S(1)}, bf16[4,64,128]{2,1,0:T(8,128)(2,1)S(1)}, u32[]{:S(2)}, u32[]{:S(2)}) %collective-permute-start.8) | collective-permute-done | bytes 65568 | tf_op jit(solution)/shard_map/ppermute | solution.py:261
  48.1 2.4 %collective-permute-start.12 = (bf16[1,64,128]{2,1,0:T(8,128)(2,1)S(1)}, bf16[1,64,128]{2,1,0:T(8,128)(2,1)S(1)}, u32[]{:S(2)}, u32[]{:S(2)}) collective-permute-start(bf16[1,64,128]{2,1,0:T(8,128)(2,1)S(1)} %slice.452), channel_id=1, source_target_pairs={{0,8},{1,129},{2,10},{3,131},{4,12},{5,133},{6,14},{7,135},{8,0},{... | collective-permute-start | bytes 49160 | tf_op jit(solution)/shard_map/ppermute | solution.py:261
  51.8 2.7 %collective-permute-done.10 = bf16[2,64,128]{2,1,0:T(8,128)(2,1)S(1)} collective-permute-done((bf16[2,64,128]{2,1,0:T(8,128)(2,1)S(1)}, bf16[2,64,128]{2,1,0:T(8,128)(2,1)S(1)}, u32[]{:S(2)}, u32[]{:S(2)}) %collective-permute-start.10) | collective-permute-done | bytes 32800 | tf_op jit(solution)/shard_map/ppermute | solution.py:261
  55.5 3.0 %collective-permute-start.15 = (bf16[6,64,128]{2,1,0:T(8,128)(2,1)S(1)}, bf16[6,64,128]{2,1,0:T(8,128)(2,1)S(1)}, u32[]{:S(2)}, u32[]{:S(2)}) collective-permute-start(bf16[6,64,128]{2,1,0:T(8,128)(2,1)S(1)} %get-tuple-element.95), channel_id=1, source_target_pairs={{0,192},{1,5},{2,194},{3,7},{4,196},{5,1},{6,198},{7,3},{8,200},{9... | collective-permute-start | bytes 294920 | tf_op jit(solution)/shard_map/ppermute | solution.py:261
  59.4 2.5 %collective-permute-done.15 = bf16[6,64,128]{2,1,0:T(8,128)(2,1)S(1)} collective-permute-done((bf16[6,64,128]{2,1,0:T(8,128)(2,1)S(1)}, bf16[6,64,128]{2,1,0:T(8,128)(2,1)S(1)}, u32[]{:S(2)}, u32[]{:S(2)}) %collective-permute-start.15) | collective-permute-done | bytes 98336 | tf_op jit(solution)/shard_map/ppermute | solution.py:261
  62.3 1.9 %collective-permute-done.16.got_ref = bf16[4,8,64,128]{3,2,1,0:T(8,128)(2,1)S(1)} collective-permute-done((bf16[4,8,64,128]{3,2,1,0:T(8,128)(2,1)S(1)}, bf16[4,8,64,128]{3,2,1,0:T(8,128)(2,1)S(1)}, u32[]{:S(2)}, u32[]{:S(2)}) %collective-permute-start.16) | collective-permute-done | bytes 524320 | tf_op jit(solution)/shard_map/ppermute | solution.py:261
  64.2 3.1 %update.2 = (f32[2048,128]{1,0:T(8,128)S(1)}, bf16[256,128]{1,0:T(8,128)(2,1)S(1)}, bf16[256,128]{1,0:T(8,128)(2,1)S(1)}) custom-call(s32[128]{0:T(128)S(1)} %reshape_squeeze.9.cols_ref, s32[512]{0:T(512)S(1)} %bitcast.106, s32[3]{0:T(128)S(1)} %pad_add_fusion.place_ref, bf16[16,8,128,128]{3,2,1,0:T(8,128)(2,1)S(1)} %bitcast.92, ...), custom_call_target="tpu_custom_call" | custom-call | flops 536870912 | bytes 8000000 | tf_op jit(solution)/shard_map/update/pallas_call | solution.py:237
  67.8 2.3 %product.3.base_ref = f32[2048,128]{1,0:T(8,128)S(1)} custom-call(s32[112]{0:T(128)S(1)} %reshape_squeeze.11.cols_ref, bf16[16,7,128,128]{3,2,1,0:T(8,128)(2,1)S(1)} %bitcast.96, f32[2048,128]{1,0:T(8,128)S(1)} %get-tuple-element.16.cur_ref, f32[2048,128]{1,0:T(8,128)S(1)} %bitcast.101), custom_call_target="tpu_custom_call" | custom-call | flops 469762048 | bytes 8000000 | tf_op jit(solution)/shard_map/product/pallas_call | solution.py:183
  71.2 4.9 %partial.3 = (f32[2048,128]{1,0:T(8,128)}, f32[4,8,64,128]{3,2,1,0:T(8,128)S(1)}, bf16[4,8,64,128]{3,2,1,0:T(8,128)(2,1)S(1)}) custom-call(s32[128]{0:T(128)S(1)} %reshape_squeeze.9.cols_ref, s32[512]{0:T(512)S(1)} %bitcast.107, s32[3]{0:T(128)S(1)} %pad_add_fusion.place_ref, bf16[16,8,128,128]{3,2,1,0:T(8,128)(2,1)S(1)} %bitcast.93, ...), custom_call_target="tpu_custom_call" | custom-call | flops 536870912 | bytes 8000000 | tf_op jit(solution)/shard_map/partial/pallas_call | solution.py:206
  76.2 1.6 %collective-permute-start.19 = (bf16[4,8,64,128]{3,2,1,0:T(8,128)(2,1)S(1)}, bf16[4,8,64,128]{3,2,1,0:T(8,128)(2,1)S(1)}, u32[]{:S(2)}, u32[]{:S(2)}) collective-permute-start(bf16[4,8,64,128]{3,2,1,0:T(8,128)(2,1)S(1)} %get-tuple-element.20), channel_id=1, source_target_pairs={{0,1},{1,0},{2,3},{3,2},{4,5},{5,4},{6,7},{7,6},{8,9},{9,8},{10,11... | collective-permute-start | bytes 1572872 | tf_op jit(solution)/shard_map/ppermute | solution.py:261
  80.3 2.5 %collective-permute-start.20 = (bf16[8,64,128]{2,1,0:T(8,128)(2,1)S(1)}, bf16[8,64,128]{2,1,0:T(8,128)(2,1)S(1)}, u32[]{:S(2)}, u32[]{:S(2)}) collective-permute-start(bf16[8,64,128]{2,1,0:T(8,128)(2,1)S(1)} %pad_maximum_fusion.3), channel_id=1, source_target_pairs={{0,8},{1,3},{2,10},{3,1},{4,12},{5,7},{6,14},{7,5},{8,0},{9,11},{1... | collective-permute-start | bytes 393224 | tf_op jit(solution)/shard_map/ppermute | solution.py:261
  82.9 3.2 %collective-permute-done.20 = bf16[8,64,128]{2,1,0:T(8,128)(2,1)S(1)} collective-permute-done((bf16[8,64,128]{2,1,0:T(8,128)(2,1)S(1)}, bf16[8,64,128]{2,1,0:T(8,128)(2,1)S(1)}, u32[]{:S(2)}, u32[]{:S(2)}) %collective-permute-start.20) | collective-permute-done | bytes 131104 | tf_op jit(solution)/shard_map/ppermute | solution.py:261
  86.2 3.2 %collective-permute-start.23 = (bf16[5,64,128]{2,1,0:T(8,128)(2,1)S(1)}, bf16[5,64,128]{2,1,0:T(8,128)(2,1)S(1)}, u32[]{:S(2)}, u32[]{:S(2)}) collective-permute-start(bf16[5,64,128]{2,1,0:T(8,128)(2,1)S(1)} %slice.757), channel_id=1, source_target_pairs={{0,2},{1,9},{2,0},{3,11},{4,6},{5,13},{6,4},{7,15},{8,10},{9,17},{... | collective-permute-start | bytes 245768 | tf_op jit(solution)/shard_map/ppermute | solution.py:261
  91.0 2.1 %collective-permute-done.24 = bf16[5,64,128]{2,1,0:T(8,128)(2,1)S(1)} collective-permute-done((bf16[5,64,128]{2,1,0:T(8,128)(2,1)S(1)}, bf16[5,64,128]{2,1,0:T(8,128)(2,1)S(1)}, u32[]{:S(2)}, u32[]{:S(2)}) %collective-permute-start.24) | collective-permute-done | bytes 81952 | tf_op jit(solution)/shard_map/ppermute | solution.py:261
  93.1 2.5 %collective-permute-start.26 = (bf16[4,64,128]{2,1,0:T(8,128)(2,1)S(1)}, bf16[4,64,128]{2,1,0:T(8,128)(2,1)S(1)}, u32[]{:S(2)}, u32[]{:S(2)}) collective-permute-start(bf16[4,64,128]{2,1,0:T(8,128)(2,1)S(1)} %pad_maximum_fusion.7), channel_id=1, source_target_pairs={{0,6},{1,25},{2,4},{3,27},{4,2},{5,29},{6,0},{7,31},{8,14},{9,33},... | collective-permute-start | bytes 196616 | tf_op jit(solution)/shard_map/ppermute | solution.py:261
  95.7 2.1 %collective-permute-start.25 = (bf16[4,64,128]{2,1,0:T(8,128)(2,1)S(1)}, bf16[4,64,128]{2,1,0:T(8,128)(2,1)S(1)}, u32[]{:S(2)}, u32[]{:S(2)}) collective-permute-start(bf16[4,64,128]{2,1,0:T(8,128)(2,1)S(1)} %pad_maximum_fusion.6), channel_id=1, source_target_pairs={{0,2},{1,41},{2,0},{3,43},{4,6},{5,45},{6,4},{7,47},{8,10},{9,49},... | collective-permute-start | bytes 196616 | tf_op jit(solution)/shard_map/ppermute | solution.py:261
  97.8 2.4 %collective-permute-done.26 = bf16[4,64,128]{2,1,0:T(8,128)(2,1)S(1)} collective-permute-done((bf16[4,64,128]{2,1,0:T(8,128)(2,1)S(1)}, bf16[4,64,128]{2,1,0:T(8,128)(2,1)S(1)}, u32[]{:S(2)}, u32[]{:S(2)}) %collective-permute-start.26) | collective-permute-done | bytes 65568 | tf_op jit(solution)/shard_map/ppermute | solution.py:261
  103.6 2.7 %collective-permute-done.27 = bf16[2,64,128]{2,1,0:T(8,128)(2,1)S(1)} collective-permute-done((bf16[2,64,128]{2,1,0:T(8,128)(2,1)S(1)}, bf16[2,64,128]{2,1,0:T(8,128)(2,1)S(1)}, u32[]{:S(2)}, u32[]{:S(2)}) %collective-permute-start.27) | collective-permute-done | bytes 32800 | tf_op jit(solution)/shard_map/ppermute | solution.py:261
  106.4 1.6 %collective-permute-start.30 = (bf16[6,64,128]{2,1,0:T(8,128)(2,1)S(1)}, bf16[6,64,128]{2,1,0:T(8,128)(2,1)S(1)}, u32[]{:S(2)}, u32[]{:S(2)}) collective-permute-start(bf16[6,64,128]{2,1,0:T(8,128)(2,1)S(1)} %get-tuple-element.87), channel_id=1, source_target_pairs={{0,64},{1,7},{2,66},{3,5},{4,68},{5,3},{6,70},{7,1},{8,72},{9,15},... | collective-permute-start | bytes 294920 | tf_op jit(solution)/shard_map/ppermute | solution.py:261
  108.1 2.3 %collective-permute-start.32 = (bf16[6,64,128]{2,1,0:T(8,128)(2,1)S(1)}, bf16[6,64,128]{2,1,0:T(8,128)(2,1)S(1)}, u32[]{:S(2)}, u32[]{:S(2)}) collective-permute-start(bf16[6,64,128]{2,1,0:T(8,128)(2,1)S(1)} %get-tuple-element.87), channel_id=1, source_target_pairs={{0,192},{1,5},{2,194},{3,7},{4,196},{5,1},{6,198},{7,3},{8,200},{9... | collective-permute-start | bytes 294920 | tf_op jit(solution)/shard_map/ppermute | solution.py:261
  116.9 3.4 %update.3 = f32[2048,128]{1,0:T(8,128)} custom-call(s32[128]{0:T(128)S(1)} %reshape_squeeze.9.cols_ref, s32[512]{0:T(512)S(1)} %bitcast.108, s32[3]{0:T(128)S(1)} %pad_add_fusion.place_ref, bf16[16,8,128,128]{3,2,1,0:T(8,128)(2,1)S(1)} %bitcast.94, bf16[4,8,64,128]{3,2,1,0:T(8,128)(2,1)S(1)} %pad_maximum_fusion.1.own_ref, ...), custom_call_target="tpu_custom_call" | custom-call | flops 536870912 | bytes 8000000 | tf_op jit(solution)/shard_map/update/pallas_call | solution.py:237
  (146 shorter events, 31.4 us)
Async XLA Ops:
  3.8 12.1 %collective-permute-start = (bf16[256,128]{1,0:T(8,128)(2,1)S(1)}, bf16[256,128]{1,0:T(8,128)(2,1)S(1)}, u32[]{:S(2)}, u32[]{:S(2)}) collective-permute-start(bf16[256,128]{1,0:T(8,128)(2,1)S(1)} %get-tuple-element.12), channel_id=1, source_target_pairs={{0,1},{1,0},{2,3},{3,2},{4,5},{5,4},{6,7},{7,6},{8,9},{9,8},{10,11... | collective-permute-start | bytes 196616 | tf_op jit(solution)/shard_map/ppermute | solution.py:294
  7.1 8.8 %collective-permute-start.1 = (bf16[256,128]{1,0:T(8,128)(2,1)S(1)}, bf16[256,128]{1,0:T(8,128)(2,1)S(1)}, u32[]{:S(2)}, u32[]{:S(2)}) collective-permute-start(bf16[256,128]{1,0:T(8,128)(2,1)S(1)} %get-tuple-element.13), channel_id=1, source_target_pairs={{0,7},{1,2},{2,1},{3,4},{4,3},{5,6},{6,5},{7,0},{8,15},{9,10},{10,... | collective-permute-start | bytes 196616 | tf_op jit(solution)/shard_map/ppermute | solution.py:295
  23.7 7.1 %collective-permute-start.4 = (bf16[6,64,128]{2,1,0:T(8,128)(2,1)S(1)}, bf16[6,64,128]{2,1,0:T(8,128)(2,1)S(1)}, u32[]{:S(2)}, u32[]{:S(2)}) collective-permute-start(bf16[6,64,128]{2,1,0:T(8,128)(2,1)S(1)} %get-tuple-element.49), channel_id=1, source_target_pairs={{0,64},{1,7},{2,66},{3,5},{4,68},{5,3},{6,70},{7,1},{8,72},{9,15},... | collective-permute-start | bytes 294920 | tf_op jit(solution)/shard_map/ppermute | solution.py:261
  25.7 5.1 %collective-permute-start.5 = (bf16[6,64,128]{2,1,0:T(8,128)(2,1)S(1)}, bf16[6,64,128]{2,1,0:T(8,128)(2,1)S(1)}, u32[]{:S(2)}, u32[]{:S(2)}) collective-permute-start(bf16[6,64,128]{2,1,0:T(8,128)(2,1)S(1)} %get-tuple-element.51), channel_id=1, source_target_pairs={{0,192},{1,5},{2,194},{3,7},{4,196},{5,1},{6,198},{7,3},{8,200},{9... | collective-permute-start | bytes 294920 | tf_op jit(solution)/shard_map/ppermute | solution.py:261
  26.3 4.4 %collective-permute-start.3 = (bf16[8,64,128]{2,1,0:T(8,128)(2,1)S(1)}, bf16[8,64,128]{2,1,0:T(8,128)(2,1)S(1)}, u32[]{:S(2)}, u32[]{:S(2)}) collective-permute-start(bf16[8,64,128]{2,1,0:T(8,128)(2,1)S(1)} %pad_maximum_fusion.2), channel_id=1, source_target_pairs={{0,8},{1,3},{2,10},{3,1},{4,12},{5,7},{6,14},{7,5},{8,0},{9,11},{1... | collective-permute-start | bytes 393224 | tf_op jit(solution)/shard_map/ppermute | solution.py:261
  30.9 7.7 %collective-permute-start.6 = (bf16[5,64,128]{2,1,0:T(8,128)(2,1)S(1)}, bf16[5,64,128]{2,1,0:T(8,128)(2,1)S(1)}, u32[]{:S(2)}, u32[]{:S(2)}) collective-permute-start(bf16[5,64,128]{2,1,0:T(8,128)(2,1)S(1)} %slice.758), channel_id=1, source_target_pairs={{0,2},{1,9},{2,0},{3,11},{4,6},{5,13},{6,4},{7,15},{8,10},{9,17},{... | collective-permute-start | bytes 245768 | tf_op jit(solution)/shard_map/ppermute | solution.py:261
  32.6 6.0 %collective-permute-start.7 = (bf16[5,64,128]{2,1,0:T(8,128)(2,1)S(1)}, bf16[5,64,128]{2,1,0:T(8,128)(2,1)S(1)}, u32[]{:S(2)}, u32[]{:S(2)}) collective-permute-start(bf16[5,64,128]{2,1,0:T(8,128)(2,1)S(1)} %slice.758), channel_id=1, source_target_pairs={{0,6},{1,57},{2,4},{3,59},{4,2},{5,61},{6,0},{7,63},{8,14},{9,1},{... | collective-permute-start | bytes 245768 | tf_op jit(solution)/shard_map/ppermute | solution.py:261
  38.7 6.3 %collective-permute-start.9 = (bf16[4,64,128]{2,1,0:T(8,128)(2,1)S(1)}, bf16[4,64,128]{2,1,0:T(8,128)(2,1)S(1)}, u32[]{:S(2)}, u32[]{:S(2)}) collective-permute-start(bf16[4,64,128]{2,1,0:T(8,128)(2,1)S(1)} %pad_maximum_fusion.5), channel_id=1, source_target_pairs={{0,6},{1,25},{2,4},{3,27},{4,2},{5,29},{6,0},{7,31},{8,14},{9,33},... | collective-permute-start | bytes 196616 | tf_op jit(solution)/shard_map/ppermute | solution.py:261
  43.1 5.0 %collective-permute-start.8 = (bf16[4,64,128]{2,1,0:T(8,128)(2,1)S(1)}, bf16[4,64,128]{2,1,0:T(8,128)(2,1)S(1)}, u32[]{:S(2)}, u32[]{:S(2)}) collective-permute-start(bf16[4,64,128]{2,1,0:T(8,128)(2,1)S(1)} %pad_maximum_fusion.4), channel_id=1, source_target_pairs={{0,2},{1,41},{2,0},{3,43},{4,6},{5,45},{6,4},{7,47},{8,10},{9,49},... | collective-permute-start | bytes 196616 | tf_op jit(solution)/shard_map/ppermute | solution.py:261
  48.1 6.4 %collective-permute-start.12 = (bf16[1,64,128]{2,1,0:T(8,128)(2,1)S(1)}, bf16[1,64,128]{2,1,0:T(8,128)(2,1)S(1)}, u32[]{:S(2)}, u32[]{:S(2)}) collective-permute-start(bf16[1,64,128]{2,1,0:T(8,128)(2,1)S(1)} %slice.452), channel_id=1, source_target_pairs={{0,8},{1,129},{2,10},{3,131},{4,12},{5,133},{6,14},{7,135},{8,0},{... | collective-permute-start | bytes 49160 | tf_op jit(solution)/shard_map/ppermute | solution.py:261
  50.6 3.9 %collective-permute-start.11 = (bf16[1,64,128]{2,1,0:T(8,128)(2,1)S(1)}, bf16[1,64,128]{2,1,0:T(8,128)(2,1)S(1)}, u32[]{:S(2)}, u32[]{:S(2)}) collective-permute-start(bf16[1,64,128]{2,1,0:T(8,128)(2,1)S(1)} %slice.452), channel_id=1, source_target_pairs={{0,6},{1,193},{2,4},{3,195},{4,2},{5,197},{6,0},{7,199},{8,14},{9,... | collective-permute-start | bytes 49160 | tf_op jit(solution)/shard_map/ppermute | solution.py:261
  51.7 2.8 %collective-permute-start.10 = (bf16[2,64,128]{2,1,0:T(8,128)(2,1)S(1)}, bf16[2,64,128]{2,1,0:T(8,128)(2,1)S(1)}, u32[]{:S(2)}, u32[]{:S(2)}) collective-permute-start(bf16[2,64,128]{2,1,0:T(8,128)(2,1)S(1)} %slice.448), channel_id=1, source_target_pairs={{0,2},{1,65},{2,0},{3,67},{4,6},{5,69},{6,4},{7,71},{8,10},{9,73},... | collective-permute-start | bytes 98312 | tf_op jit(solution)/shard_map/ppermute | solution.py:261
  54.6 4.8 %collective-permute-start.13 = (bf16[6,64,128]{2,1,0:T(8,128)(2,1)S(1)}, bf16[6,64,128]{2,1,0:T(8,128)(2,1)S(1)}, u32[]{:S(2)}, u32[]{:S(2)}) collective-permute-start(bf16[6,64,128]{2,1,0:T(8,128)(2,1)S(1)} %get-tuple-element.95), channel_id=1, source_target_pairs={{0,64},{1,7},{2,66},{3,5},{4,68},{5,3},{6,70},{7,1},{8,72},{9,15},... | collective-permute-start | bytes 294920 | tf_op jit(solution)/shard_map/ppermute | solution.py:261
  55.5 3.9 %collective-permute-start.14 = (bf16[8,64,128]{2,1,0:T(8,128)(2,1)S(1)}, bf16[8,64,128]{2,1,0:T(8,128)(2,1)S(1)}, u32[]{:S(2)}, u32[]{:S(2)}) collective-permute-start(bf16[8,64,128]{2,1,0:T(8,128)(2,1)S(1)} %get-tuple-element.94), channel_id=1, source_target_pairs={{0,8},{1,3},{2,10},{3,1},{4,12},{5,7},{6,14},{7,5},{8,0},{9,11},{1... | collective-permute-start | bytes 393224 | tf_op jit(solution)/shard_map/ppermute | solution.py:261
  55.5 6.4 %collective-permute-start.15 = (bf16[6,64,128]{2,1,0:T(8,128)(2,1)S(1)}, bf16[6,64,128]{2,1,0:T(8,128)(2,1)S(1)}, u32[]{:S(2)}, u32[]{:S(2)}) collective-permute-start(bf16[6,64,128]{2,1,0:T(8,128)(2,1)S(1)} %get-tuple-element.95), channel_id=1, source_target_pairs={{0,192},{1,5},{2,194},{3,7},{4,196},{5,1},{6,198},{7,3},{8,200},{9... | collective-permute-start | bytes 294920 | tf_op jit(solution)/shard_map/ppermute | solution.py:261
  67.3 2.8 %collective-permute-start.17 = (bf16[256,128]{1,0:T(8,128)(2,1)S(1)}, bf16[256,128]{1,0:T(8,128)(2,1)S(1)}, u32[]{:S(2)}, u32[]{:S(2)}) collective-permute-start(bf16[256,128]{1,0:T(8,128)(2,1)S(1)} %get-tuple-element.17), channel_id=1, source_target_pairs={{0,1},{1,0},{2,3},{3,2},{4,5},{5,4},{6,7},{7,6},{8,9},{9,8},{10,11... | collective-permute-start | bytes 196616 | tf_op jit(solution)/shard_map/ppermute | solution.py:294
  67.5 3.7 %collective-permute-start.18 = (bf16[256,128]{1,0:T(8,128)(2,1)S(1)}, bf16[256,128]{1,0:T(8,128)(2,1)S(1)}, u32[]{:S(2)}, u32[]{:S(2)}) collective-permute-start(bf16[256,128]{1,0:T(8,128)(2,1)S(1)} %get-tuple-element.18), channel_id=1, source_target_pairs={{0,7},{1,2},{2,1},{3,4},{4,3},{5,6},{6,5},{7,0},{8,15},{9,10},{10,... | collective-permute-start | bytes 196616 | tf_op jit(solution)/shard_map/ppermute | solution.py:295
  76.2 3.1 %collective-permute-start.19 = (bf16[4,8,64,128]{3,2,1,0:T(8,128)(2,1)S(1)}, bf16[4,8,64,128]{3,2,1,0:T(8,128)(2,1)S(1)}, u32[]{:S(2)}, u32[]{:S(2)}) collective-permute-start(bf16[4,8,64,128]{3,2,1,0:T(8,128)(2,1)S(1)} %get-tuple-element.20), channel_id=1, source_target_pairs={{0,1},{1,0},{2,3},{3,2},{4,5},{5,4},{6,7},{7,6},{8,9},{9,8},{10,11... | collective-permute-start | bytes 1572872 | tf_op jit(solution)/shard_map/ppermute | solution.py:261
  79.4 6.8 %collective-permute-start.21 = (bf16[6,64,128]{2,1,0:T(8,128)(2,1)S(1)}, bf16[6,64,128]{2,1,0:T(8,128)(2,1)S(1)}, u32[]{:S(2)}, u32[]{:S(2)}) collective-permute-start(bf16[6,64,128]{2,1,0:T(8,128)(2,1)S(1)} %get-tuple-element.46), channel_id=1, source_target_pairs={{0,64},{1,7},{2,66},{3,5},{4,68},{5,3},{6,70},{7,1},{8,72},{9,15},... | collective-permute-start | bytes 294920 | tf_op jit(solution)/shard_map/ppermute | solution.py:261
  80.3 5.9 %collective-permute-start.22 = (bf16[6,64,128]{2,1,0:T(8,128)(2,1)S(1)}, bf16[6,64,128]{2,1,0:T(8,128)(2,1)S(1)}, u32[]{:S(2)}, u32[]{:S(2)}) collective-permute-start(bf16[6,64,128]{2,1,0:T(8,128)(2,1)S(1)} %get-tuple-element.47), channel_id=1, source_target_pairs={{0,192},{1,5},{2,194},{3,7},{4,196},{5,1},{6,198},{7,3},{8,200},{9... | collective-permute-start | bytes 294920 | tf_op jit(solution)/shard_map/ppermute | solution.py:261
  80.3 5.8 %collective-permute-start.20 = (bf16[8,64,128]{2,1,0:T(8,128)(2,1)S(1)}, bf16[8,64,128]{2,1,0:T(8,128)(2,1)S(1)}, u32[]{:S(2)}, u32[]{:S(2)}) collective-permute-start(bf16[8,64,128]{2,1,0:T(8,128)(2,1)S(1)} %pad_maximum_fusion.3), channel_id=1, source_target_pairs={{0,8},{1,3},{2,10},{3,1},{4,12},{5,7},{6,14},{7,5},{8,0},{9,11},{1... | collective-permute-start | bytes 393224 | tf_op jit(solution)/shard_map/ppermute | solution.py:261
  86.2 4.7 %collective-permute-start.23 = (bf16[5,64,128]{2,1,0:T(8,128)(2,1)S(1)}, bf16[5,64,128]{2,1,0:T(8,128)(2,1)S(1)}, u32[]{:S(2)}, u32[]{:S(2)}) collective-permute-start(bf16[5,64,128]{2,1,0:T(8,128)(2,1)S(1)} %slice.757), channel_id=1, source_target_pairs={{0,2},{1,9},{2,0},{3,11},{4,6},{5,13},{6,4},{7,15},{8,10},{9,17},{... | collective-permute-start | bytes 245768 | tf_op jit(solution)/shard_map/ppermute | solution.py:261
  89.5 3.6 %collective-permute-start.24 = (bf16[5,64,128]{2,1,0:T(8,128)(2,1)S(1)}, bf16[5,64,128]{2,1,0:T(8,128)(2,1)S(1)}, u32[]{:S(2)}, u32[]{:S(2)}) collective-permute-start(bf16[5,64,128]{2,1,0:T(8,128)(2,1)S(1)} %slice.757), channel_id=1, source_target_pairs={{0,6},{1,57},{2,4},{3,59},{4,2},{5,61},{6,0},{7,63},{8,14},{9,1},{... | collective-permute-start | bytes 245768 | tf_op jit(solution)/shard_map/ppermute | solution.py:261
  93.1 7.1 %collective-permute-start.26 = (bf16[4,64,128]{2,1,0:T(8,128)(2,1)S(1)}, bf16[4,64,128]{2,1,0:T(8,128)(2,1)S(1)}, u32[]{:S(2)}, u32[]{:S(2)}) collective-permute-start(bf16[4,64,128]{2,1,0:T(8,128)(2,1)S(1)} %pad_maximum_fusion.7), channel_id=1, source_target_pairs={{0,6},{1,25},{2,4},{3,27},{4,2},{5,29},{6,0},{7,31},{8,14},{9,33},... | collective-permute-start | bytes 196616 | tf_op jit(solution)/shard_map/ppermute | solution.py:261
  95.7 5.0 %collective-permute-start.25 = (bf16[4,64,128]{2,1,0:T(8,128)(2,1)S(1)}, bf16[4,64,128]{2,1,0:T(8,128)(2,1)S(1)}, u32[]{:S(2)}, u32[]{:S(2)}) collective-permute-start(bf16[4,64,128]{2,1,0:T(8,128)(2,1)S(1)} %pad_maximum_fusion.6), channel_id=1, source_target_pairs={{0,2},{1,41},{2,0},{3,43},{4,6},{5,45},{6,4},{7,47},{8,10},{9,49},... | collective-permute-start | bytes 196616 | tf_op jit(solution)/shard_map/ppermute | solution.py:261
  100.8 5.6 %collective-permute-start.29 = (bf16[1,64,128]{2,1,0:T(8,128)(2,1)S(1)}, bf16[1,64,128]{2,1,0:T(8,128)(2,1)S(1)}, u32[]{:S(2)}, u32[]{:S(2)}) collective-permute-start(bf16[1,64,128]{2,1,0:T(8,128)(2,1)S(1)} %slice.493), channel_id=1, source_target_pairs={{0,8},{1,129},{2,10},{3,131},{4,12},{5,133},{6,14},{7,135},{8,0},{... | collective-permute-start | bytes 49160 | tf_op jit(solution)/shard_map/ppermute | solution.py:261
  102.2 4.2 %collective-permute-start.28 = (bf16[1,64,128]{2,1,0:T(8,128)(2,1)S(1)}, bf16[1,64,128]{2,1,0:T(8,128)(2,1)S(1)}, u32[]{:S(2)}, u32[]{:S(2)}) collective-permute-start(bf16[1,64,128]{2,1,0:T(8,128)(2,1)S(1)} %slice.493), channel_id=1, source_target_pairs={{0,6},{1,193},{2,4},{3,195},{4,2},{5,197},{6,0},{7,199},{8,14},{9,... | collective-permute-start | bytes 49160 | tf_op jit(solution)/shard_map/ppermute | solution.py:261
  103.3 3.1 %collective-permute-start.27 = (bf16[2,64,128]{2,1,0:T(8,128)(2,1)S(1)}, bf16[2,64,128]{2,1,0:T(8,128)(2,1)S(1)}, u32[]{:S(2)}, u32[]{:S(2)}) collective-permute-start(bf16[2,64,128]{2,1,0:T(8,128)(2,1)S(1)} %slice.489), channel_id=1, source_target_pairs={{0,2},{1,65},{2,0},{3,67},{4,6},{5,69},{6,4},{7,71},{8,10},{9,73},... | collective-permute-start | bytes 98312 | tf_op jit(solution)/shard_map/ppermute | solution.py:261
  106.4 4.8 %collective-permute-start.30 = (bf16[6,64,128]{2,1,0:T(8,128)(2,1)S(1)}, bf16[6,64,128]{2,1,0:T(8,128)(2,1)S(1)}, u32[]{:S(2)}, u32[]{:S(2)}) collective-permute-start(bf16[6,64,128]{2,1,0:T(8,128)(2,1)S(1)} %get-tuple-element.87), channel_id=1, source_target_pairs={{0,64},{1,7},{2,66},{3,5},{4,68},{5,3},{6,70},{7,1},{8,72},{9,15},... | collective-permute-start | bytes 294920 | tf_op jit(solution)/shard_map/ppermute | solution.py:261
  108.1 4.1 %collective-permute-start.31 = (bf16[8,64,128]{2,1,0:T(8,128)(2,1)S(1)}, bf16[8,64,128]{2,1,0:T(8,128)(2,1)S(1)}, u32[]{:S(2)}, u32[]{:S(2)}) collective-permute-start(bf16[8,64,128]{2,1,0:T(8,128)(2,1)S(1)} %get-tuple-element.86), channel_id=1, source_target_pairs={{0,8},{1,3},{2,10},{3,1},{4,12},{5,7},{6,14},{7,5},{8,0},{9,11},{1... | collective-permute-start | bytes 393224 | tf_op jit(solution)/shard_map/ppermute | solution.py:261
  108.1 5.7 %collective-permute-start.32 = (bf16[6,64,128]{2,1,0:T(8,128)(2,1)S(1)}, bf16[6,64,128]{2,1,0:T(8,128)(2,1)S(1)}, u32[]{:S(2)}, u32[]{:S(2)}) collective-permute-start(bf16[6,64,128]{2,1,0:T(8,128)(2,1)S(1)} %get-tuple-element.87), channel_id=1, source_target_pairs={{0,192},{1,5},{2,194},{3,7},{4,196},{5,1},{6,198},{7,3},{8,200},{9... | collective-permute-start | bytes 294920 | tf_op jit(solution)/shard_map/ppermute | solution.py:261
  113.9 3.0 %collective-permute-start.33 = (bf16[4,8,64,128]{3,2,1,0:T(8,128)(2,1)S(1)}, bf16[4,8,64,128]{3,2,1,0:T(8,128)(2,1)S(1)}, u32[]{:S(2)}, u32[]{:S(2)}) collective-permute-start(bf16[4,8,64,128]{3,2,1,0:T(8,128)(2,1)S(1)} %pad_maximum_fusion.1.own_ref), channel_id=1, source_target_pairs={{0,1},{1,0},{2,3},{3,2},{4,5},{5,4},{6,7},{7,6},{8,9},{9,8},{10,11... | collective-permute-start | bytes 1572872 | tf_op jit(solution)/shard_map/ppermute | solution.py:261
  (12 other events, 129.3 us)

commit v3 on v2

--- a/solution.py
+++ b/solution.py
@@ -43,34 +43,35 @@
     outer_ref[...] = rows_ref[FACE : 2 * FACE, :].astype(bf16)
 
 
-def faces_kernel(face_ref, place_ref, cur_ref, inner_ref, outer_ref, rows_ref):
+def faces_kernel(face_ref, place_ref, cur_ref, inner_ref, outer_ref, curb_ref, rows_ref):
+    curb_ref[...] = cur_ref[...].astype(bf16)
     gather_rows(cur_ref, face_ref, place_ref, rows_ref, inner_ref, outer_ref)
 
 
-def product_kernel(cols_ref, stiff_ref, cur_ref, applied_ref, out_ref, curb_ref):
+def product_kernel(cols_ref, stiff_ref, curb_ref, out_ref):
+    g = pl.program_id(0)
+    for ii in range(GROUP):
+        row = g * GROUP + ii
+        mats = jnp.concatenate([stiff_ref[row, j] for j in range(KNZ)], axis=1)
+        blocks = [pl.ds(pl.multiple_of(cols_ref[j, row] * BLK, BLK), BLK) for j in range(KNZ)]
+        picked = jnp.concatenate([curb_ref[block, :] for block in blocks], axis=0)
+        rows = pl.ds(pl.multiple_of(row * BLK, BLK), BLK)
+        out_ref[rows, :] = jnp.dot(mats, picked, preferred_element_type=f32)
+
+
+def partial_kernel(
+    last, cols_ref, face_ref, place_ref, inv_ref, applied_ref, prod_ref, inner_ref, outer_ref,
+    couple_ref, keep_ref, send_ref, *rest,
+):
+    if last:
+        out_ref, side_ref, acc_ref, res_ref = rest
+    else:
+        side_ref, acc_ref, res_ref = rest
     g = pl.program_id(0)
 
     @pl.when(g == 0)
     def _():
-        curb_ref[...] = cur_ref[...].astype(bf16).reshape(NB, BLK, BLK)
-
-    for ii in range(GROUP):
-        row = (g * GROUP + ii) * KNZ
-        mats = jnp.concatenate([stiff_ref[ii, j] for j in range(KNZ)], axis=1)
-        picked = jnp.concatenate([curb_ref[cols_ref[row + j]] for j in range(KNZ)], axis=0)
-        prod = jnp.dot(mats, picked, preferred_element_type=f32)
-        out_ref[ii * BLK : (ii + 1) * BLK, :] = applied_ref[ii * BLK : (ii + 1) * BLK, :] - prod
-
-
-def partial_kernel(
-    cols_ref, face_ref, place_ref, inv_ref, base_ref, inner_ref, outer_ref, couple_ref,
-    res_ref, keep_ref, send_ref, side_ref, acc_ref,
-):
-    g = pl.program_id(0)
-
-    @pl.when(g == 0)
-    def _():
-        res_ref[...] = base_ref[...]
+        res_ref[...] = applied_ref[...] - prod_ref[...]
         core = place_ref[0]
         inner = inner_ref[...]
         outer = jnp.where(place_ref[2] != 0, outer_ref[...], jnp.zeros_like(inner))
@@ -92,11 +93,14 @@
 
     for ii in range(GROUP):
         i = g * GROUP + ii
-        block = res_ref[pl.ds(pl.multiple_of(i * BLK, BLK), BLK), :].astype(bf16)
-        mats = jnp.concatenate([inv_ref[ii, j] for j in range(XNZ)], axis=1)
+        block = res_ref[pl.ds(pl.multiple_of(i * BLK, BLK), BLK), :]
+        if last:
+            out_ref[ii * BLK : (ii + 1) * BLK, :] = block
+        block = block.astype(bf16)
+        mats = jnp.concatenate([inv_ref[i, j] for j in range(XNZ)], axis=1)
         terms = jnp.dot(block.T, mats, preferred_element_type=f32)
         for j in range(XNZ):
-            acc_ref[cols_ref[i * XNZ + j]] += terms[:, j * BLK : (j + 1) * BLK]
+            acc_ref[cols_ref[j, i]] += terms[:, j * BLK : (j + 1) * BLK]
 
     @pl.when(g == NB // GROUP - 1)
     def _():
@@ -111,7 +115,7 @@
 
 def update_kernel(gather, cols_ref, face_ref, place_ref, inv_ref, own_ref, got_ref, cur_ref, *rest):
     if gather:
-        new_ref, low_ref, high_ref, coeff_ref, rows_ref = rest
+        new_ref, low_ref, high_ref, curb_ref, coeff_ref, rows_ref = rest
     else:
         new_ref, coeff_ref = rest
     g = pl.program_id(0)
@@ -137,11 +141,16 @@
 
     for ii in range(GROUP):
         i = g * GROUP + ii
-        mats = jnp.concatenate([inv_ref[ii, j] for j in range(XNZ)], axis=1)
-        picked = jnp.concatenate([coeff_ref[cols_ref[i * XNZ + j]] for j in range(XNZ)], axis=1)
+        mats = jnp.concatenate([inv_ref[i, j] for j in range(XNZ)], axis=1)
+        picked = jnp.concatenate([coeff_ref[cols_ref[j, i]] for j in range(XNZ)], axis=1)
         upd = lax.dot_general(mats, picked, (((1,), (1,)), ((), ())), preferred_element_type=f32)
         rows = pl.ds(pl.multiple_of(i * BLK, BLK), BLK)
-        new_ref[rows, :] = cur_ref[rows, :] + upd
+        new = cur_ref[rows, :] + upd
+        if gather:
+            new_ref[rows, :] = new
+            curb_ref[rows, :] = new.astype(bf16)
+        else:
+            new_ref[ii * BLK : (ii + 1) * BLK, :] = new
 
     if gather:
 
@@ -154,107 +163,81 @@
     return jax.ShapeDtypeStruct(shape, dtype)
 
 
-def whole(shape):
-    return pl.BlockSpec(shape, lambda g, *_: (0,) * len(shape))
+def resident(count):
+    return [pl.BlockSpec(memory_space=VMEM)] * count
 
 
 ROWS = NB * BLK
 STEPS = NB // GROUP
+FACES_COST = 60_000_000
 KEEP = (SLICES, LEVELS, PIECE, BLK)
 
 
+STEP_ROWS = pl.BlockSpec((GROUP * BLK, BLK), lambda g, *_: (g, 0))
+
+
+def call(kernel, name, steps, scalars, inputs, out_shape, out_specs, scratch, cost):
+    return pl.pallas_call(
+        kernel,
+        grid_spec=pltpu.PrefetchScalarGridSpec(
+            num_scalar_prefetch=len(scalars),
+            grid=(steps,),
+            in_specs=resident(len(inputs)),
+            out_specs=out_specs,
+            scratch_shapes=scratch,
+        ),
+        out_shape=out_shape,
+        cost_estimate=cost,
+        compiler_params=pltpu.CompilerParams(vmem_limit_bytes=LIMIT),
+        name=name,
+    )(*scalars, *inputs)
+
+
+def cost_of(blocks, moved):
+    return pl.CostEstimate(flops=2 * blocks * BLK**3, bytes_accessed=moved, transcendentals=0)
+
+
+FACE_OUTS = [sds((FACE, BLK), bf16)] * 2 + [sds((ROWS, BLK), bf16)]
+
+
 def faces_of(cur, faces, place):
-    return pl.pallas_call(
-        faces_kernel,
-        grid_spec=pltpu.PrefetchScalarGridSpec(
-            num_scalar_prefetch=2,
-            grid=(1,),
-            in_specs=[whole((ROWS, BLK))],
-            out_specs=[whole((FACE, BLK))] * 2,
-            scratch_shapes=[VMEM((2 * FACE, BLK), f32)],
-        ),
-        out_shape=[sds((FACE, BLK), bf16)] * 2,
-        compiler_params=pltpu.CompilerParams(vmem_limit_bytes=LIMIT),
-        name="faces",
-    )(faces, place, cur)
-
-
-def base_of(cur, applied, stiff, cols):
-    return pl.pallas_call(
-        product_kernel,
-        grid_spec=pltpu.PrefetchScalarGridSpec(
-            num_scalar_prefetch=1,
-            grid=(STEPS,),
-            in_specs=[
-                pl.BlockSpec((GROUP, KNZ, BLK, BLK), lambda g, *_: (g, 0, 0, 0)),
-                whole((ROWS, BLK)),
-                pl.BlockSpec((GROUP * BLK, BLK), lambda g, *_: (g, 0)),
-            ],
-            out_specs=pl.BlockSpec((GROUP * BLK, BLK), lambda g, *_: (g, 0)),
-            scratch_shapes=[VMEM((NB, BLK, BLK), bf16)],
-        ),
-        out_shape=sds((ROWS, BLK), f32),
-        cost_estimate=pl.CostEstimate(
-            flops=2 * NB * KNZ * BLK**3, bytes_accessed=8_000_000, transcendentals=0
-        ),
-        compiler_params=pltpu.CompilerParams(vmem_limit_bytes=LIMIT),
-        name="product",
-    )(cols, stiff, cur, applied)
-
-
-def partial_of(base, inner, outer, couple, inverse, cols, faces, place):
-    return pl.pallas_call(
-        partial_kernel,
-        grid_spec=pltpu.PrefetchScalarGridSpec(
-            num_scalar_prefetch=3,
-            grid=(STEPS,),
-            in_specs=[
-                pl.BlockSpec((GROUP, XNZ, BLK, BLK), lambda g, *_: (g, 0, 0, 0)),
-                whole((ROWS, BLK)),
-                whole((FACE, BLK)),
-                whole((FACE, BLK)),
-                whole((2, FACE, FACE)),
-            ],
-            out_specs=[whole((ROWS, BLK)), whole(KEEP), whole(KEEP)],
-            scratch_shapes=[VMEM((2 * FACE, BLK), f32), VMEM((NB, BLK, BLK), f32)],
-        ),
-        out_shape=[sds((ROWS, BLK), f32), sds(KEEP, f32), sds(KEEP, bf16)],
-        cost_estimate=pl.CostEstimate(
-            flops=2 * NB * XNZ * BLK**3, bytes_accessed=8_000_000, transcendentals=0
-        ),
-        compiler_params=pltpu.CompilerParams(vmem_limit_bytes=LIMIT),
-        name="partial",
-    )(cols, faces, place, inverse, base, inner, outer, couple)
+    return call(
+        faces_kernel, "faces", 1, (faces, place), (cur,), FACE_OUTS, resident(3),
+        [VMEM((2 * FACE, BLK), f32)], cost_of(0, FACES_COST),
+    )
+
+
+def product_of(curb, stiff, cols):
+    return call(
+        product_kernel, "product", STEPS, (cols,), (stiff, curb), [sds((ROWS, BLK), f32)],
+        resident(1), [], cost_of(NB * KNZ, 8_000_000),
+    )[0]
+
+
+def partial_of(applied, product, inner, outer, couple, inverse, cols, faces, place, last):
+    outs, specs = [sds(KEEP, f32), sds(KEEP, bf16)], resident(2)
+    if last:
+        outs.append(sds((ROWS, BLK), f32))
+        specs.append(STEP_ROWS)
+    return call(
+        functools.partial(partial_kernel, last), "partial", STEPS, (cols, faces, place),
+        (inverse, applied, product, inner, outer, couple), outs, specs,
+        [VMEM((2 * FACE, BLK), f32), VMEM((NB, BLK, BLK), f32), VMEM((ROWS, BLK), f32)],
+        cost_of(NB * XNZ, 8_000_000),
+    )
 
 
 def update_of(own, got, cur, inverse, cols, faces, place, gather):
     scratch = [VMEM((NB, BLK, BLK), bf16)]
-    outs, specs = [sds((ROWS, BLK), f32)], [whole((ROWS, BLK))]
+    outs, specs = [sds((ROWS, BLK), f32)], [STEP_ROWS]
     if gather:
         scratch.append(VMEM((2 * FACE, BLK), f32))
-        outs += [sds((FACE, BLK), bf16)] * 2
-        specs += [whole((FACE, BLK))] * 2
-    return pl.pallas_call(
-        functools.partial(update_kernel, gather),
-        grid_spec=pltpu.PrefetchScalarGridSpec(
-            num_scalar_prefetch=3,
-            grid=(STEPS,),
-            in_specs=[
-                pl.BlockSpec((GROUP, XNZ, BLK, BLK), lambda g, *_: (g, 0, 0, 0)),
-                whole(KEEP),
-                whole(KEEP),
-                whole((ROWS, BLK)),
-            ],
-            out_specs=specs,
-            scratch_shapes=scratch,
-        ),
-        out_shape=outs,
-        cost_estimate=pl.CostEstimate(
-            flops=2 * NB * XNZ * BLK**3, bytes_accessed=8_000_000, transcendentals=0
-        ),
-        compiler_params=pltpu.CompilerParams(vmem_limit_bytes=LIMIT),
-        name="update",
-    )(cols, faces, place, inverse, own, got, cur)
+        outs += FACE_OUTS
+        specs = resident(4)
+    return call(
+        functools.partial(update_kernel, gather), "update", STEPS, (cols, faces, place),
+        (inverse, own, got, cur), outs, specs, scratch, cost_of(NB * XNZ, 8_000_000),
+    )
 
 
 def moved(value, pairs):
@@ -361,30 +344,30 @@
     current = displacement[0, 0]
     applied = applied_loads[0, 0]
     stiff = stiff_blocks[0, 0]
-    stiff_cols = stiff_columns[0, 0].reshape(-1)
+    stiff_cols = stiff_columns[0, 0].T
     faces = face_rows[0, 0].reshape(-1)
     couple = coupling[0, 0]
     inverse = inverse_blocks[0, 0]
-    inverse_cols = inverse_columns[0, 0].reshape(-1)
+    inverse_cols = inverse_columns[0, 0].T
     spot = lax.axis_index("wide").astype(jnp.int32) % Z
     number = lax.axis_index("narrow").astype(jnp.int32)
     core, bit0, bit1 = number & 1, (number >> 1) & 1, (number >> 2) & 1
     inside = ((number > 0) & (number < lax.axis_size("narrow") - 1)).astype(jnp.int32)
     place = jnp.stack([core, (bit0 ^ bit1) * 2 + bit1, inside])
-    inner, outer = faces_of(current, faces, place)
+    inner, outer, rounded_current = faces_of(current, faces, place)
     for sweep in range(ITERS):
         inner, outer = faces_swapped(inner, outer)
-        base = base_of(current, applied, stiff, stiff_cols)
-        residual, keep, send = partial_of(
-            base, inner, outer, couple, inverse, inverse_cols, faces, place
+        product = product_of(rounded_current, stiff, stiff_cols)
+        last = sweep == ITERS - 1
+        keep, send, *residual = partial_of(
+            applied, product, inner, outer, couple, inverse, inverse_cols, faces, place, last
         )
         own, got = summed(keep, send, spot)
-        last = sweep == ITERS - 1
         outs = update_of(own, got, current, inverse, inverse_cols, faces, place, not last)
         current = outs[0]
         if not last:
-            inner, outer = outs[1:]
-    return (current[None, None], residual[None, None])
+            inner, outer, rounded_current = outs[1:]
+    return (current[None, None], residual[0][None, None])
 
 
 def solution(mesh):

time: 121 us -> 117 us (0.967)
  local copies, waits for them, and re-layouts: 8.61 us -> 5.23 us
    unnamed x30 -> x27, local copies, waits for them, and re-layouts: 8.32 us -> 5.11 us
  transfers between devices with their start and end apart: 34 -> 34, of which waited for: 21 -> 22; matrix products, arithmetic and copies ran while one was open for 2% -> 1% of each run, Pallas kernels for 4% -> 4%
where the time goes in v3:
time: 117 us; the launch traced here: 116 us
  starting transfers between devices  47.2 us (40%)
  waiting for transfers between devices  40 us (34%)
  Pallas kernels  21.5 us (18%)
  local copies, waits for them, and re-layouts  5.23 us (4%)
  other arithmetic  1.29 us (1%)
  between operations  1.23 us (1%)
    ppermute x30, starting transfers between devices, moved(): return lax.ppermute(value, ('wide', 'narrow'), pairs)  43.5 us
    ppermute x30, waiting for transfers between devices, moved(): return lax.ppermute(value, ('wide', 'narrow'), pairs)  38.7 us
    pallas_call x7, Pallas kernels, call(): pl.pallas_call(kernel, grid_spec=pltpu.PrefetchScalarGridSpec(num_scalar_...  21.5 us
    unnamed x27, local copies, waits for them, and re-layouts  5.11 us
    ppermute x2, starting transfers between devices, faces_swapped(): lax.ppermute(inner, 'narrow', [(i, i ^ 1) for i in range(count)])  3.51 us
  transfers between devices with their start and end apart: 34, of which 22 were waited for; matrix products, arithmetic and copies ran while one was open for 1% of the time, Pallas kernels for 4%

profile of v3, /device:TPU:1, one launch (start us, length us, event | category | flops | bytes accessed | tf_op | source)
XLA Modules:
  0.0 116.5 jit_solution(8211139023305451456)
XLA Ops:
  4.3 3.3 %collective-permute-start = (bf16[256,128]{1,0:T(8,128)(2,1)S(1)}, bf16[256,128]{1,0:T(8,128)(2,1)S(1)}, u32[]{:S(2)}, u32[]{:S(2)}) collective-permute-start(bf16[256,128]{1,0:T(8,128)(2,1)S(1)} %get-tuple-element.15), channel_id=1, source_target_pairs={{0,1},{1,0},{2,3},{3,2},{4,5},{5,4},{6,7},{7,6},{8,9},{9,8},{10,11... | collective-permute-start | bytes 196616 | tf_op jit(solution)/shard_map/ppermute | solution.py:277
  8.2 2.0 %copy-done.2 = bf16[1,1,16,7,128,128]{5,4,3,2,1,0:T(8,128)(2,1)S(1)} copy-done((bf16[1,1,16,7,128,128]{5,4,3,2,1,0:T(8,128)(2,1)S(1)}, bf16[1,1,16,7,128,128]{5,4,3,2,1,0:T(8,128)(2,1)}, u32[]{:S(2)}) %copy-start.2) | copy-done | bytes 3670040
  10.3 2.2 %product.2.prod_ref = f32[2048,128]{1,0:T(8,128)S(1)} custom-call(s32[7,16]{1,0:T(8,128)S(1)} %bitcast.116, bf16[16,7,128,128]{3,2,1,0:T(8,128)(2,1)S(1)} %bitcast.99, bf16[2048,128]{1,0:T(8,128)(2,1)S(1)} %get-tuple-element.14.curb_ref), custom_call_target="tpu_custom_call" | custom-call | flops 469762048 | bytes 8000000 | tf_op jit(solution)/shard_map/product/pallas_call | solution.py:180
  12.6 4.1 %partial.2 = (f32[4,8,64,128]{3,2,1,0:T(8,128)S(1)}, bf16[4,8,64,128]{3,2,1,0:T(8,128)(2,1)S(1)}) custom-call(s32[8,16]{1,0:T(8,128)S(1)} %bitcast.112, s32[512]{0:T(512)S(1)} %bitcast.108, s32[3]{0:T(128)S(1)} %pad_add_fusion.place_ref, bf16[16,8,128,128]{3,2,1,0:T(8,128)(2,1)S(1)} %bitcast.95, f32[2048,128]{1,0:T(8,128)S(1)} %bitcast.103, ...), custom_call_target="tpu_custom_call" | custom-call | flops 536870912 | bytes 8000000 | tf_op jit(solution)/shard_map/partial/pallas_call | solution.py:180
  19.6 1.9 %collective-permute-start.4 = (bf16[6,64,128]{2,1,0:T(8,128)(2,1)S(1)}, bf16[6,64,128]{2,1,0:T(8,128)(2,1)S(1)}, u32[]{:S(2)}, u32[]{:S(2)}) collective-permute-start(bf16[6,64,128]{2,1,0:T(8,128)(2,1)S(1)} %get-tuple-element.53), channel_id=1, source_target_pairs={{0,64},{1,7},{2,66},{3,5},{4,68},{5,3},{6,70},{7,1},{8,72},{9,15},... | collective-permute-start | bytes 294920 | tf_op jit(solution)/shard_map/ppermute | solution.py:244
  23.1 3.5 %collective-permute-done.3 = bf16[8,64,128]{2,1,0:T(8,128)(2,1)S(1)} collective-permute-done((bf16[8,64,128]{2,1,0:T(8,128)(2,1)S(1)}, bf16[8,64,128]{2,1,0:T(8,128)(2,1)S(1)}, u32[]{:S(2)}, u32[]{:S(2)}) %collective-permute-start.3) | collective-permute-done | bytes 131104 | tf_op jit(solution)/shard_map/ppermute | solution.py:244
  26.8 1.7 %collective-permute-start.6 = (bf16[5,64,128]{2,1,0:T(8,128)(2,1)S(1)}, bf16[5,64,128]{2,1,0:T(8,128)(2,1)S(1)}, u32[]{:S(2)}, u32[]{:S(2)}) collective-permute-start(bf16[5,64,128]{2,1,0:T(8,128)(2,1)S(1)} %slice.758), channel_id=1, source_target_pairs={{0,2},{1,9},{2,0},{3,11},{4,6},{5,13},{6,4},{7,15},{8,10},{9,17},{... | collective-permute-start | bytes 245768 | tf_op jit(solution)/shard_map/ppermute | solution.py:244
  28.5 4.0 %collective-permute-start.7 = (bf16[5,64,128]{2,1,0:T(8,128)(2,1)S(1)}, bf16[5,64,128]{2,1,0:T(8,128)(2,1)S(1)}, u32[]{:S(2)}, u32[]{:S(2)}) collective-permute-start(bf16[5,64,128]{2,1,0:T(8,128)(2,1)S(1)} %slice.758), channel_id=1, source_target_pairs={{0,6},{1,57},{2,4},{3,59},{4,2},{5,61},{6,0},{7,63},{8,14},{9,1},{... | collective-permute-start | bytes 245768 | tf_op jit(solution)/shard_map/ppermute | solution.py:244
  32.5 1.9 %collective-permute-done.6 = bf16[5,64,128]{2,1,0:T(8,128)(2,1)S(1)} collective-permute-done((bf16[5,64,128]{2,1,0:T(8,128)(2,1)S(1)}, bf16[5,64,128]{2,1,0:T(8,128)(2,1)S(1)}, u32[]{:S(2)}, u32[]{:S(2)}) %collective-permute-start.6) | collective-permute-done | bytes 81952 | tf_op jit(solution)/shard_map/ppermute | solution.py:244
  34.6 4.4 %collective-permute-start.9 = (bf16[4,64,128]{2,1,0:T(8,128)(2,1)S(1)}, bf16[4,64,128]{2,1,0:T(8,128)(2,1)S(1)}, u32[]{:S(2)}, u32[]{:S(2)}) collective-permute-start(bf16[4,64,128]{2,1,0:T(8,128)(2,1)S(1)} %pad_maximum_fusion.5), channel_id=1, source_target_pairs={{0,6},{1,25},{2,4},{3,27},{4,2},{5,29},{6,0},{7,31},{8,14},{9,33},... | collective-permute-start | bytes 196616 | tf_op jit(solution)/shard_map/ppermute | solution.py:244
  39.2 1.6 %collective-permute-done.9 = bf16[4,64,128]{2,1,0:T(8,128)(2,1)S(1)} collective-permute-done((bf16[4,64,128]{2,1,0:T(8,128)(2,1)S(1)}, bf16[4,64,128]{2,1,0:T(8,128)(2,1)S(1)}, u32[]{:S(2)}, u32[]{:S(2)}) %collective-permute-start.9) | collective-permute-done | bytes 65568 | tf_op jit(solution)/shard_map/ppermute | solution.py:244
  40.9 3.1 %collective-permute-done.8 = bf16[4,64,128]{2,1,0:T(8,128)(2,1)S(1)} collective-permute-done((bf16[4,64,128]{2,1,0:T(8,128)(2,1)S(1)}, bf16[4,64,128]{2,1,0:T(8,128)(2,1)S(1)}, u32[]{:S(2)}, u32[]{:S(2)}) %collective-permute-start.8) | collective-permute-done | bytes 65568 | tf_op jit(solution)/shard_map/ppermute | solution.py:244
  44.0 2.4 %collective-permute-start.12 = (bf16[1,64,128]{2,1,0:T(8,128)(2,1)S(1)}, bf16[1,64,128]{2,1,0:T(8,128)(2,1)S(1)}, u32[]{:S(2)}, u32[]{:S(2)}) collective-permute-start(bf16[1,64,128]{2,1,0:T(8,128)(2,1)S(1)} %slice.452), channel_id=1, source_target_pairs={{0,8},{1,129},{2,10},{3,131},{4,12},{5,133},{6,14},{7,135},{8,0},{... | collective-permute-start | bytes 49160 | tf_op jit(solution)/shard_map/ppermute | solution.py:244
  47.7 2.7 %collective-permute-done.10 = bf16[2,64,128]{2,1,0:T(8,128)(2,1)S(1)} collective-permute-done((bf16[2,64,128]{2,1,0:T(8,128)(2,1)S(1)}, bf16[2,64,128]{2,1,0:T(8,128)(2,1)S(1)}, u32[]{:S(2)}, u32[]{:S(2)}) %collective-permute-start.10) | collective-permute-done | bytes 32800 | tf_op jit(solution)/shard_map/ppermute | solution.py:244
  51.4 3.1 %collective-permute-start.15 = (bf16[6,64,128]{2,1,0:T(8,128)(2,1)S(1)}, bf16[6,64,128]{2,1,0:T(8,128)(2,1)S(1)}, u32[]{:S(2)}, u32[]{:S(2)}) collective-permute-start(bf16[6,64,128]{2,1,0:T(8,128)(2,1)S(1)} %get-tuple-element.99), channel_id=1, source_target_pairs={{0,192},{1,5},{2,194},{3,7},{4,196},{5,1},{6,198},{7,3},{8,200},{9... | collective-permute-start | bytes 294920 | tf_op jit(solution)/shard_map/ppermute | solution.py:244
  55.3 2.5 %collective-permute-done.15 = bf16[6,64,128]{2,1,0:T(8,128)(2,1)S(1)} collective-permute-done((bf16[6,64,128]{2,1,0:T(8,128)(2,1)S(1)}, bf16[6,64,128]{2,1,0:T(8,128)(2,1)S(1)}, u32[]{:S(2)}, u32[]{:S(2)}) %collective-permute-start.15) | collective-permute-done | bytes 98336 | tf_op jit(solution)/shard_map/ppermute | solution.py:244
  58.2 1.9 %collective-permute-done.16.got_ref = bf16[4,8,64,128]{3,2,1,0:T(8,128)(2,1)S(1)} collective-permute-done((bf16[4,8,64,128]{3,2,1,0:T(8,128)(2,1)S(1)}, bf16[4,8,64,128]{3,2,1,0:T(8,128)(2,1)S(1)}, u32[]{:S(2)}, u32[]{:S(2)}) %collective-permute-start.16) | collective-permute-done | bytes 524320 | tf_op jit(solution)/shard_map/ppermute | solution.py:244
  60.1 3.3 %update.2 = (f32[2048,128]{1,0:T(8,128)S(1)}, bf16[256,128]{1,0:T(8,128)(2,1)S(1)}, bf16[256,128]{1,0:T(8,128)(2,1)S(1)}, bf16[2048,128]{1,0:T(8,128)(2,1)S(1)}) custom-call(s32[8,16]{1,0:T(8,128)S(1)} %bitcast.113, s32[512]{0:T(512)S(1)} %bitcast.109, s32[3]{0:T(128)S(1)} %pad_add_fusion.place_ref, bf16[16,8,128,128]{3,2,1,0:T(8,128)(2,1)S(1)} %bitcast.96, ...), custom_call_target="tpu_custom_call" | custom-call | flops 536870912 | bytes 8000000 | tf_op jit(solution)/shard_map/update/pallas_call | solution.py:180
  63.8 2.2 %product.3.prod_ref = f32[2048,128]{1,0:T(8,128)S(1)} custom-call(s32[7,16]{1,0:T(8,128)S(1)} %bitcast.117, bf16[16,7,128,128]{3,2,1,0:T(8,128)(2,1)S(1)} %bitcast.100, bf16[2048,128]{1,0:T(8,128)(2,1)S(1)} %get-tuple-element.19.curb_ref), custom_call_target="tpu_custom_call" | custom-call | flops 469762048 | bytes 8000000 | tf_op jit(solution)/shard_map/product/pallas_call | solution.py:180
  67.3 4.9 %partial.3 = (f32[4,8,64,128]{3,2,1,0:T(8,128)S(1)}, bf16[4,8,64,128]{3,2,1,0:T(8,128)(2,1)S(1)}, f32[2048,128]{1,0:T(8,128)}) custom-call(s32[8,16]{1,0:T(8,128)S(1)} %bitcast.114, s32[512]{0:T(512)S(1)} %bitcast.110, s32[3]{0:T(128)S(1)} %pad_add_fusion.place_ref, bf16[16,8,128,128]{3,2,1,0:T(8,128)(2,1)S(1)} %bitcast.97, f32[2048,128]{1,0:T(8,128)S(1)} %bitcast.104, ...), custom_call_target="tpu_custom_call" | custom-call | flops 536870912 | bytes 8000000 | tf_op jit(solution)/shard_map/partial/pallas_call | solution.py:180
  76.3 2.6 %collective-permute-start.20 = (bf16[8,64,128]{2,1,0:T(8,128)(2,1)S(1)}, bf16[8,64,128]{2,1,0:T(8,128)(2,1)S(1)}, u32[]{:S(2)}, u32[]{:S(2)}) collective-permute-start(bf16[8,64,128]{2,1,0:T(8,128)(2,1)S(1)} %pad_maximum_fusion.3), channel_id=1, source_target_pairs={{0,8},{1,3},{2,10},{3,1},{4,12},{5,7},{6,14},{7,5},{8,0},{9,11},{1... | collective-permute-start | bytes 393224 | tf_op jit(solution)/shard_map/ppermute | solution.py:244
  79.0 3.2 %collective-permute-done.20 = bf16[8,64,128]{2,1,0:T(8,128)(2,1)S(1)} collective-permute-done((bf16[8,64,128]{2,1,0:T(8,128)(2,1)S(1)}, bf16[8,64,128]{2,1,0:T(8,128)(2,1)S(1)}, u32[]{:S(2)}, u32[]{:S(2)}) %collective-permute-start.20) | collective-permute-done | bytes 131104 | tf_op jit(solution)/shard_map/ppermute | solution.py:244
  82.4 3.2 %collective-permute-start.23 = (bf16[5,64,128]{2,1,0:T(8,128)(2,1)S(1)}, bf16[5,64,128]{2,1,0:T(8,128)(2,1)S(1)}, u32[]{:S(2)}, u32[]{:S(2)}) collective-permute-start(bf16[5,64,128]{2,1,0:T(8,128)(2,1)S(1)} %slice.757), channel_id=1, source_target_pairs={{0,2},{1,9},{2,0},{3,11},{4,6},{5,13},{6,4},{7,15},{8,10},{9,17},{... | collective-permute-start | bytes 245768 | tf_op jit(solution)/shard_map/ppermute | solution.py:244
  87.1 2.1 %collective-permute-done.24 = bf16[5,64,128]{2,1,0:T(8,128)(2,1)S(1)} collective-permute-done((bf16[5,64,128]{2,1,0:T(8,128)(2,1)S(1)}, bf16[5,64,128]{2,1,0:T(8,128)(2,1)S(1)}, u32[]{:S(2)}, u32[]{:S(2)}) %collective-permute-start.24) | collective-permute-done | bytes 81952 | tf_op jit(solution)/shard_map/ppermute | solution.py:244
  89.2 2.5 %collective-permute-start.26 = (bf16[4,64,128]{2,1,0:T(8,128)(2,1)S(1)}, bf16[4,64,128]{2,1,0:T(8,128)(2,1)S(1)}, u32[]{:S(2)}, u32[]{:S(2)}) collective-permute-start(bf16[4,64,128]{2,1,0:T(8,128)(2,1)S(1)} %pad_maximum_fusion.7), channel_id=1, source_target_pairs={{0,6},{1,25},{2,4},{3,27},{4,2},{5,29},{6,0},{7,31},{8,14},{9,33},... | collective-permute-start | bytes 196616 | tf_op jit(solution)/shard_map/ppermute | solution.py:244
  91.7 2.1 %collective-permute-start.25 = (bf16[4,64,128]{2,1,0:T(8,128)(2,1)S(1)}, bf16[4,64,128]{2,1,0:T(8,128)(2,1)S(1)}, u32[]{:S(2)}, u32[]{:S(2)}) collective-permute-start(bf16[4,64,128]{2,1,0:T(8,128)(2,1)S(1)} %pad_maximum_fusion.6), channel_id=1, source_target_pairs={{0,2},{1,41},{2,0},{3,43},{4,6},{5,45},{6,4},{7,47},{8,10},{9,49},... | collective-permute-start | bytes 196616 | tf_op jit(solution)/shard_map/ppermute | solution.py:244
  93.9 2.5 %collective-permute-done.26 = bf16[4,64,128]{2,1,0:T(8,128)(2,1)S(1)} collective-permute-done((bf16[4,64,128]{2,1,0:T(8,128)(2,1)S(1)}, bf16[4,64,128]{2,1,0:T(8,128)(2,1)S(1)}, u32[]{:S(2)}, u32[]{:S(2)}) %collective-permute-start.26) | collective-permute-done | bytes 65568 | tf_op jit(solution)/shard_map/ppermute | solution.py:244
  96.8 2.0 %collective-permute-start.29 = (bf16[1,64,128]{2,1,0:T(8,128)(2,1)S(1)}, bf16[1,64,128]{2,1,0:T(8,128)(2,1)S(1)}, u32[]{:S(2)}, u32[]{:S(2)}) collective-permute-start(bf16[1,64,128]{2,1,0:T(8,128)(2,1)S(1)} %slice.493), channel_id=1, source_target_pairs={{0,8},{1,129},{2,10},{3,131},{4,12},{5,133},{6,14},{7,135},{8,0},{... | collective-permute-start | bytes 49160 | tf_op jit(solution)/shard_map/ppermute | solution.py:244
  99.6 2.8 %collective-permute-done.27 = bf16[2,64,128]{2,1,0:T(8,128)(2,1)S(1)} collective-permute-done((bf16[2,64,128]{2,1,0:T(8,128)(2,1)S(1)}, bf16[2,64,128]{2,1,0:T(8,128)(2,1)S(1)}, u32[]{:S(2)}, u32[]{:S(2)}) %collective-permute-start.27) | collective-permute-done | bytes 32800 | tf_op jit(solution)/shard_map/ppermute | solution.py:244
  104.2 2.6 %collective-permute-start.32 = (bf16[6,64,128]{2,1,0:T(8,128)(2,1)S(1)}, bf16[6,64,128]{2,1,0:T(8,128)(2,1)S(1)}, u32[]{:S(2)}, u32[]{:S(2)}) collective-permute-start(bf16[6,64,128]{2,1,0:T(8,128)(2,1)S(1)} %get-tuple-element.91), channel_id=1, source_target_pairs={{0,192},{1,5},{2,194},{3,7},{4,196},{5,1},{6,198},{7,3},{8,200},{9... | collective-permute-start | bytes 294920 | tf_op jit(solution)/shard_map/ppermute | solution.py:244
  108.3 1.8 %collective-permute-done.32 = bf16[6,64,128]{2,1,0:T(8,128)(2,1)S(1)} collective-permute-done((bf16[6,64,128]{2,1,0:T(8,128)(2,1)S(1)}, bf16[6,64,128]{2,1,0:T(8,128)(2,1)S(1)}, u32[]{:S(2)}, u32[]{:S(2)}) %collective-permute-start.32) | collective-permute-done | bytes 98336 | tf_op jit(solution)/shard_map/ppermute | solution.py:244
  113.0 3.5 %update.3 = f32[2048,128]{1,0:T(8,128)} custom-call(s32[8,16]{1,0:T(8,128)S(1)} %bitcast.115, s32[512]{0:T(512)S(1)} %bitcast.111, s32[3]{0:T(128)S(1)} %pad_add_fusion.place_ref, bf16[16,8,128,128]{3,2,1,0:T(8,128)(2,1)S(1)} %bitcast.98, bf16[4,8,64,128]{3,2,1,0:T(8,128)(2,1)S(1)} %pad_maximum_fusion.1.own_ref, ...), custom_call_target="tpu_custom_call" | custom-call | flops 536870912 | bytes 8000000 | tf_op jit(solution)/shard_map/update/pallas_call | solution.py:180
  (141 shorter events, 27.4 us)
Async XLA Ops:
  4.3 8.3 %collective-permute-start = (bf16[256,128]{1,0:T(8,128)(2,1)S(1)}, bf16[256,128]{1,0:T(8,128)(2,1)S(1)}, u32[]{:S(2)}, u32[]{:S(2)}) collective-permute-start(bf16[256,128]{1,0:T(8,128)(2,1)S(1)} %get-tuple-element.15), channel_id=1, source_target_pairs={{0,1},{1,0},{2,3},{3,2},{4,5},{5,4},{6,7},{7,6},{8,9},{9,8},{10,11... | collective-permute-start | bytes 196616 | tf_op jit(solution)/shard_map/ppermute | solution.py:277
  7.5 5.0 %collective-permute-start.1 = (bf16[256,128]{1,0:T(8,128)(2,1)S(1)}, bf16[256,128]{1,0:T(8,128)(2,1)S(1)}, u32[]{:S(2)}, u32[]{:S(2)}) collective-permute-start(bf16[256,128]{1,0:T(8,128)(2,1)S(1)} %get-tuple-element.16), channel_id=1, source_target_pairs={{0,7},{1,2},{2,1},{3,4},{4,3},{5,6},{6,5},{7,0},{8,15},{9,10},{10,... | collective-permute-start | bytes 196616 | tf_op jit(solution)/shard_map/ppermute | solution.py:278
  16.7 2.8 %collective-permute-start.2 = (bf16[4,8,64,128]{3,2,1,0:T(8,128)(2,1)S(1)}, bf16[4,8,64,128]{3,2,1,0:T(8,128)(2,1)S(1)}, u32[]{:S(2)}, u32[]{:S(2)}) collective-permute-start(bf16[4,8,64,128]{3,2,1,0:T(8,128)(2,1)S(1)} %get-tuple-element.18), channel_id=1, source_target_pairs={{0,1},{1,0},{2,3},{3,2},{4,5},{5,4},{6,7},{7,6},{8,9},{9,8},{10,11... | collective-permute-start | bytes 1572872 | tf_op jit(solution)/shard_map/ppermute | solution.py:244
  19.6 7.1 %collective-permute-start.4 = (bf16[6,64,128]{2,1,0:T(8,128)(2,1)S(1)}, bf16[6,64,128]{2,1,0:T(8,128)(2,1)S(1)}, u32[]{:S(2)}, u32[]{:S(2)}) collective-permute-start(bf16[6,64,128]{2,1,0:T(8,128)(2,1)S(1)} %get-tuple-element.53), channel_id=1, source_target_pairs={{0,64},{1,7},{2,66},{3,5},{4,68},{5,3},{6,70},{7,1},{8,72},{9,15},... | collective-permute-start | bytes 294920 | tf_op jit(solution)/shard_map/ppermute | solution.py:244
  21.5 5.1 %collective-permute-start.5 = (bf16[6,64,128]{2,1,0:T(8,128)(2,1)S(1)}, bf16[6,64,128]{2,1,0:T(8,128)(2,1)S(1)}, u32[]{:S(2)}, u32[]{:S(2)}) collective-permute-start(bf16[6,64,128]{2,1,0:T(8,128)(2,1)S(1)} %get-tuple-element.55), channel_id=1, source_target_pairs={{0,192},{1,5},{2,194},{3,7},{4,196},{5,1},{6,198},{7,3},{8,200},{9... | collective-permute-start | bytes 294920 | tf_op jit(solution)/shard_map/ppermute | solution.py:244
  22.2 4.4 %collective-permute-start.3 = (bf16[8,64,128]{2,1,0:T(8,128)(2,1)S(1)}, bf16[8,64,128]{2,1,0:T(8,128)(2,1)S(1)}, u32[]{:S(2)}, u32[]{:S(2)}) collective-permute-start(bf16[8,64,128]{2,1,0:T(8,128)(2,1)S(1)} %pad_maximum_fusion.2), channel_id=1, source_target_pairs={{0,8},{1,3},{2,10},{3,1},{4,12},{5,7},{6,14},{7,5},{8,0},{9,11},{1... | collective-permute-start | bytes 393224 | tf_op jit(solution)/shard_map/ppermute | solution.py:244
  26.8 7.7 %collective-permute-start.6 = (bf16[5,64,128]{2,1,0:T(8,128)(2,1)S(1)}, bf16[5,64,128]{2,1,0:T(8,128)(2,1)S(1)}, u32[]{:S(2)}, u32[]{:S(2)}) collective-permute-start(bf16[5,64,128]{2,1,0:T(8,128)(2,1)S(1)} %slice.758), channel_id=1, source_target_pairs={{0,2},{1,9},{2,0},{3,11},{4,6},{5,13},{6,4},{7,15},{8,10},{9,17},{... | collective-permute-start | bytes 245768 | tf_op jit(solution)/shard_map/ppermute | solution.py:244
  28.5 6.0 %collective-permute-start.7 = (bf16[5,64,128]{2,1,0:T(8,128)(2,1)S(1)}, bf16[5,64,128]{2,1,0:T(8,128)(2,1)S(1)}, u32[]{:S(2)}, u32[]{:S(2)}) collective-permute-start(bf16[5,64,128]{2,1,0:T(8,128)(2,1)S(1)} %slice.758), channel_id=1, source_target_pairs={{0,6},{1,57},{2,4},{3,59},{4,2},{5,61},{6,0},{7,63},{8,14},{9,1},{... | collective-permute-start | bytes 245768 | tf_op jit(solution)/shard_map/ppermute | solution.py:244
  34.6 6.3 %collective-permute-start.9 = (bf16[4,64,128]{2,1,0:T(8,128)(2,1)S(1)}, bf16[4,64,128]{2,1,0:T(8,128)(2,1)S(1)}, u32[]{:S(2)}, u32[]{:S(2)}) collective-permute-start(bf16[4,64,128]{2,1,0:T(8,128)(2,1)S(1)} %pad_maximum_fusion.5), channel_id=1, source_target_pairs={{0,6},{1,25},{2,4},{3,27},{4,2},{5,29},{6,0},{7,31},{8,14},{9,33},... | collective-permute-start | bytes 196616 | tf_op jit(solution)/shard_map/ppermute | solution.py:244
  39.0 5.0 %collective-permute-start.8 = (bf16[4,64,128]{2,1,0:T(8,128)(2,1)S(1)}, bf16[4,64,128]{2,1,0:T(8,128)(2,1)S(1)}, u32[]{:S(2)}, u32[]{:S(2)}) collective-permute-start(bf16[4,64,128]{2,1,0:T(8,128)(2,1)S(1)} %pad_maximum_fusion.4), channel_id=1, source_target_pairs={{0,2},{1,41},{2,0},{3,43},{4,6},{5,45},{6,4},{7,47},{8,10},{9,49},... | collective-permute-start | bytes 196616 | tf_op jit(solution)/shard_map/ppermute | solution.py:244
  44.0 6.4 %collective-permute-start.12 = (bf16[1,64,128]{2,1,0:T(8,128)(2,1)S(1)}, bf16[1,64,128]{2,1,0:T(8,128)(2,1)S(1)}, u32[]{:S(2)}, u32[]{:S(2)}) collective-permute-start(bf16[1,64,128]{2,1,0:T(8,128)(2,1)S(1)} %slice.452), channel_id=1, source_target_pairs={{0,8},{1,129},{2,10},{3,131},{4,12},{5,133},{6,14},{7,135},{8,0},{... | collective-permute-start | bytes 49160 | tf_op jit(solution)/shard_map/ppermute | solution.py:244
  46.5 4.0 %collective-permute-start.11 = (bf16[1,64,128]{2,1,0:T(8,128)(2,1)S(1)}, bf16[1,64,128]{2,1,0:T(8,128)(2,1)S(1)}, u32[]{:S(2)}, u32[]{:S(2)}) collective-permute-start(bf16[1,64,128]{2,1,0:T(8,128)(2,1)S(1)} %slice.452), channel_id=1, source_target_pairs={{0,6},{1,193},{2,4},{3,195},{4,2},{5,197},{6,0},{7,199},{8,14},{9,... | collective-permute-start | bytes 49160 | tf_op jit(solution)/shard_map/ppermute | solution.py:244
  47.6 2.8 %collective-permute-start.10 = (bf16[2,64,128]{2,1,0:T(8,128)(2,1)S(1)}, bf16[2,64,128]{2,1,0:T(8,128)(2,1)S(1)}, u32[]{:S(2)}, u32[]{:S(2)}) collective-permute-start(bf16[2,64,128]{2,1,0:T(8,128)(2,1)S(1)} %slice.448), channel_id=1, source_target_pairs={{0,2},{1,65},{2,0},{3,67},{4,6},{5,69},{6,4},{7,71},{8,10},{9,73},... | collective-permute-start | bytes 98312 | tf_op jit(solution)/shard_map/ppermute | solution.py:244
  50.5 4.8 %collective-permute-start.13 = (bf16[6,64,128]{2,1,0:T(8,128)(2,1)S(1)}, bf16[6,64,128]{2,1,0:T(8,128)(2,1)S(1)}, u32[]{:S(2)}, u32[]{:S(2)}) collective-permute-start(bf16[6,64,128]{2,1,0:T(8,128)(2,1)S(1)} %get-tuple-element.99), channel_id=1, source_target_pairs={{0,64},{1,7},{2,66},{3,5},{4,68},{5,3},{6,70},{7,1},{8,72},{9,15},... | collective-permute-start | bytes 294920 | tf_op jit(solution)/shard_map/ppermute | solution.py:244
  51.3 3.9 %collective-permute-start.14 = (bf16[8,64,128]{2,1,0:T(8,128)(2,1)S(1)}, bf16[8,64,128]{2,1,0:T(8,128)(2,1)S(1)}, u32[]{:S(2)}, u32[]{:S(2)}) collective-permute-start(bf16[8,64,128]{2,1,0:T(8,128)(2,1)S(1)} %get-tuple-element.98), channel_id=1, source_target_pairs={{0,8},{1,3},{2,10},{3,1},{4,12},{5,7},{6,14},{7,5},{8,0},{9,11},{1... | collective-permute-start | bytes 393224 | tf_op jit(solution)/shard_map/ppermute | solution.py:244
  51.4 6.5 %collective-permute-start.15 = (bf16[6,64,128]{2,1,0:T(8,128)(2,1)S(1)}, bf16[6,64,128]{2,1,0:T(8,128)(2,1)S(1)}, u32[]{:S(2)}, u32[]{:S(2)}) collective-permute-start(bf16[6,64,128]{2,1,0:T(8,128)(2,1)S(1)} %get-tuple-element.99), channel_id=1, source_target_pairs={{0,192},{1,5},{2,194},{3,7},{4,196},{5,1},{6,198},{7,3},{8,200},{9... | collective-permute-start | bytes 294920 | tf_op jit(solution)/shard_map/ppermute | solution.py:244
  63.6 3.7 %collective-permute-start.18 = (bf16[256,128]{1,0:T(8,128)(2,1)S(1)}, bf16[256,128]{1,0:T(8,128)(2,1)S(1)}, u32[]{:S(2)}, u32[]{:S(2)}) collective-permute-start(bf16[256,128]{1,0:T(8,128)(2,1)S(1)} %get-tuple-element.21), channel_id=1, source_target_pairs={{0,7},{1,2},{2,1},{3,4},{4,3},{5,6},{6,5},{7,0},{8,15},{9,10},{10,... | collective-permute-start | bytes 196616 | tf_op jit(solution)/shard_map/ppermute | solution.py:278
  72.3 3.1 %collective-permute-start.19 = (bf16[4,8,64,128]{3,2,1,0:T(8,128)(2,1)S(1)}, bf16[4,8,64,128]{3,2,1,0:T(8,128)(2,1)S(1)}, u32[]{:S(2)}, u32[]{:S(2)}) collective-permute-start(bf16[4,8,64,128]{3,2,1,0:T(8,128)(2,1)S(1)} %get-tuple-element.23), channel_id=1, source_target_pairs={{0,1},{1,0},{2,3},{3,2},{4,5},{5,4},{6,7},{7,6},{8,9},{9,8},{10,11... | collective-permute-start | bytes 1572872 | tf_op jit(solution)/shard_map/ppermute | solution.py:244
  75.5 6.8 %collective-permute-start.21 = (bf16[6,64,128]{2,1,0:T(8,128)(2,1)S(1)}, bf16[6,64,128]{2,1,0:T(8,128)(2,1)S(1)}, u32[]{:S(2)}, u32[]{:S(2)}) collective-permute-start(bf16[6,64,128]{2,1,0:T(8,128)(2,1)S(1)} %get-tuple-element.50), channel_id=1, source_target_pairs={{0,64},{1,7},{2,66},{3,5},{4,68},{5,3},{6,70},{7,1},{8,72},{9,15},... | collective-permute-start | bytes 294920 | tf_op jit(solution)/shard_map/ppermute | solution.py:244
  76.3 6.0 %collective-permute-start.22 = (bf16[6,64,128]{2,1,0:T(8,128)(2,1)S(1)}, bf16[6,64,128]{2,1,0:T(8,128)(2,1)S(1)}, u32[]{:S(2)}, u32[]{:S(2)}) collective-permute-start(bf16[6,64,128]{2,1,0:T(8,128)(2,1)S(1)} %get-tuple-element.51), channel_id=1, source_target_pairs={{0,192},{1,5},{2,194},{3,7},{4,196},{5,1},{6,198},{7,3},{8,200},{9... | collective-permute-start | bytes 294920 | tf_op jit(solution)/shard_map/ppermute | solution.py:244
  76.3 5.9 %collective-permute-start.20 = (bf16[8,64,128]{2,1,0:T(8,128)(2,1)S(1)}, bf16[8,64,128]{2,1,0:T(8,128)(2,1)S(1)}, u32[]{:S(2)}, u32[]{:S(2)}) collective-permute-start(bf16[8,64,128]{2,1,0:T(8,128)(2,1)S(1)} %pad_maximum_fusion.3), channel_id=1, source_target_pairs={{0,8},{1,3},{2,10},{3,1},{4,12},{5,7},{6,14},{7,5},{8,0},{9,11},{1... | collective-permute-start | bytes 393224 | tf_op jit(solution)/shard_map/ppermute | solution.py:244
  82.4 4.7 %collective-permute-start.23 = (bf16[5,64,128]{2,1,0:T(8,128)(2,1)S(1)}, bf16[5,64,128]{2,1,0:T(8,128)(2,1)S(1)}, u32[]{:S(2)}, u32[]{:S(2)}) collective-permute-start(bf16[5,64,128]{2,1,0:T(8,128)(2,1)S(1)} %slice.757), channel_id=1, source_target_pairs={{0,2},{1,9},{2,0},{3,11},{4,6},{5,13},{6,4},{7,15},{8,10},{9,17},{... | collective-permute-start | bytes 245768 | tf_op jit(solution)/shard_map/ppermute | solution.py:244
  85.6 3.6 %collective-permute-start.24 = (bf16[5,64,128]{2,1,0:T(8,128)(2,1)S(1)}, bf16[5,64,128]{2,1,0:T(8,128)(2,1)S(1)}, u32[]{:S(2)}, u32[]{:S(2)}) collective-permute-start(bf16[5,64,128]{2,1,0:T(8,128)(2,1)S(1)} %slice.757), channel_id=1, source_target_pairs={{0,6},{1,57},{2,4},{3,59},{4,2},{5,61},{6,0},{7,63},{8,14},{9,1},{... | collective-permute-start | bytes 245768 | tf_op jit(solution)/shard_map/ppermute | solution.py:244
  89.2 7.1 %collective-permute-start.26 = (bf16[4,64,128]{2,1,0:T(8,128)(2,1)S(1)}, bf16[4,64,128]{2,1,0:T(8,128)(2,1)S(1)}, u32[]{:S(2)}, u32[]{:S(2)}) collective-permute-start(bf16[4,64,128]{2,1,0:T(8,128)(2,1)S(1)} %pad_maximum_fusion.7), channel_id=1, source_target_pairs={{0,6},{1,25},{2,4},{3,27},{4,2},{5,29},{6,0},{7,31},{8,14},{9,33},... | collective-permute-start | bytes 196616 | tf_op jit(solution)/shard_map/ppermute | solution.py:244
  91.7 5.0 %collective-permute-start.25 = (bf16[4,64,128]{2,1,0:T(8,128)(2,1)S(1)}, bf16[4,64,128]{2,1,0:T(8,128)(2,1)S(1)}, u32[]{:S(2)}, u32[]{:S(2)}) collective-permute-start(bf16[4,64,128]{2,1,0:T(8,128)(2,1)S(1)} %pad_maximum_fusion.6), channel_id=1, source_target_pairs={{0,2},{1,41},{2,0},{3,43},{4,6},{5,45},{6,4},{7,47},{8,10},{9,49},... | collective-permute-start | bytes 196616 | tf_op jit(solution)/shard_map/ppermute | solution.py:244
  96.8 5.6 %collective-permute-start.29 = (bf16[1,64,128]{2,1,0:T(8,128)(2,1)S(1)}, bf16[1,64,128]{2,1,0:T(8,128)(2,1)S(1)}, u32[]{:S(2)}, u32[]{:S(2)}) collective-permute-start(bf16[1,64,128]{2,1,0:T(8,128)(2,1)S(1)} %slice.493), channel_id=1, source_target_pairs={{0,8},{1,129},{2,10},{3,131},{4,12},{5,133},{6,14},{7,135},{8,0},{... | collective-permute-start | bytes 49160 | tf_op jit(solution)/shard_map/ppermute | solution.py:244
  98.8 3.9 %collective-permute-start.28 = (bf16[1,64,128]{2,1,0:T(8,128)(2,1)S(1)}, bf16[1,64,128]{2,1,0:T(8,128)(2,1)S(1)}, u32[]{:S(2)}, u32[]{:S(2)}) collective-permute-start(bf16[1,64,128]{2,1,0:T(8,128)(2,1)S(1)} %slice.493), channel_id=1, source_target_pairs={{0,6},{1,193},{2,4},{3,195},{4,2},{5,197},{6,0},{7,199},{8,14},{9,... | collective-permute-start | bytes 49160 | tf_op jit(solution)/shard_map/ppermute | solution.py:244
  99.3 3.1 %collective-permute-start.27 = (bf16[2,64,128]{2,1,0:T(8,128)(2,1)S(1)}, bf16[2,64,128]{2,1,0:T(8,128)(2,1)S(1)}, u32[]{:S(2)}, u32[]{:S(2)}) collective-permute-start(bf16[2,64,128]{2,1,0:T(8,128)(2,1)S(1)} %slice.489), channel_id=1, source_target_pairs={{0,2},{1,65},{2,0},{3,67},{4,6},{5,69},{6,4},{7,71},{8,10},{9,73},... | collective-permute-start | bytes 98312 | tf_op jit(solution)/shard_map/ppermute | solution.py:244
  102.8 4.8 %collective-permute-start.30 = (bf16[6,64,128]{2,1,0:T(8,128)(2,1)S(1)}, bf16[6,64,128]{2,1,0:T(8,128)(2,1)S(1)}, u32[]{:S(2)}, u32[]{:S(2)}) collective-permute-start(bf16[6,64,128]{2,1,0:T(8,128)(2,1)S(1)} %get-tuple-element.91), channel_id=1, source_target_pairs={{0,64},{1,7},{2,66},{3,5},{4,68},{5,3},{6,70},{7,1},{8,72},{9,15},... | collective-permute-start | bytes 294920 | tf_op jit(solution)/shard_map/ppermute | solution.py:244
  104.1 4.1 %collective-permute-start.31 = (bf16[8,64,128]{2,1,0:T(8,128)(2,1)S(1)}, bf16[8,64,128]{2,1,0:T(8,128)(2,1)S(1)}, u32[]{:S(2)}, u32[]{:S(2)}) collective-permute-start(bf16[8,64,128]{2,1,0:T(8,128)(2,1)S(1)} %get-tuple-element.90), channel_id=1, source_target_pairs={{0,8},{1,3},{2,10},{3,1},{4,12},{5,7},{6,14},{7,5},{8,0},{9,11},{1... | collective-permute-start | bytes 393224 | tf_op jit(solution)/shard_map/ppermute | solution.py:244
  104.2 6.0 %collective-permute-start.32 = (bf16[6,64,128]{2,1,0:T(8,128)(2,1)S(1)}, bf16[6,64,128]{2,1,0:T(8,128)(2,1)S(1)}, u32[]{:S(2)}, u32[]{:S(2)}) collective-permute-start(bf16[6,64,128]{2,1,0:T(8,128)(2,1)S(1)} %get-tuple-element.91), channel_id=1, source_target_pairs={{0,192},{1,5},{2,194},{3,7},{4,196},{5,1},{6,198},{7,3},{8,200},{9... | collective-permute-start | bytes 294920 | tf_op jit(solution)/shard_map/ppermute | solution.py:244
  110.2 2.7 %collective-permute-start.33 = (bf16[4,8,64,128]{3,2,1,0:T(8,128)(2,1)S(1)}, bf16[4,8,64,128]{3,2,1,0:T(8,128)(2,1)S(1)}, u32[]{:S(2)}, u32[]{:S(2)}) collective-permute-start(bf16[4,8,64,128]{3,2,1,0:T(8,128)(2,1)S(1)} %pad_maximum_fusion.1.own_ref), channel_id=1, source_target_pairs={{0,1},{1,0},{2,3},{3,2},{4,5},{5,4},{6,7},{7,6},{8,9},{9,8},{10,11... | collective-permute-start | bytes 1572872 | tf_op jit(solution)/shard_map/ppermute | solution.py:244
  (11 other events, 126.4 us)

commit v4 on v3

--- a/solution.py
+++ b/solution.py
@@ -18,7 +18,6 @@
 SLICES = 4
 HALF = BLK // SLICES
 PIECE = 2 * HALF
-Z = 8
 
 LIMIT = 20 * 2**20
 
@@ -258,12 +257,9 @@
     return lambda w, n: (w ^ wide_mask, n ^ narrow_mask)
 
 
-def along_z(steps):
-    return lambda w, n: (w - w % Z + (w + steps) % Z, n)
-
-
 X1, X2, X3 = masked(0, 2), masked(0, 4), masked(0, 6)
-Z1, Y1, Y2, Y3 = masked(1, 0), masked(8, 0), masked(16, 0), masked(24, 0)
+Y1, Y2, Y3 = masked(8, 0), masked(16, 0), masked(24, 0)
+Z1, Z2, Z6, Z5 = masked(1, 0), masked(2, 0), masked(6, 0), masked(5, 0)
 
 
 def handed(value):
@@ -283,7 +279,7 @@
     return (total * f32(2.0 ** (-level / 2))).astype(bf16)
 
 
-def summed(keep, send, spot):
+def summed(keep, send):
     got = handed(send)
 
     def pair(slices, levels):
@@ -299,23 +295,16 @@
     total = pair(0, upper) + near[2:] + across + far
     done3 = rounded(total[:1], 3)
 
-    own = total[1:]
-    wire = own.astype(bf16)
-    left = sent(wire, along_z(1), X1)
-    right = sent(wire, along_z(-1), X3)
-    done4 = rounded(own[:1] + jnp.where(spot % 2 == 1, left[:1], right[:1]), 4)
-    first, last = spot % 4 == 0, spot % 4 == 3
-    own, left, right = own[1:], left[1:], right[1:]
-    zero = jnp.zeros_like(own[:1])
-    quad = own[:1]
-    window = left[1:] + own[1:] + right[1:]
-    down = jnp.concatenate([left[:1] + jnp.where(last, quad, zero), window], axis=0)
-    up = jnp.concatenate([right[:1] + jnp.where(first, quad, zero), own[1:] + right[1:]], axis=0)
-    above = sent(down.astype(bf16), along_z(-3), X1)
-    below = sent(up.astype(bf16), along_z(3), X3)
-    quad = quad + jnp.where(first, zero, left[:1]) + jnp.where(last, zero, right[:1])
-    done5 = rounded(quad + jnp.where(spot % 4 < 2, above[:1], below[:1]), 5)
-    total = window + above[1:] + below[1:]
+    total = total[1:]
+    total = total + sent(total.astype(bf16), Z1, X1)
+    done4 = rounded(total[:1], 4)
+    wire = total[1:].astype(bf16)
+    near = sent(wire, Z2, X1)
+    across = sent(wire[1:], Z6, X3)
+    far = sent(wire[1:], Z5, Y1)
+    total = total[1:] + near
+    done5 = rounded(total[:1], 5)
+    total = total[1:] + across + far
     done6 = rounded(total[:1], 6)
 
     own = total[1:]
@@ -349,7 +338,6 @@
     couple = coupling[0, 0]
     inverse = inverse_blocks[0, 0]
     inverse_cols = inverse_columns[0, 0].T
-    spot = lax.axis_index("wide").astype(jnp.int32) % Z
     number = lax.axis_index("narrow").astype(jnp.int32)
     core, bit0, bit1 = number & 1, (number >> 1) & 1, (number >> 2) & 1
     inside = ((number > 0) & (number < lax.axis_size("narrow") - 1)).astype(jnp.int32)
@@ -362,7 +350,7 @@
         keep, send, *residual = partial_of(
             applied, product, inner, outer, couple, inverse, inverse_cols, faces, place, last
         )
-        own, got = summed(keep, send, spot)
+        own, got = summed(keep, send)
         outs = update_of(own, got, current, inverse, inverse_cols, faces, place, not last)
         current = outs[0]
         if not last:

time: 117 us -> 113 us (0.966)
  waiting for transfers between devices: 40 us -> 38.3 us
  starting transfers between devices: 47.2 us -> 45.9 us
    ppermute x30, starting transfers between devices: 43.5 us -> 41.9 us  [moved(): return lax.ppermute(value, ('wide', 'narrow'), pairs)]
    ppermute x30, waiting for transfers between devices: 38.7 us -> 37.2 us  [moved(): return lax.ppermute(value, ('wide', 'narrow'), pairs)]
    unnamed x27 -> x22, local copies, waits for them, and re-layouts: 5.11 us -> 5.06 us
where the time goes in v4:
time: 113 us
  starting transfers between devices  45.9 us (41%)
  waiting for transfers between devices  38.3 us (34%)
  Pallas kernels  21.5 us (19%)
  local copies, waits for them, and re-layouts  5.22 us (5%)
  other arithmetic  1.15 us (1%)
  between operations  1.15 us (1%)
    ppermute x30, starting transfers between devices, moved(): return lax.ppermute(value, ('wide', 'narrow'), pairs)  41.9 us
    ppermute x30, waiting for transfers between devices, moved(): return lax.ppermute(value, ('wide', 'narrow'), pairs)  37.2 us
    pallas_call x7, Pallas kernels, call(): pl.pallas_call(kernel, grid_spec=pltpu.PrefetchScalarGridSpec(num_scalar_...  21.5 us
    unnamed x22, local copies, waits for them, and re-layouts  5.06 us
    ppermute x2, starting transfers between devices, faces_swapped(): lax.ppermute(inner, 'narrow', [(i, i ^ 1) for i in range(count)])  3.69 us
  transfers between devices with their start and end apart: 34, of which 22 were waited for; matrix products, arithmetic and copies ran while one was open for 1% of the time, Pallas kernels for 4%

profile of v4, /device:TPU:1, one launch (start us, length us, event | category | flops | bytes accessed | tf_op | source)
XLA Modules:
  0.0 113.3 jit_solution(719198018498377834)
XLA Ops:
  4.3 3.3 %collective-permute-start = (bf16[256,128]{1,0:T(8,128)(2,1)S(1)}, bf16[256,128]{1,0:T(8,128)(2,1)S(1)}, u32[]{:S(2)}, u32[]{:S(2)}) collective-permute-start(bf16[256,128]{1,0:T(8,128)(2,1)S(1)} %get-tuple-element.15), channel_id=1, source_target_pairs={{0,1},{1,0},{2,3},{3,2},{4,5},{5,4},{6,7},{7,6},{8,9},{9,8},{10,11... | collective-permute-start | bytes 196616 | tf_op jit(solution)/shard_map/ppermute | solution.py:273
  8.2 2.0 %copy-done.1 = bf16[1,1,16,7,128,128]{5,4,3,2,1,0:T(8,128)(2,1)S(1)} copy-done((bf16[1,1,16,7,128,128]{5,4,3,2,1,0:T(8,128)(2,1)S(1)}, bf16[1,1,16,7,128,128]{5,4,3,2,1,0:T(8,128)(2,1)}, u32[]{:S(2)}) %copy-start.1) | copy-done | bytes 3670040
  10.3 2.2 %product.2.prod_ref = f32[2048,128]{1,0:T(8,128)S(1)} custom-call(s32[7,16]{1,0:T(8,128)S(1)} %bitcast.116, bf16[16,7,128,128]{3,2,1,0:T(8,128)(2,1)S(1)} %bitcast.99, bf16[2048,128]{1,0:T(8,128)(2,1)S(1)} %get-tuple-element.14.curb_ref), custom_call_target="tpu_custom_call" | custom-call | flops 469762048 | bytes 8000000 | tf_op jit(solution)/shard_map/product/pallas_call | solution.py:179
  12.6 4.1 %partial.2 = (f32[4,8,64,128]{3,2,1,0:T(8,128)S(1)}, bf16[4,8,64,128]{3,2,1,0:T(8,128)(2,1)S(1)}) custom-call(s32[8,16]{1,0:T(8,128)S(1)} %bitcast.112, s32[512]{0:T(512)S(1)} %bitcast.108, s32[3]{0:T(128)S(1)} %pad_add_fusion.place_ref, bf16[16,8,128,128]{3,2,1,0:T(8,128)(2,1)S(1)} %bitcast.95, f32[2048,128]{1,0:T(8,128)S(1)} %bitcast.103, ...), custom_call_target="tpu_custom_call" | custom-call | flops 536870912 | bytes 8000000 | tf_op jit(solution)/shard_map/partial/pallas_call | solution.py:179
  18.0 1.5 %collective-permute-done.2 = bf16[4,8,64,128]{3,2,1,0:T(8,128)(2,1)S(1)} collective-permute-done((bf16[4,8,64,128]{3,2,1,0:T(8,128)(2,1)S(1)}, bf16[4,8,64,128]{3,2,1,0:T(8,128)(2,1)S(1)}, u32[]{:S(2)}, u32[]{:S(2)}) %collective-permute-start.2) | collective-permute-done | bytes 524320 | tf_op jit(solution)/shard_map/ppermute | solution.py:243
  19.6 1.9 %collective-permute-start.4 = (bf16[6,64,128]{2,1,0:T(8,128)(2,1)S(1)}, bf16[6,64,128]{2,1,0:T(8,128)(2,1)S(1)}, u32[]{:S(2)}, u32[]{:S(2)}) collective-permute-start(bf16[6,64,128]{2,1,0:T(8,128)(2,1)S(1)} %get-tuple-element.45), channel_id=1, source_target_pairs={{0,64},{1,7},{2,66},{3,5},{4,68},{5,3},{6,70},{7,1},{8,72},{9,15},... | collective-permute-start | bytes 294920 | tf_op jit(solution)/shard_map/ppermute | solution.py:243
  23.1 3.5 %collective-permute-done.3 = bf16[8,64,128]{2,1,0:T(8,128)(2,1)S(1)} collective-permute-done((bf16[8,64,128]{2,1,0:T(8,128)(2,1)S(1)}, bf16[8,64,128]{2,1,0:T(8,128)(2,1)S(1)}, u32[]{:S(2)}, u32[]{:S(2)}) %collective-permute-start.3) | collective-permute-done | bytes 131104 | tf_op jit(solution)/shard_map/ppermute | solution.py:243
  26.8 1.7 %collective-permute-start.6 = (bf16[5,64,128]{2,1,0:T(8,128)(2,1)S(1)}, bf16[5,64,128]{2,1,0:T(8,128)(2,1)S(1)}, u32[]{:S(2)}, u32[]{:S(2)}) collective-permute-start(bf16[5,64,128]{2,1,0:T(8,128)(2,1)S(1)} %slice.604), channel_id=1, source_target_pairs={{0,2},{1,9},{2,0},{3,11},{4,6},{5,13},{6,4},{7,15},{8,10},{9,1},{1... | collective-permute-start | bytes 245768 | tf_op jit(solution)/shard_map/ppermute | solution.py:243
  28.5 1.8 %collective-permute-done.6 = bf16[5,64,128]{2,1,0:T(8,128)(2,1)S(1)} collective-permute-done((bf16[5,64,128]{2,1,0:T(8,128)(2,1)S(1)}, bf16[5,64,128]{2,1,0:T(8,128)(2,1)S(1)}, u32[]{:S(2)}, u32[]{:S(2)}) %collective-permute-start.6) | collective-permute-done | bytes 81952 | tf_op jit(solution)/shard_map/ppermute | solution.py:243
  30.4 6.4 %collective-permute-start.9 = (bf16[3,64,128]{2,1,0:T(8,128)(2,1)S(1)}, bf16[3,64,128]{2,1,0:T(8,128)(2,1)S(1)}, u32[]{:S(2)}, u32[]{:S(2)}) collective-permute-start(bf16[3,64,128]{2,1,0:T(8,128)(2,1)S(1)} %slice.344), channel_id=1, source_target_pairs={{0,64},{1,41},{2,66},{3,43},{4,68},{5,45},{6,70},{7,47},{8,72},{9,... | collective-permute-start | bytes 147464 | tf_op jit(solution)/shard_map/ppermute | solution.py:243
  37.9 3.8 %collective-permute-done.7 = bf16[4,64,128]{2,1,0:T(8,128)(2,1)S(1)} collective-permute-done((bf16[4,64,128]{2,1,0:T(8,128)(2,1)S(1)}, bf16[4,64,128]{2,1,0:T(8,128)(2,1)S(1)}, u32[]{:S(2)}, u32[]{:S(2)}) %collective-permute-start.7) | collective-permute-done | bytes 65568 | tf_op jit(solution)/shard_map/ppermute | solution.py:243
  41.9 3.0 %collective-permute-start.12 = (bf16[1,64,128]{2,1,0:T(8,128)(2,1)S(1)}, bf16[1,64,128]{2,1,0:T(8,128)(2,1)S(1)}, u32[]{:S(2)}, u32[]{:S(2)}) collective-permute-start(bf16[1,64,128]{2,1,0:T(8,128)(2,1)S(1)} %slice.351), channel_id=1, source_target_pairs={{0,8},{1,129},{2,10},{3,131},{4,12},{5,133},{6,14},{7,135},{8,0},{... | collective-permute-start | bytes 49160 | tf_op jit(solution)/shard_map/ppermute | solution.py:243
  45.8 2.7 %collective-permute-done.10 = bf16[2,64,128]{2,1,0:T(8,128)(2,1)S(1)} collective-permute-done((bf16[2,64,128]{2,1,0:T(8,128)(2,1)S(1)}, bf16[2,64,128]{2,1,0:T(8,128)(2,1)S(1)}, u32[]{:S(2)}, u32[]{:S(2)}) %collective-permute-start.10) | collective-permute-done | bytes 32800 | tf_op jit(solution)/shard_map/ppermute | solution.py:243
  49.8 2.9 %collective-permute-start.15 = (bf16[6,64,128]{2,1,0:T(8,128)(2,1)S(1)}, bf16[6,64,128]{2,1,0:T(8,128)(2,1)S(1)}, u32[]{:S(2)}, u32[]{:S(2)}) collective-permute-start(bf16[6,64,128]{2,1,0:T(8,128)(2,1)S(1)} %get-tuple-element.89), channel_id=1, source_target_pairs={{0,192},{1,5},{2,194},{3,7},{4,196},{5,1},{6,198},{7,3},{8,200},{9... | collective-permute-start | bytes 294920 | tf_op jit(solution)/shard_map/ppermute | solution.py:243
  54.0 2.2 %collective-permute-done.15 = bf16[6,64,128]{2,1,0:T(8,128)(2,1)S(1)} collective-permute-done((bf16[6,64,128]{2,1,0:T(8,128)(2,1)S(1)}, bf16[6,64,128]{2,1,0:T(8,128)(2,1)S(1)}, u32[]{:S(2)}, u32[]{:S(2)}) %collective-permute-start.15) | collective-permute-done | bytes 98336 | tf_op jit(solution)/shard_map/ppermute | solution.py:243
  56.3 1.9 %collective-permute-done.16.got_ref = bf16[4,8,64,128]{3,2,1,0:T(8,128)(2,1)S(1)} collective-permute-done((bf16[4,8,64,128]{3,2,1,0:T(8,128)(2,1)S(1)}, bf16[4,8,64,128]{3,2,1,0:T(8,128)(2,1)S(1)}, u32[]{:S(2)}, u32[]{:S(2)}) %collective-permute-start.16) | collective-permute-done | bytes 524320 | tf_op jit(solution)/shard_map/ppermute | solution.py:243
  58.2 3.3 %update.2 = (f32[2048,128]{1,0:T(8,128)S(1)}, bf16[256,128]{1,0:T(8,128)(2,1)S(1)}, bf16[256,128]{1,0:T(8,128)(2,1)S(1)}, bf16[2048,128]{1,0:T(8,128)(2,1)S(1)}) custom-call(s32[8,16]{1,0:T(8,128)S(1)} %bitcast.113, s32[512]{0:T(512)S(1)} %bitcast.109, s32[3]{0:T(128)S(1)} %pad_add_fusion.place_ref, bf16[16,8,128,128]{3,2,1,0:T(8,128)(2,1)S(1)} %bitcast.96, ...), custom_call_target="tpu_custom_call" | custom-call | flops 536870912 | bytes 8000000 | tf_op jit(solution)/shard_map/update/pallas_call | solution.py:179
  62.3 2.2 %product.3.prod_ref = f32[2048,128]{1,0:T(8,128)S(1)} custom-call(s32[7,16]{1,0:T(8,128)S(1)} %bitcast.117, bf16[16,7,128,128]{3,2,1,0:T(8,128)(2,1)S(1)} %bitcast.100, bf16[2048,128]{1,0:T(8,128)(2,1)S(1)} %get-tuple-element.19.curb_ref), custom_call_target="tpu_custom_call" | custom-call | flops 469762048 | bytes 8000000 | tf_op jit(solution)/shard_map/product/pallas_call | solution.py:179
  65.6 4.9 %partial.3 = (f32[4,8,64,128]{3,2,1,0:T(8,128)S(1)}, bf16[4,8,64,128]{3,2,1,0:T(8,128)(2,1)S(1)}, f32[2048,128]{1,0:T(8,128)}) custom-call(s32[8,16]{1,0:T(8,128)S(1)} %bitcast.114, s32[512]{0:T(512)S(1)} %bitcast.110, s32[3]{0:T(128)S(1)} %pad_add_fusion.place_ref, bf16[16,8,128,128]{3,2,1,0:T(8,128)(2,1)S(1)} %bitcast.97, f32[2048,128]{1,0:T(8,128)S(1)} %bitcast.104, ...), custom_call_target="tpu_custom_call" | custom-call | flops 536870912 | bytes 8000000 | tf_op jit(solution)/shard_map/partial/pallas_call | solution.py:179
  70.5 1.6 %collective-permute-start.19 = (bf16[4,8,64,128]{3,2,1,0:T(8,128)(2,1)S(1)}, bf16[4,8,64,128]{3,2,1,0:T(8,128)(2,1)S(1)}, u32[]{:S(2)}, u32[]{:S(2)}) collective-permute-start(bf16[4,8,64,128]{3,2,1,0:T(8,128)(2,1)S(1)} %get-tuple-element.23), channel_id=1, source_target_pairs={{0,1},{1,0},{2,3},{3,2},{4,5},{5,4},{6,7},{7,6},{8,9},{9,8},{10,11... | collective-permute-start | bytes 1572872 | tf_op jit(solution)/shard_map/ppermute | solution.py:243
  72.1 1.5 %collective-permute-done.19 = bf16[4,8,64,128]{3,2,1,0:T(8,128)(2,1)S(1)} collective-permute-done((bf16[4,8,64,128]{3,2,1,0:T(8,128)(2,1)S(1)}, bf16[4,8,64,128]{3,2,1,0:T(8,128)(2,1)S(1)}, u32[]{:S(2)}, u32[]{:S(2)}) %collective-permute-start.19) | collective-permute-done | bytes 524320 | tf_op jit(solution)/shard_map/ppermute | solution.py:243
  74.8 2.4 %collective-permute-start.20 = (bf16[8,64,128]{2,1,0:T(8,128)(2,1)S(1)}, bf16[8,64,128]{2,1,0:T(8,128)(2,1)S(1)}, u32[]{:S(2)}, u32[]{:S(2)}) collective-permute-start(bf16[8,64,128]{2,1,0:T(8,128)(2,1)S(1)} %pad_maximum_fusion.3), channel_id=1, source_target_pairs={{0,8},{1,3},{2,10},{3,1},{4,12},{5,7},{6,14},{7,5},{8,0},{9,11},{1... | collective-permute-start | bytes 393224 | tf_op jit(solution)/shard_map/ppermute | solution.py:243
  77.3 3.5 %collective-permute-done.20 = bf16[8,64,128]{2,1,0:T(8,128)(2,1)S(1)} collective-permute-done((bf16[8,64,128]{2,1,0:T(8,128)(2,1)S(1)}, bf16[8,64,128]{2,1,0:T(8,128)(2,1)S(1)}, u32[]{:S(2)}, u32[]{:S(2)}) %collective-permute-start.20) | collective-permute-done | bytes 131104 | tf_op jit(solution)/shard_map/ppermute | solution.py:243
  81.7 2.6 %collective-permute-done.23 = bf16[5,64,128]{2,1,0:T(8,128)(2,1)S(1)} collective-permute-done((bf16[5,64,128]{2,1,0:T(8,128)(2,1)S(1)}, bf16[5,64,128]{2,1,0:T(8,128)(2,1)S(1)}, u32[]{:S(2)}, u32[]{:S(2)}) %collective-permute-start.23) | collective-permute-done | bytes 81952 | tf_op jit(solution)/shard_map/ppermute | solution.py:243
  84.4 5.4 %collective-permute-start.26 = (bf16[3,64,128]{2,1,0:T(8,128)(2,1)S(1)}, bf16[3,64,128]{2,1,0:T(8,128)(2,1)S(1)}, u32[]{:S(2)}, u32[]{:S(2)}) collective-permute-start(bf16[3,64,128]{2,1,0:T(8,128)(2,1)S(1)} %slice.378), channel_id=1, source_target_pairs={{0,64},{1,41},{2,66},{3,43},{4,68},{5,45},{6,70},{7,47},{8,72},{9,... | collective-permute-start | bytes 147464 | tf_op jit(solution)/shard_map/ppermute | solution.py:243
  91.0 3.7 %collective-permute-done.24 = bf16[4,64,128]{2,1,0:T(8,128)(2,1)S(1)} collective-permute-done((bf16[4,64,128]{2,1,0:T(8,128)(2,1)S(1)}, bf16[4,64,128]{2,1,0:T(8,128)(2,1)S(1)}, u32[]{:S(2)}, u32[]{:S(2)}) %collective-permute-start.24) | collective-permute-done | bytes 65568 | tf_op jit(solution)/shard_map/ppermute | solution.py:243
  95.1 1.5 %collective-permute-start.28 = (bf16[1,64,128]{2,1,0:T(8,128)(2,1)S(1)}, bf16[1,64,128]{2,1,0:T(8,128)(2,1)S(1)}, u32[]{:S(2)}, u32[]{:S(2)}) collective-permute-start(bf16[1,64,128]{2,1,0:T(8,128)(2,1)S(1)} %slice.385), channel_id=1, source_target_pairs={{0,6},{1,193},{2,4},{3,195},{4,2},{5,197},{6,0},{7,199},{8,14},{9,... | collective-permute-start | bytes 49160 | tf_op jit(solution)/shard_map/ppermute | solution.py:243
  97.7 1.9 %collective-permute-done.27 = bf16[2,64,128]{2,1,0:T(8,128)(2,1)S(1)} collective-permute-done((bf16[2,64,128]{2,1,0:T(8,128)(2,1)S(1)}, bf16[2,64,128]{2,1,0:T(8,128)(2,1)S(1)}, u32[]{:S(2)}, u32[]{:S(2)}) %collective-permute-start.27) | collective-permute-done | bytes 32800 | tf_op jit(solution)/shard_map/ppermute | solution.py:243
  100.6 3.1 %collective-permute-start.32 = (bf16[6,64,128]{2,1,0:T(8,128)(2,1)S(1)}, bf16[6,64,128]{2,1,0:T(8,128)(2,1)S(1)}, u32[]{:S(2)}, u32[]{:S(2)}) collective-permute-start(bf16[6,64,128]{2,1,0:T(8,128)(2,1)S(1)} %get-tuple-element.85), channel_id=1, source_target_pairs={{0,192},{1,5},{2,194},{3,7},{4,196},{5,1},{6,198},{7,3},{8,200},{9... | collective-permute-start | bytes 294920 | tf_op jit(solution)/shard_map/ppermute | solution.py:243
  104.8 2.4 %collective-permute-done.32 = bf16[6,64,128]{2,1,0:T(8,128)(2,1)S(1)} collective-permute-done((bf16[6,64,128]{2,1,0:T(8,128)(2,1)S(1)}, bf16[6,64,128]{2,1,0:T(8,128)(2,1)S(1)}, u32[]{:S(2)}, u32[]{:S(2)}) %collective-permute-start.32) | collective-permute-done | bytes 98336 | tf_op jit(solution)/shard_map/ppermute | solution.py:243
  108.2 1.5 %collective-permute-done.33.got_ref = bf16[4,8,64,128]{3,2,1,0:T(8,128)(2,1)S(1)} collective-permute-done((bf16[4,8,64,128]{3,2,1,0:T(8,128)(2,1)S(1)}, bf16[4,8,64,128]{3,2,1,0:T(8,128)(2,1)S(1)}, u32[]{:S(2)}, u32[]{:S(2)}) %collective-permute-start.33) | collective-permute-done | bytes 524320 | tf_op jit(solution)/shard_map/ppermute | solution.py:243
  109.8 3.5 %update.3 = f32[2048,128]{1,0:T(8,128)} custom-call(s32[8,16]{1,0:T(8,128)S(1)} %bitcast.115, s32[512]{0:T(512)S(1)} %bitcast.111, s32[3]{0:T(128)S(1)} %pad_add_fusion.place_ref, bf16[16,8,128,128]{3,2,1,0:T(8,128)(2,1)S(1)} %bitcast.98, bf16[4,8,64,128]{3,2,1,0:T(8,128)(2,1)S(1)} %pad_maximum_fusion.1.own_ref, ...), custom_call_target="tpu_custom_call" | custom-call | flops 536870912 | bytes 8000000 | tf_op jit(solution)/shard_map/update/pallas_call | solution.py:179
  (128 shorter events, 21.9 us)
Async XLA Ops:
  4.3 8.3 %collective-permute-start = (bf16[256,128]{1,0:T(8,128)(2,1)S(1)}, bf16[256,128]{1,0:T(8,128)(2,1)S(1)}, u32[]{:S(2)}, u32[]{:S(2)}) collective-permute-start(bf16[256,128]{1,0:T(8,128)(2,1)S(1)} %get-tuple-element.15), channel_id=1, source_target_pairs={{0,1},{1,0},{2,3},{3,2},{4,5},{5,4},{6,7},{7,6},{8,9},{9,8},{10,11... | collective-permute-start | bytes 196616 | tf_op jit(solution)/shard_map/ppermute | solution.py:273
  7.5 5.0 %collective-permute-start.1 = (bf16[256,128]{1,0:T(8,128)(2,1)S(1)}, bf16[256,128]{1,0:T(8,128)(2,1)S(1)}, u32[]{:S(2)}, u32[]{:S(2)}) collective-permute-start(bf16[256,128]{1,0:T(8,128)(2,1)S(1)} %get-tuple-element.16), channel_id=1, source_target_pairs={{0,7},{1,2},{2,1},{3,4},{4,3},{5,6},{6,5},{7,0},{8,15},{9,10},{10,... | collective-permute-start | bytes 196616 | tf_op jit(solution)/shard_map/ppermute | solution.py:274
  16.7 2.8 %collective-permute-start.2 = (bf16[4,8,64,128]{3,2,1,0:T(8,128)(2,1)S(1)}, bf16[4,8,64,128]{3,2,1,0:T(8,128)(2,1)S(1)}, u32[]{:S(2)}, u32[]{:S(2)}) collective-permute-start(bf16[4,8,64,128]{3,2,1,0:T(8,128)(2,1)S(1)} %get-tuple-element.18), channel_id=1, source_target_pairs={{0,1},{1,0},{2,3},{3,2},{4,5},{5,4},{6,7},{7,6},{8,9},{9,8},{10,11... | collective-permute-start | bytes 1572872 | tf_op jit(solution)/shard_map/ppermute | solution.py:243
  19.6 7.1 %collective-permute-start.4 = (bf16[6,64,128]{2,1,0:T(8,128)(2,1)S(1)}, bf16[6,64,128]{2,1,0:T(8,128)(2,1)S(1)}, u32[]{:S(2)}, u32[]{:S(2)}) collective-permute-start(bf16[6,64,128]{2,1,0:T(8,128)(2,1)S(1)} %get-tuple-element.45), channel_id=1, source_target_pairs={{0,64},{1,7},{2,66},{3,5},{4,68},{5,3},{6,70},{7,1},{8,72},{9,15},... | collective-permute-start | bytes 294920 | tf_op jit(solution)/shard_map/ppermute | solution.py:243
  21.5 5.2 %collective-permute-start.5 = (bf16[6,64,128]{2,1,0:T(8,128)(2,1)S(1)}, bf16[6,64,128]{2,1,0:T(8,128)(2,1)S(1)}, u32[]{:S(2)}, u32[]{:S(2)}) collective-permute-start(bf16[6,64,128]{2,1,0:T(8,128)(2,1)S(1)} %get-tuple-element.46), channel_id=1, source_target_pairs={{0,192},{1,5},{2,194},{3,7},{4,196},{5,1},{6,198},{7,3},{8,200},{9... | collective-permute-start | bytes 294920 | tf_op jit(solution)/shard_map/ppermute | solution.py:243
  22.2 4.5 %collective-permute-start.3 = (bf16[8,64,128]{2,1,0:T(8,128)(2,1)S(1)}, bf16[8,64,128]{2,1,0:T(8,128)(2,1)S(1)}, u32[]{:S(2)}, u32[]{:S(2)}) collective-permute-start(bf16[8,64,128]{2,1,0:T(8,128)(2,1)S(1)} %pad_maximum_fusion.2), channel_id=1, source_target_pairs={{0,8},{1,3},{2,10},{3,1},{4,12},{5,7},{6,14},{7,5},{8,0},{9,11},{1... | collective-permute-start | bytes 393224 | tf_op jit(solution)/shard_map/ppermute | solution.py:243
  26.8 3.5 %collective-permute-start.6 = (bf16[5,64,128]{2,1,0:T(8,128)(2,1)S(1)}, bf16[5,64,128]{2,1,0:T(8,128)(2,1)S(1)}, u32[]{:S(2)}, u32[]{:S(2)}) collective-permute-start(bf16[5,64,128]{2,1,0:T(8,128)(2,1)S(1)} %slice.604), channel_id=1, source_target_pairs={{0,2},{1,9},{2,0},{3,11},{4,6},{5,13},{6,4},{7,15},{8,10},{9,1},{1... | collective-permute-start | bytes 245768 | tf_op jit(solution)/shard_map/ppermute | solution.py:243
  30.4 11.4 %collective-permute-start.9 = (bf16[3,64,128]{2,1,0:T(8,128)(2,1)S(1)}, bf16[3,64,128]{2,1,0:T(8,128)(2,1)S(1)}, u32[]{:S(2)}, u32[]{:S(2)}) collective-permute-start(bf16[3,64,128]{2,1,0:T(8,128)(2,1)S(1)} %slice.344), channel_id=1, source_target_pairs={{0,64},{1,41},{2,66},{3,43},{4,68},{5,45},{6,70},{7,47},{8,72},{9,... | collective-permute-start | bytes 147464 | tf_op jit(solution)/shard_map/ppermute | solution.py:243
  36.8 5.1 %collective-permute-start.8 = (bf16[3,64,128]{2,1,0:T(8,128)(2,1)S(1)}, bf16[3,64,128]{2,1,0:T(8,128)(2,1)S(1)}, u32[]{:S(2)}, u32[]{:S(2)}) collective-permute-start(bf16[3,64,128]{2,1,0:T(8,128)(2,1)S(1)} %slice.344), channel_id=1, source_target_pairs={{0,6},{1,49},{2,4},{3,51},{4,2},{5,53},{6,0},{7,55},{8,14},{9,57},... | collective-permute-start | bytes 147464 | tf_op jit(solution)/shard_map/ppermute | solution.py:243
  37.0 4.7 %collective-permute-start.7 = (bf16[4,64,128]{2,1,0:T(8,128)(2,1)S(1)}, bf16[4,64,128]{2,1,0:T(8,128)(2,1)S(1)}, u32[]{:S(2)}, u32[]{:S(2)}) collective-permute-start(bf16[4,64,128]{2,1,0:T(8,128)(2,1)S(1)} %slice.606), channel_id=1, source_target_pairs={{0,2},{1,17},{2,0},{3,19},{4,6},{5,21},{6,4},{7,23},{8,10},{9,25},... | collective-permute-start | bytes 196616 | tf_op jit(solution)/shard_map/ppermute | solution.py:243
  41.9 6.6 %collective-permute-start.12 = (bf16[1,64,128]{2,1,0:T(8,128)(2,1)S(1)}, bf16[1,64,128]{2,1,0:T(8,128)(2,1)S(1)}, u32[]{:S(2)}, u32[]{:S(2)}) collective-permute-start(bf16[1,64,128]{2,1,0:T(8,128)(2,1)S(1)} %slice.351), channel_id=1, source_target_pairs={{0,8},{1,129},{2,10},{3,131},{4,12},{5,133},{6,14},{7,135},{8,0},{... | collective-permute-start | bytes 49160 | tf_op jit(solution)/shard_map/ppermute | solution.py:243
  44.9 3.8 %collective-permute-start.11 = (bf16[1,64,128]{2,1,0:T(8,128)(2,1)S(1)}, bf16[1,64,128]{2,1,0:T(8,128)(2,1)S(1)}, u32[]{:S(2)}, u32[]{:S(2)}) collective-permute-start(bf16[1,64,128]{2,1,0:T(8,128)(2,1)S(1)} %slice.351), channel_id=1, source_target_pairs={{0,6},{1,193},{2,4},{3,195},{4,2},{5,197},{6,0},{7,199},{8,14},{9,... | collective-permute-start | bytes 49160 | tf_op jit(solution)/shard_map/ppermute | solution.py:243
  45.7 2.8 %collective-permute-start.10 = (bf16[2,64,128]{2,1,0:T(8,128)(2,1)S(1)}, bf16[2,64,128]{2,1,0:T(8,128)(2,1)S(1)}, u32[]{:S(2)}, u32[]{:S(2)}) collective-permute-start(bf16[2,64,128]{2,1,0:T(8,128)(2,1)S(1)} %slice.347), channel_id=1, source_target_pairs={{0,2},{1,65},{2,0},{3,67},{4,6},{5,69},{6,4},{7,71},{8,10},{9,73},... | collective-permute-start | bytes 98312 | tf_op jit(solution)/shard_map/ppermute | solution.py:243
  48.8 4.8 %collective-permute-start.13 = (bf16[6,64,128]{2,1,0:T(8,128)(2,1)S(1)}, bf16[6,64,128]{2,1,0:T(8,128)(2,1)S(1)}, u32[]{:S(2)}, u32[]{:S(2)}) collective-permute-start(bf16[6,64,128]{2,1,0:T(8,128)(2,1)S(1)} %get-tuple-element.89), channel_id=1, source_target_pairs={{0,64},{1,7},{2,66},{3,5},{4,68},{5,3},{6,70},{7,1},{8,72},{9,15},... | collective-permute-start | bytes 294920 | tf_op jit(solution)/shard_map/ppermute | solution.py:243
  49.8 4.1 %collective-permute-start.14 = (bf16[8,64,128]{2,1,0:T(8,128)(2,1)S(1)}, bf16[8,64,128]{2,1,0:T(8,128)(2,1)S(1)}, u32[]{:S(2)}, u32[]{:S(2)}) collective-permute-start(bf16[8,64,128]{2,1,0:T(8,128)(2,1)S(1)} %get-tuple-element.88), channel_id=1, source_target_pairs={{0,8},{1,3},{2,10},{3,1},{4,12},{5,7},{6,14},{7,5},{8,0},{9,11},{1... | collective-permute-start | bytes 393224 | tf_op jit(solution)/shard_map/ppermute | solution.py:243
  49.8 6.3 %collective-permute-start.15 = (bf16[6,64,128]{2,1,0:T(8,128)(2,1)S(1)}, bf16[6,64,128]{2,1,0:T(8,128)(2,1)S(1)}, u32[]{:S(2)}, u32[]{:S(2)}) collective-permute-start(bf16[6,64,128]{2,1,0:T(8,128)(2,1)S(1)} %get-tuple-element.89), channel_id=1, source_target_pairs={{0,192},{1,5},{2,194},{3,7},{4,196},{5,1},{6,198},{7,3},{8,200},{9... | collective-permute-start | bytes 294920 | tf_op jit(solution)/shard_map/ppermute | solution.py:243
  61.5 3.0 %collective-permute-start.17 = (bf16[256,128]{1,0:T(8,128)(2,1)S(1)}, bf16[256,128]{1,0:T(8,128)(2,1)S(1)}, u32[]{:S(2)}, u32[]{:S(2)}) collective-permute-start(bf16[256,128]{1,0:T(8,128)(2,1)S(1)} %get-tuple-element.20), channel_id=1, source_target_pairs={{0,1},{1,0},{2,3},{3,2},{4,5},{5,4},{6,7},{7,6},{8,9},{9,8},{10,11... | collective-permute-start | bytes 196616 | tf_op jit(solution)/shard_map/ppermute | solution.py:273
  61.9 3.7 %collective-permute-start.18 = (bf16[256,128]{1,0:T(8,128)(2,1)S(1)}, bf16[256,128]{1,0:T(8,128)(2,1)S(1)}, u32[]{:S(2)}, u32[]{:S(2)}) collective-permute-start(bf16[256,128]{1,0:T(8,128)(2,1)S(1)} %get-tuple-element.21), channel_id=1, source_target_pairs={{0,7},{1,2},{2,1},{3,4},{4,3},{5,6},{6,5},{7,0},{8,15},{9,10},{10,... | collective-permute-start | bytes 196616 | tf_op jit(solution)/shard_map/ppermute | solution.py:274
  70.5 3.1 %collective-permute-start.19 = (bf16[4,8,64,128]{3,2,1,0:T(8,128)(2,1)S(1)}, bf16[4,8,64,128]{3,2,1,0:T(8,128)(2,1)S(1)}, u32[]{:S(2)}, u32[]{:S(2)}) collective-permute-start(bf16[4,8,64,128]{3,2,1,0:T(8,128)(2,1)S(1)} %get-tuple-element.23), channel_id=1, source_target_pairs={{0,1},{1,0},{2,3},{3,2},{4,5},{5,4},{6,7},{7,6},{8,9},{9,8},{10,11... | collective-permute-start | bytes 1572872 | tf_op jit(solution)/shard_map/ppermute | solution.py:243
  73.7 7.1 %collective-permute-start.21 = (bf16[6,64,128]{2,1,0:T(8,128)(2,1)S(1)}, bf16[6,64,128]{2,1,0:T(8,128)(2,1)S(1)}, u32[]{:S(2)}, u32[]{:S(2)}) collective-permute-start(bf16[6,64,128]{2,1,0:T(8,128)(2,1)S(1)} %get-tuple-element.42), channel_id=1, source_target_pairs={{0,64},{1,7},{2,66},{3,5},{4,68},{5,3},{6,70},{7,1},{8,72},{9,15},... | collective-permute-start | bytes 294920 | tf_op jit(solution)/shard_map/ppermute | solution.py:243
  74.7 6.1 %collective-permute-start.22 = (bf16[6,64,128]{2,1,0:T(8,128)(2,1)S(1)}, bf16[6,64,128]{2,1,0:T(8,128)(2,1)S(1)}, u32[]{:S(2)}, u32[]{:S(2)}) collective-permute-start(bf16[6,64,128]{2,1,0:T(8,128)(2,1)S(1)} %get-tuple-element.44), channel_id=1, source_target_pairs={{0,192},{1,5},{2,194},{3,7},{4,196},{5,1},{6,198},{7,3},{8,200},{9... | collective-permute-start | bytes 294920 | tf_op jit(solution)/shard_map/ppermute | solution.py:243
  74.8 6.0 %collective-permute-start.20 = (bf16[8,64,128]{2,1,0:T(8,128)(2,1)S(1)}, bf16[8,64,128]{2,1,0:T(8,128)(2,1)S(1)}, u32[]{:S(2)}, u32[]{:S(2)}) collective-permute-start(bf16[8,64,128]{2,1,0:T(8,128)(2,1)S(1)} %pad_maximum_fusion.3), channel_id=1, source_target_pairs={{0,8},{1,3},{2,10},{3,1},{4,12},{5,7},{6,14},{7,5},{8,0},{9,11},{1... | collective-permute-start | bytes 393224 | tf_op jit(solution)/shard_map/ppermute | solution.py:243
  80.9 3.4 %collective-permute-start.23 = (bf16[5,64,128]{2,1,0:T(8,128)(2,1)S(1)}, bf16[5,64,128]{2,1,0:T(8,128)(2,1)S(1)}, u32[]{:S(2)}, u32[]{:S(2)}) collective-permute-start(bf16[5,64,128]{2,1,0:T(8,128)(2,1)S(1)} %slice.603), channel_id=1, source_target_pairs={{0,2},{1,9},{2,0},{3,11},{4,6},{5,13},{6,4},{7,15},{8,10},{9,1},{1... | collective-permute-start | bytes 245768 | tf_op jit(solution)/shard_map/ppermute | solution.py:243
  84.4 10.4 %collective-permute-start.26 = (bf16[3,64,128]{2,1,0:T(8,128)(2,1)S(1)}, bf16[3,64,128]{2,1,0:T(8,128)(2,1)S(1)}, u32[]{:S(2)}, u32[]{:S(2)}) collective-permute-start(bf16[3,64,128]{2,1,0:T(8,128)(2,1)S(1)} %slice.378), channel_id=1, source_target_pairs={{0,64},{1,41},{2,66},{3,43},{4,68},{5,45},{6,70},{7,47},{8,72},{9,... | collective-permute-start | bytes 147464 | tf_op jit(solution)/shard_map/ppermute | solution.py:243
  89.8 5.1 %collective-permute-start.25 = (bf16[3,64,128]{2,1,0:T(8,128)(2,1)S(1)}, bf16[3,64,128]{2,1,0:T(8,128)(2,1)S(1)}, u32[]{:S(2)}, u32[]{:S(2)}) collective-permute-start(bf16[3,64,128]{2,1,0:T(8,128)(2,1)S(1)} %slice.378), channel_id=1, source_target_pairs={{0,6},{1,49},{2,4},{3,51},{4,2},{5,53},{6,0},{7,55},{8,14},{9,57},... | collective-permute-start | bytes 147464 | tf_op jit(solution)/shard_map/ppermute | solution.py:243
  90.0 4.7 %collective-permute-start.24 = (bf16[4,64,128]{2,1,0:T(8,128)(2,1)S(1)}, bf16[4,64,128]{2,1,0:T(8,128)(2,1)S(1)}, u32[]{:S(2)}, u32[]{:S(2)}) collective-permute-start(bf16[4,64,128]{2,1,0:T(8,128)(2,1)S(1)} %slice.605), channel_id=1, source_target_pairs={{0,2},{1,17},{2,0},{3,19},{4,6},{5,21},{6,4},{7,23},{8,10},{9,25},... | collective-permute-start | bytes 196616 | tf_op jit(solution)/shard_map/ppermute | solution.py:243
  95.0 4.7 %collective-permute-start.29 = (bf16[1,64,128]{2,1,0:T(8,128)(2,1)S(1)}, bf16[1,64,128]{2,1,0:T(8,128)(2,1)S(1)}, u32[]{:S(2)}, u32[]{:S(2)}) collective-permute-start(bf16[1,64,128]{2,1,0:T(8,128)(2,1)S(1)} %slice.385), channel_id=1, source_target_pairs={{0,8},{1,129},{2,10},{3,131},{4,12},{5,133},{6,14},{7,135},{8,0},{... | collective-permute-start | bytes 49160 | tf_op jit(solution)/shard_map/ppermute | solution.py:243
  95.1 4.6 %collective-permute-start.28 = (bf16[1,64,128]{2,1,0:T(8,128)(2,1)S(1)}, bf16[1,64,128]{2,1,0:T(8,128)(2,1)S(1)}, u32[]{:S(2)}, u32[]{:S(2)}) collective-permute-start(bf16[1,64,128]{2,1,0:T(8,128)(2,1)S(1)} %slice.385), channel_id=1, source_target_pairs={{0,6},{1,193},{2,4},{3,195},{4,2},{5,197},{6,0},{7,199},{8,14},{9,... | collective-permute-start | bytes 49160 | tf_op jit(solution)/shard_map/ppermute | solution.py:243
  96.6 3.0 %collective-permute-start.27 = (bf16[2,64,128]{2,1,0:T(8,128)(2,1)S(1)}, bf16[2,64,128]{2,1,0:T(8,128)(2,1)S(1)}, u32[]{:S(2)}, u32[]{:S(2)}) collective-permute-start(bf16[2,64,128]{2,1,0:T(8,128)(2,1)S(1)} %slice.381), channel_id=1, source_target_pairs={{0,2},{1,65},{2,0},{3,67},{4,6},{5,69},{6,4},{7,71},{8,10},{9,73},... | collective-permute-start | bytes 98312 | tf_op jit(solution)/shard_map/ppermute | solution.py:243
  99.8 4.8 %collective-permute-start.30 = (bf16[6,64,128]{2,1,0:T(8,128)(2,1)S(1)}, bf16[6,64,128]{2,1,0:T(8,128)(2,1)S(1)}, u32[]{:S(2)}, u32[]{:S(2)}) collective-permute-start(bf16[6,64,128]{2,1,0:T(8,128)(2,1)S(1)} %get-tuple-element.85), channel_id=1, source_target_pairs={{0,64},{1,7},{2,66},{3,5},{4,68},{5,3},{6,70},{7,1},{8,72},{9,15},... | collective-permute-start | bytes 294920 | tf_op jit(solution)/shard_map/ppermute | solution.py:243
  100.6 4.1 %collective-permute-start.31 = (bf16[8,64,128]{2,1,0:T(8,128)(2,1)S(1)}, bf16[8,64,128]{2,1,0:T(8,128)(2,1)S(1)}, u32[]{:S(2)}, u32[]{:S(2)}) collective-permute-start(bf16[8,64,128]{2,1,0:T(8,128)(2,1)S(1)} %get-tuple-element.84), channel_id=1, source_target_pairs={{0,8},{1,3},{2,10},{3,1},{4,12},{5,7},{6,14},{7,5},{8,0},{9,11},{1... | collective-permute-start | bytes 393224 | tf_op jit(solution)/shard_map/ppermute | solution.py:243
  100.6 6.5 %collective-permute-start.32 = (bf16[6,64,128]{2,1,0:T(8,128)(2,1)S(1)}, bf16[6,64,128]{2,1,0:T(8,128)(2,1)S(1)}, u32[]{:S(2)}, u32[]{:S(2)}) collective-permute-start(bf16[6,64,128]{2,1,0:T(8,128)(2,1)S(1)} %get-tuple-element.85), channel_id=1, source_target_pairs={{0,192},{1,5},{2,194},{3,7},{4,196},{5,1},{6,198},{7,3},{8,200},{9... | collective-permute-start | bytes 294920 | tf_op jit(solution)/shard_map/ppermute | solution.py:243
  (10 other events, 86.7 us)
